TPU v7x, 32 devices: a whole 2x2x4 slice. The times are simulated.
32 devices in a mesh: groups: 2 (over y), tile: 4 (over x, core), slab: 4 (over z).
Axes of the slice: x: 2, y: 2, z: 4, core: 2. Of those that a mesh axis runs over, the one named last changes fastest.
Arguments:
- start_states: float32 [8, 49, 256, 128], P(('groups', 'slab'), None, 'tile'), parts along dimension 0, may hold values from -6 to 6
- end_adjoints: float32 [8, 49, 256, 128], P(('groups', 'slab'), None, 'tile'), parts along dimension 0, may hold values from -6 to 6
- misfits: float32 [8, 4, 256, 128], P(('groups', 'slab'), None, 'tile'), parts along dimension 0, may hold values from -6 to 6
- water_depth: float32 [512, 128], P(('groups', 'tile')), parts along dimension 0, may hold values from 0.5 to 2
- drag_coef: float32 [512, 128], P(('groups', 'tile')), parts along dimension 0, may hold values from 0.5 to 2
- sea_mask: int32 [512, 128], P(('groups', 'tile')), parts along dimension 0, may hold values 0 or 1
- bottom_level: int32 [512, 128], P(('groups', 'tile')), parts along dimension 0, may hold values from 1 to 24
Outputs:
- next_starts: float32 [8, 49, 256, 128], P(('groups', 'slab'), None, 'tile'), parts along dimension 0
- next_end_adjoints: float32 [8, 49, 256, 128], P(('groups', 'slab'), None, 'tile'), parts along dimension 0
- drag_gradient: float32 [512, 128], P(('groups', 'tile')), parts along dimension 0
There are 2 independent parts, one for each index of `groups`. A program takes and returns all parts, laid end to end along the dimension named above; each array names one. Nothing has to cross between parts.
Inputs may be any that keep to these rules, and one draw needn't show every extreme that they name: `sea_mask`: 1 for a sea column, 0 for a land column.
All inputs are finite; a program needn't handle non-finite values. No bound on the sum of `sea_mask` on one device may be relied on, other than what follows from the above.
Results may differ from a plain program's by a relative error of at most 0.0003.
Values sent between devices are 32-bit elements; how exact they have to be, the bound alone decides.
No kernel may reach another device: no remote copies, remote signals or barrier semaphores. Data moves between devices by JAX's collectives and lax.ppermute only.
A program may use at most 64 MiB of HBM per device.

v0:
```python
import jax
import jax.numpy as jnp
from jax import lax
from jax.sharding import PartitionSpec as P

STEPS = 4


def padded_2(block, sides, width):
    for axis, dim in sides:
        count = lax.axis_size(axis)
        forward = [(i, i + 1) for i in range(count - 1)]
        backward = [(target, source) for source, target in forward]
        low = lax.ppermute(
            lax.slice_in_dim(block, block.shape[dim] - width, None, axis=dim), axis, forward
        )
        high = lax.ppermute(lax.slice_in_dim(block, 0, width, axis=dim), axis, backward)
        block = jnp.concatenate([low, block, high], axis=dim)
    return block


def shifted(block, axis, distance):
    devices = range(lax.axis_size(axis))
    route = [(i - distance, i) for i in devices if i - distance in devices]
    return lax.ppermute(block, axis, route)


def passed_along(block, axis, distance):
    devices = range(lax.axis_size(axis))
    route = [((i - distance) % len(devices), i) for i in devices]
    return lax.ppermute(block, axis, route)


def column_diff(values):
    padded = jnp.pad(values, [(0, 0)] * (values.ndim - 1) + [(1, 1)])
    return padded[..., 2:] - padded[..., :-2]


def vertical_mix(values, active_in):
    zeros_row = jnp.zeros_like(values[:1])
    zeros_mask = jnp.zeros_like(active_in[:1])
    upper_level = jnp.concatenate([zeros_row, values[:-1]], 0)
    lower_level = jnp.concatenate([values[1:], zeros_row], 0)
    upper_active = jnp.concatenate([zeros_mask, active_in[:-1]], 0)
    lower_active = jnp.concatenate([active_in[1:], zeros_mask], 0)
    return upper_active * (upper_level - values) + lower_active * (lower_level - values)


def advance(state, statics):
    levels = (state.shape[0] - 1) // 2
    water_depth = statics[0]
    wet_levels = statics[1]
    drag_field = statics[2]
    sea_cells = jnp.minimum(wet_levels, 1.0)
    level_index = jnp.arange(levels).astype(jnp.float32)[:, None, None]
    active = (level_index < wet_levels[None]).astype(jnp.float32)
    bottom = (level_index == wet_levels[None] - 1.0).astype(jnp.float32)
    thickness = water_depth / jnp.maximum(wet_levels, 1.0)
    u_active = state[1 : levels + 1] * active
    v_active = state[levels + 1 :] * active
    flux_x = thickness * jnp.sum(u_active, 0)
    flux_y = thickness * jnp.sum(v_active, 0)
    diverge = flux_x[2:] - flux_x[:-2] + column_diff(flux_y)[1:-1]
    surface = sea_cells[1:-1] * (state[0, 1:-1] - 0.2 * diverge)
    slope_x = surface[2:] - surface[:-2]
    slope_y = column_diff(surface)[1:-1]
    u_inner = u_active[:, 2:-2]
    v_inner = v_active[:, 2:-2]
    active_in = active[:, 2:-2]
    bottom_in = bottom[:, 2:-2]
    thick_in = thickness[2:-2]
    sea_in = sea_cells[2:-2]
    drag_in = drag_field[2:-2]
    u_next = u_inner + 0.1 * v_inner - 0.2 * slope_x + 0.1 * vertical_mix(u_inner, active_in)
    v_next = v_inner - 0.1 * u_inner - 0.2 * slope_y + 0.1 * vertical_mix(v_inner, active_in)
    u_bottom = jnp.sum(bottom_in * u_inner, 0)
    v_bottom = jnp.sum(bottom_in * v_inner, 0)
    bottom_speed = jnp.sqrt(u_bottom * u_bottom + v_bottom * v_bottom + 0.0025)
    factor = thick_in / (thick_in + 0.1 * drag_in * bottom_speed + 1.0 - sea_in)
    retain = sea_in * active_in * (1.0 - bottom_in + bottom_in * factor)
    return jnp.concatenate([surface[1:-1][None], u_next * retain, v_next * retain], 0)


def settle(cotangent, border, from_above, from_below):
    middle = cotangent[:, border : cotangent.shape[1] - border]
    row_count = middle.shape[1]
    upper_part = jnp.pad(from_above, ((0, 0), (0, row_count - border), (0, 0)))
    lower_part = jnp.pad(from_below, ((0, 0), (row_count - border, 0), (0, 0)))
    return middle + upper_part + lower_part


def add_surface(cotangent, misfit_row):
    return jnp.concatenate([(cotangent[0] + misfit_row)[None], cotangent[1:]], 0)


def march_steps(initial, stat_pad):

    def step_map(padded_state, drag_field):
        return advance(padded_state, jnp.concatenate([stat_pad[:2], drag_field[None]], 0))

    state = initial
    pullbacks = []
    for number in range(STEPS):
        padded = padded_2(state, (("tile", 1),), 2)
        state, pullback = jax.vjp(step_map, padded, stat_pad[2])
        pullbacks.append(pullback)
    return (state, pullbacks)


def body(start_states, end_adjoints, misfits, water_depth, drag_coef, sea_mask, bottom_level):
    initial = start_states[0]
    adjoint = end_adjoints[0]
    misfit_slab = misfits[0]
    wet_levels = (sea_mask * bottom_level).astype(jnp.float32)
    statics = jnp.stack([water_depth, wet_levels, drag_coef])
    border = 2
    stat_pad = padded_2(statics, (("tile", 1),), border)
    final_state, pullbacks = march_steps(initial, stat_pad)
    cotangent = add_surface(adjoint, misfit_slab[STEPS - 1])
    gradient = jnp.zeros_like(water_depth)
    for number in reversed(range(STEPS)):
        state_part, drag_part = pullbacks[number](cotangent)
        gradient = gradient + drag_part[2:-2]
        from_above = shifted(state_part[:, state_part.shape[1] - 2 :], "tile", 1)
        from_below = shifted(state_part[:, :2], "tile", -1)
        cotangent = settle(state_part, 2, from_above, from_below)
        if number > 0:
            cotangent = add_surface(cotangent, misfit_slab[number - 1])
    next_state = passed_along(final_state, "slab", 1)
    next_adjoint = passed_along(cotangent, "slab", -1)
    drag_total = lax.psum(gradient, "slab")
    return (next_state[None], next_adjoint[None], drag_total)


def solution(mesh):
    return jax.shard_map(
        body,
        mesh=mesh,
        in_specs=(
            P(("groups", "slab"), None, "tile", None),
            P(("groups", "slab"), None, "tile", None),
            P(("groups", "slab"), None, "tile", None),
            P(("groups", "tile"), None),
            P(("groups", "tile"), None),
            P(("groups", "tile"), None),
            P(("groups", "tile"), None),
        ),
        out_specs=(
            P(("groups", "slab"), None, "tile", None),
            P(("groups", "slab"), None, "tile", None),
            P(("groups", "tile"), None),
        ),
        check_vma=False,
    )
```

profile of v0, /device:TPU:1, one launch (start us, length us, event | category | flops | bytes accessed | tf_op | source)
XLA Modules:
  0.0 150.2 jit_solution(8915341922728667692)
XLA Ops:
  2.2 4.5 %collective-permute-start = (f32[3,2,128]{2,1,0:T(2,128)S(1)}, f32[3,2,128]{2,1,0:T(2,128)S(1)}, u32[]{:S(2)}, u32[]{:S(2)}) collective-permute-start(f32[3,2,128]{2,1,0:T(2,128)S(1)} %get-tuple-element.203), channel_id=1, source_target_pairs={{0,4},{4,8},{8,12},{1,5},{5,9},{9,13},{2,6},{6,10},{10,14},{3,7},{... | collective-permute-start | bytes 9224 | tf_op jit(solution)/shard_map/ppermute | solution.py:14
  6.7 1.9 %collective-permute-start.1 = (f32[3,2,128]{2,1,0:T(2,128)S(1)}, f32[3,2,128]{2,1,0:T(2,128)S(1)}, u32[]{:S(2)}, u32[]{:S(2)}) collective-permute-start(f32[3,2,128]{2,1,0:T(2,128)S(1)} %get-tuple-element.204), channel_id=1, source_target_pairs={{4,0},{8,4},{12,8},{5,1},{9,5},{13,9},{6,2},{10,6},{14,10},{7,3},{... | collective-permute-start | bytes 9224 | tf_op jit(solution)/shard_map/ppermute | solution.py:17
  9.7 3.6 %collective-permute-start.2 = (f32[49,2,128]{2,1,0:T(2,128)S(1)}, f32[49,2,128]{2,1,0:T(2,128)S(1)}, u32[]{:S(2)}, u32[]{:S(2)}) collective-permute-start(f32[49,2,128]{2,1,0:T(2,128)S(1)} %get-tuple-element.151), channel_id=1, source_target_pairs={{0,4},{4,8},{8,12},{1,5},{5,9},{9,13},{2,6},{6,10},{10,14},{3,7},{... | collective-permute-start | bytes 150536 | tf_op jit(solution)/shard_map/ppermute | solution.py:14
  13.3 1.9 %collective-permute-start.3 = (f32[49,2,128]{2,1,0:T(2,128)S(1)}, f32[49,2,128]{2,1,0:T(2,128)S(1)}, u32[]{:S(2)}, u32[]{:S(2)}) collective-permute-start(f32[49,2,128]{2,1,0:T(2,128)S(1)} %get-tuple-element.152), channel_id=1, source_target_pairs={{4,0},{8,4},{12,8},{5,1},{9,5},{13,9},{6,2},{10,6},{14,10},{7,3},{... | collective-permute-start | bytes 150536 | tf_op jit(solution)/shard_map/ppermute | solution.py:17
  15.7 3.1 %collective-permute-done.3 = f32[49,2,128]{2,1,0:T(2,128)S(1)} collective-permute-done((f32[49,2,128]{2,1,0:T(2,128)S(1)}, f32[49,2,128]{2,1,0:T(2,128)S(1)}, u32[]{:S(2)}, u32[]{:S(2)}) %collective-permute-start.3) | collective-permute-done | bytes 50208 | tf_op jit(solution)/shard_map/ppermute | solution.py:17
  21.4 1.9 %collective-permute-start.4 = (f32[49,2,128]{2,1,0:T(2,128)S(1)}, f32[49,2,128]{2,1,0:T(2,128)S(1)}, u32[]{:S(2)}, u32[]{:S(2)}) collective-permute-start(f32[49,2,128]{2,1,0:T(2,128)S(1)} %get-tuple-element.149), channel_id=1, source_target_pairs={{0,4},{4,8},{8,12},{1,5},{5,9},{9,13},{2,6},{6,10},{10,14},{3,7},{... | collective-permute-start | bytes 150536 | tf_op jit(solution)/shard_map/ppermute | solution.py:14
  23.4 2.4 %collective-permute-start.5 = (f32[49,2,128]{2,1,0:T(2,128)S(1)}, f32[49,2,128]{2,1,0:T(2,128)S(1)}, u32[]{:S(2)}, u32[]{:S(2)}) collective-permute-start(f32[49,2,128]{2,1,0:T(2,128)S(1)} %get-tuple-element.150), channel_id=1, source_target_pairs={{4,0},{8,4},{12,8},{5,1},{9,5},{13,9},{6,2},{10,6},{14,10},{7,3},{... | collective-permute-start | bytes 150536 | tf_op jit(solution)/shard_map/ppermute | solution.py:17
  25.8 3.0 %collective-permute-done.5 = f32[49,2,128]{2,1,0:T(2,128)S(1)} collective-permute-done((f32[49,2,128]{2,1,0:T(2,128)S(1)}, f32[49,2,128]{2,1,0:T(2,128)S(1)}, u32[]{:S(2)}, u32[]{:S(2)}) %collective-permute-start.5) | collective-permute-done | bytes 50208 | tf_op jit(solution)/shard_map/ppermute | solution.py:17
  31.4 1.9 %collective-permute-start.6 = (f32[49,2,128]{2,1,0:T(2,128)S(1)}, f32[49,2,128]{2,1,0:T(2,128)S(1)}, u32[]{:S(2)}, u32[]{:S(2)}) collective-permute-start(f32[49,2,128]{2,1,0:T(2,128)S(1)} %get-tuple-element.147), channel_id=1, source_target_pairs={{0,4},{4,8},{8,12},{1,5},{5,9},{9,13},{2,6},{6,10},{10,14},{3,7},{... | collective-permute-start | bytes 150536 | tf_op jit(solution)/shard_map/ppermute | solution.py:14
  33.4 2.4 %collective-permute-start.7 = (f32[49,2,128]{2,1,0:T(2,128)S(1)}, f32[49,2,128]{2,1,0:T(2,128)S(1)}, u32[]{:S(2)}, u32[]{:S(2)}) collective-permute-start(f32[49,2,128]{2,1,0:T(2,128)S(1)} %get-tuple-element.148), channel_id=1, source_target_pairs={{4,0},{8,4},{12,8},{5,1},{9,5},{13,9},{6,2},{10,6},{14,10},{7,3},{... | collective-permute-start | bytes 150536 | tf_op jit(solution)/shard_map/ppermute | solution.py:17
  35.8 3.0 %collective-permute-done.7 = f32[49,2,128]{2,1,0:T(2,128)S(1)} collective-permute-done((f32[49,2,128]{2,1,0:T(2,128)S(1)}, f32[49,2,128]{2,1,0:T(2,128)S(1)}, u32[]{:S(2)}, u32[]{:S(2)}) %collective-permute-start.7) | collective-permute-done | bytes 50208 | tf_op jit(solution)/shard_map/ppermute | solution.py:17
  41.5 2.1 %collective-permute-start.8 = (f32[49,2,128]{2,1,0:T(2,128)S(1)}, f32[49,2,128]{2,1,0:T(2,128)S(1)}, u32[]{:S(2)}, u32[]{:S(2)}) collective-permute-start(f32[49,2,128]{2,1,0:T(2,128)S(1)} %get-tuple-element.145), channel_id=1, source_target_pairs={{0,4},{4,8},{8,12},{1,5},{5,9},{9,13},{2,6},{6,10},{10,14},{3,7},{... | collective-permute-start | bytes 150536 | tf_op jit(solution)/shard_map/ppermute | solution.py:14
  43.6 2.6 %collective-permute-start.9 = (f32[49,2,128]{2,1,0:T(2,128)S(1)}, f32[49,2,128]{2,1,0:T(2,128)S(1)}, u32[]{:S(2)}, u32[]{:S(2)}) collective-permute-start(f32[49,2,128]{2,1,0:T(2,128)S(1)} %get-tuple-element.146), channel_id=1, source_target_pairs={{4,0},{8,4},{12,8},{5,1},{9,5},{13,9},{6,2},{10,6},{14,10},{7,3},{... | collective-permute-start | bytes 150536 | tf_op jit(solution)/shard_map/ppermute | solution.py:17
  46.2 2.8 %collective-permute-done.9 = f32[49,2,128]{2,1,0:T(2,128)S(1)} collective-permute-done((f32[49,2,128]{2,1,0:T(2,128)S(1)}, f32[49,2,128]{2,1,0:T(2,128)S(1)}, u32[]{:S(2)}, u32[]{:S(2)}) %collective-permute-start.9) | collective-permute-done | bytes 50208 | tf_op jit(solution)/shard_map/ppermute | solution.py:17
  54.4 1.9 %collective-permute-start.11 = (f32[49,2,128]{2,1,0:T(2,128)S(1)}, f32[49,2,128]{2,1,0:T(2,128)S(1)}, u32[]{:S(2)}, u32[]{:S(2)}) collective-permute-start(f32[49,2,128]{2,1,0:T(2,128)S(1)} %get-tuple-element.132), channel_id=1, source_target_pairs={{0,4},{4,8},{8,12},{1,5},{5,9},{9,13},{2,6},{6,10},{10,14},{3,7},{... | collective-permute-start | bytes 150536 | tf_op jit(solution)/shard_map/ppermute | solution.py:25
  56.4 2.4 %collective-permute-start.12 = (f32[49,2,128]{2,1,0:T(2,128)S(1)}, f32[49,2,128]{2,1,0:T(2,128)S(1)}, u32[]{:S(2)}, u32[]{:S(2)}) collective-permute-start(f32[49,2,128]{2,1,0:T(2,128)S(1)} %get-tuple-element.133), channel_id=1, source_target_pairs={{4,0},{8,4},{12,8},{5,1},{9,5},{13,9},{6,2},{10,6},{14,10},{7,3},{... | collective-permute-start | bytes 150536 | tf_op jit(solution)/shard_map/ppermute | solution.py:25
  59.0 1.3 collective-permute-start.10
  60.3 1.5 collective-permute-done.12
  65.8 2.0 %collective-permute-start.13 = (f32[49,2,128]{2,1,0:T(2,128)S(1)}, f32[49,2,128]{2,1,0:T(2,128)S(1)}, u32[]{:S(2)}, u32[]{:S(2)}) collective-permute-start(f32[49,2,128]{2,1,0:T(2,128)S(1)} %get-tuple-element.130), channel_id=1, source_target_pairs={{0,4},{4,8},{8,12},{1,5},{5,9},{9,13},{2,6},{6,10},{10,14},{3,7},{... | collective-permute-start | bytes 150536 | tf_op jit(solution)/shard_map/ppermute | solution.py:25
  67.7 2.6 %collective-permute-start.14 = (f32[49,2,128]{2,1,0:T(2,128)S(1)}, f32[49,2,128]{2,1,0:T(2,128)S(1)}, u32[]{:S(2)}, u32[]{:S(2)}) collective-permute-start(f32[49,2,128]{2,1,0:T(2,128)S(1)} %get-tuple-element.131), channel_id=1, source_target_pairs={{4,0},{8,4},{12,8},{5,1},{9,5},{13,9},{6,2},{10,6},{14,10},{7,3},{... | collective-permute-start | bytes 150536 | tf_op jit(solution)/shard_map/ppermute | solution.py:25
  70.5 3.0 %collective-permute-done.14 = f32[49,2,128]{2,1,0:T(2,128)S(1)} collective-permute-done((f32[49,2,128]{2,1,0:T(2,128)S(1)}, f32[49,2,128]{2,1,0:T(2,128)S(1)}, u32[]{:S(2)}, u32[]{:S(2)}) %collective-permute-start.14) | collective-permute-done | bytes 50208 | tf_op jit(solution)/shard_map/ppermute | solution.py:25
  77.4 1.9 %collective-permute-start.15 = (f32[49,2,128]{2,1,0:T(2,128)S(1)}, f32[49,2,128]{2,1,0:T(2,128)S(1)}, u32[]{:S(2)}, u32[]{:S(2)}) collective-permute-start(f32[49,2,128]{2,1,0:T(2,128)S(1)} %get-tuple-element.128), channel_id=1, source_target_pairs={{0,4},{4,8},{8,12},{1,5},{5,9},{9,13},{2,6},{6,10},{10,14},{3,7},{... | collective-permute-start | bytes 150536 | tf_op jit(solution)/shard_map/ppermute | solution.py:25
  79.4 2.4 %collective-permute-start.16 = (f32[49,2,128]{2,1,0:T(2,128)S(1)}, f32[49,2,128]{2,1,0:T(2,128)S(1)}, u32[]{:S(2)}, u32[]{:S(2)}) collective-permute-start(f32[49,2,128]{2,1,0:T(2,128)S(1)} %get-tuple-element.129), channel_id=1, source_target_pairs={{4,0},{8,4},{12,8},{5,1},{9,5},{13,9},{6,2},{10,6},{14,10},{7,3},{... | collective-permute-start | bytes 150536 | tf_op jit(solution)/shard_map/ppermute | solution.py:25
  81.9 3.2 %collective-permute-done.16 = f32[49,2,128]{2,1,0:T(2,128)S(1)} collective-permute-done((f32[49,2,128]{2,1,0:T(2,128)S(1)}, f32[49,2,128]{2,1,0:T(2,128)S(1)}, u32[]{:S(2)}, u32[]{:S(2)}) %collective-permute-start.16) | collective-permute-done | bytes 50208 | tf_op jit(solution)/shard_map/ppermute | solution.py:25
  89.1 1.9 %collective-permute-start.17 = (f32[49,2,128]{2,1,0:T(2,128)S(1)}, f32[49,2,128]{2,1,0:T(2,128)S(1)}, u32[]{:S(2)}, u32[]{:S(2)}) collective-permute-start(f32[49,2,128]{2,1,0:T(2,128)S(1)} %get-tuple-element.126), channel_id=1, source_target_pairs={{0,4},{4,8},{8,12},{1,5},{5,9},{9,13},{2,6},{6,10},{10,14},{3,7},{... | collective-permute-start | bytes 150536 | tf_op jit(solution)/shard_map/ppermute | solution.py:25
  91.0 2.4 %collective-permute-start.18 = (f32[49,2,128]{2,1,0:T(2,128)S(1)}, f32[49,2,128]{2,1,0:T(2,128)S(1)}, u32[]{:S(2)}, u32[]{:S(2)}) collective-permute-start(f32[49,2,128]{2,1,0:T(2,128)S(1)} %get-tuple-element.127), channel_id=1, source_target_pairs={{4,0},{8,4},{12,8},{5,1},{9,5},{13,9},{6,2},{10,6},{14,10},{7,3},{... | collective-permute-start | bytes 150536 | tf_op jit(solution)/shard_map/ppermute | solution.py:25
  93.6 3.2 %collective-permute-done.18 = f32[49,2,128]{2,1,0:T(2,128)S(1)} collective-permute-done((f32[49,2,128]{2,1,0:T(2,128)S(1)}, f32[49,2,128]{2,1,0:T(2,128)S(1)}, u32[]{:S(2)}, u32[]{:S(2)}) %collective-permute-start.18) | collective-permute-done | bytes 50208 | tf_op jit(solution)/shard_map/ppermute | solution.py:25
  96.7 1.4 fusion
  98.1 3.3 %collective-permute-start.19 = (f32[49,64,128]{2,1,0:T(8,128)}, f32[49,64,128]{2,1,0:T(8,128)}, u32[]{:S(2)}, u32[]{:S(2)}) collective-permute-start(f32[49,64,128]{2,1,0:T(8,128)} %fusion), channel_id=1, source_target_pairs={{1,0},{2,1},{3,2},{0,3},{5,4},{6,5},{7,6},{4,7},{9,8},{10,9},{11,1... | collective-permute-start | bytes 4816904 | tf_op jit(solution)/shard_map/ppermute | solution.py:31
  101.5 44.8 %psum.7 = f32[64,128]{1,0:T(8,128)} all-reduce(f32[64,128]{1,0:T(8,128)S(1)} %fusion.112), channel_id=1, replica_groups=mesh['groups'=2,'tile'=4,'slab'=4] {'slab'}, use_global_device_ids=true, to_apply=%region_32.33 | all-reduce | flops 8192 | bytes 65536 | tf_op jit(solution)/shard_map/psum | solution.py:131
  146.3 1.2 copy.12
  147.5 2.8 %copy.13 = f32[1,49,64,128]{3,2,1,0:T(8,128)} copy(f32[1,49,64,128]{3,2,1,0:T(8,128)} %bitcast.29) | data formatting | bytes 3211264
  (182 shorter events, 28.2 us)
Async XLA Ops:
  2.2 13.1 %collective-permute-start = (f32[3,2,128]{2,1,0:T(2,128)S(1)}, f32[3,2,128]{2,1,0:T(2,128)S(1)}, u32[]{:S(2)}, u32[]{:S(2)}) collective-permute-start(f32[3,2,128]{2,1,0:T(2,128)S(1)} %get-tuple-element.203), channel_id=1, source_target_pairs={{0,4},{4,8},{8,12},{1,5},{5,9},{9,13},{2,6},{6,10},{10,14},{3,7},{... | collective-permute-start | bytes 9224 | tf_op jit(solution)/shard_map/ppermute | solution.py:14
  6.7 8.6 %collective-permute-start.1 = (f32[3,2,128]{2,1,0:T(2,128)S(1)}, f32[3,2,128]{2,1,0:T(2,128)S(1)}, u32[]{:S(2)}, u32[]{:S(2)}) collective-permute-start(f32[3,2,128]{2,1,0:T(2,128)S(1)} %get-tuple-element.204), channel_id=1, source_target_pairs={{4,0},{8,4},{12,8},{5,1},{9,5},{13,9},{6,2},{10,6},{14,10},{7,3},{... | collective-permute-start | bytes 9224 | tf_op jit(solution)/shard_map/ppermute | solution.py:17
  9.7 6.0 %collective-permute-start.2 = (f32[49,2,128]{2,1,0:T(2,128)S(1)}, f32[49,2,128]{2,1,0:T(2,128)S(1)}, u32[]{:S(2)}, u32[]{:S(2)}) collective-permute-start(f32[49,2,128]{2,1,0:T(2,128)S(1)} %get-tuple-element.151), channel_id=1, source_target_pairs={{0,4},{4,8},{8,12},{1,5},{5,9},{9,13},{2,6},{6,10},{10,14},{3,7},{... | collective-permute-start | bytes 150536 | tf_op jit(solution)/shard_map/ppermute | solution.py:14
  13.3 5.4 %collective-permute-start.3 = (f32[49,2,128]{2,1,0:T(2,128)S(1)}, f32[49,2,128]{2,1,0:T(2,128)S(1)}, u32[]{:S(2)}, u32[]{:S(2)}) collective-permute-start(f32[49,2,128]{2,1,0:T(2,128)S(1)} %get-tuple-element.152), channel_id=1, source_target_pairs={{4,0},{8,4},{12,8},{5,1},{9,5},{13,9},{6,2},{10,6},{14,10},{7,3},{... | collective-permute-start | bytes 150536 | tf_op jit(solution)/shard_map/ppermute | solution.py:17
  15.4 3.3 %copy-start = (f32[1,49,64,128]{3,2,1,0:T(8,128)S(1)}, f32[1,49,64,128]{3,2,1,0:T(8,128)}, u32[]{:S(2)}) copy-start(f32[1,49,64,128]{3,2,1,0:T(8,128)} %param.7) | copy-start | bytes 4816900
  15.6 3.5 %copy-start.2 = (f32[64,128]{1,0:T(8,128)S(1)}, f32[64,128]{1,0:T(8,128)}, u32[]{:S(2)}) copy-start(f32[64,128]{1,0:T(8,128)} %param.11) | copy-start | bytes 98308
  15.6 3.5 %copy-start.3 = (f32[64,128]{1,0:T(8,128)S(1)}, f32[64,128]{1,0:T(8,128)}, u32[]{:S(2)}) copy-start(f32[64,128]{1,0:T(8,128)} %param.10) | copy-start | bytes 98308
  21.4 4.3 %collective-permute-start.4 = (f32[49,2,128]{2,1,0:T(2,128)S(1)}, f32[49,2,128]{2,1,0:T(2,128)S(1)}, u32[]{:S(2)}, u32[]{:S(2)}) collective-permute-start(f32[49,2,128]{2,1,0:T(2,128)S(1)} %get-tuple-element.149), channel_id=1, source_target_pairs={{0,4},{4,8},{8,12},{1,5},{5,9},{9,13},{2,6},{6,10},{10,14},{3,7},{... | collective-permute-start | bytes 150536 | tf_op jit(solution)/shard_map/ppermute | solution.py:14
  23.4 5.4 %collective-permute-start.5 = (f32[49,2,128]{2,1,0:T(2,128)S(1)}, f32[49,2,128]{2,1,0:T(2,128)S(1)}, u32[]{:S(2)}, u32[]{:S(2)}) collective-permute-start(f32[49,2,128]{2,1,0:T(2,128)S(1)} %get-tuple-element.150), channel_id=1, source_target_pairs={{4,0},{8,4},{12,8},{5,1},{9,5},{13,9},{6,2},{10,6},{14,10},{7,3},{... | collective-permute-start | bytes 150536 | tf_op jit(solution)/shard_map/ppermute | solution.py:17
  31.4 4.3 %collective-permute-start.6 = (f32[49,2,128]{2,1,0:T(2,128)S(1)}, f32[49,2,128]{2,1,0:T(2,128)S(1)}, u32[]{:S(2)}, u32[]{:S(2)}) collective-permute-start(f32[49,2,128]{2,1,0:T(2,128)S(1)} %get-tuple-element.147), channel_id=1, source_target_pairs={{0,4},{4,8},{8,12},{1,5},{5,9},{9,13},{2,6},{6,10},{10,14},{3,7},{... | collective-permute-start | bytes 150536 | tf_op jit(solution)/shard_map/ppermute | solution.py:14
  33.4 5.4 %collective-permute-start.7 = (f32[49,2,128]{2,1,0:T(2,128)S(1)}, f32[49,2,128]{2,1,0:T(2,128)S(1)}, u32[]{:S(2)}, u32[]{:S(2)}) collective-permute-start(f32[49,2,128]{2,1,0:T(2,128)S(1)} %get-tuple-element.148), channel_id=1, source_target_pairs={{4,0},{8,4},{12,8},{5,1},{9,5},{13,9},{6,2},{10,6},{14,10},{7,3},{... | collective-permute-start | bytes 150536 | tf_op jit(solution)/shard_map/ppermute | solution.py:17
  40.8 5.4 %copy-start.4 = (f32[1,4,64,128]{3,2,1,0:T(8,128)S(1)}, f32[1,4,64,128]{3,2,1,0:T(8,128)}, u32[]{:S(2)}) copy-start(f32[1,4,64,128]{3,2,1,0:T(8,128)} %param.9) | copy-start | bytes 393220
  41.5 4.7 %copy-start.1 = (f32[1,49,64,128]{3,2,1,0:T(8,128)S(1)}, f32[1,49,64,128]{3,2,1,0:T(8,128)}, u32[]{:S(2)}) copy-start(f32[1,49,64,128]{3,2,1,0:T(8,128)} %param.8) | copy-start | bytes 4816900
  41.5 4.7 %collective-permute-start.8 = (f32[49,2,128]{2,1,0:T(2,128)S(1)}, f32[49,2,128]{2,1,0:T(2,128)S(1)}, u32[]{:S(2)}, u32[]{:S(2)}) collective-permute-start(f32[49,2,128]{2,1,0:T(2,128)S(1)} %get-tuple-element.145), channel_id=1, source_target_pairs={{0,4},{4,8},{8,12},{1,5},{5,9},{9,13},{2,6},{6,10},{10,14},{3,7},{... | collective-permute-start | bytes 150536 | tf_op jit(solution)/shard_map/ppermute | solution.py:14
  43.6 5.4 %collective-permute-start.9 = (f32[49,2,128]{2,1,0:T(2,128)S(1)}, f32[49,2,128]{2,1,0:T(2,128)S(1)}, u32[]{:S(2)}, u32[]{:S(2)}) collective-permute-start(f32[49,2,128]{2,1,0:T(2,128)S(1)} %get-tuple-element.146), channel_id=1, source_target_pairs={{4,0},{8,4},{12,8},{5,1},{9,5},{13,9},{6,2},{10,6},{14,10},{7,3},{... | collective-permute-start | bytes 150536 | tf_op jit(solution)/shard_map/ppermute | solution.py:17
  54.4 5.9 %collective-permute-start.11 = (f32[49,2,128]{2,1,0:T(2,128)S(1)}, f32[49,2,128]{2,1,0:T(2,128)S(1)}, u32[]{:S(2)}, u32[]{:S(2)}) collective-permute-start(f32[49,2,128]{2,1,0:T(2,128)S(1)} %get-tuple-element.132), channel_id=1, source_target_pairs={{0,4},{4,8},{8,12},{1,5},{5,9},{9,13},{2,6},{6,10},{10,14},{3,7},{... | collective-permute-start | bytes 150536 | tf_op jit(solution)/shard_map/ppermute | solution.py:25
  56.4 5.4 %collective-permute-start.12 = (f32[49,2,128]{2,1,0:T(2,128)S(1)}, f32[49,2,128]{2,1,0:T(2,128)S(1)}, u32[]{:S(2)}, u32[]{:S(2)}) collective-permute-start(f32[49,2,128]{2,1,0:T(2,128)S(1)} %get-tuple-element.133), channel_id=1, source_target_pairs={{4,0},{8,4},{12,8},{5,1},{9,5},{13,9},{6,2},{10,6},{14,10},{7,3},{... | collective-permute-start | bytes 150536 | tf_op jit(solution)/shard_map/ppermute | solution.py:25
  59.0 87.4 %collective-permute-start.10 = (f32[49,64,128]{2,1,0:T(8,128)S(1)}, f32[49,64,128]{2,1,0:T(8,128)S(1)}, u32[]{:S(2)}, u32[]{:S(2)}) collective-permute-start(f32[49,64,128]{2,1,0:T(8,128)S(1)} %pad_maximum_fusion), channel_id=1, source_target_pairs={{3,0},{0,1},{1,2},{2,3},{7,4},{4,5},{5,6},{6,7},{11,8},{8,9},{9,10... | collective-permute-start | bytes 4816904 | tf_op jit(solution)/shard_map/ppermute | solution.py:31
  65.8 4.7 %collective-permute-start.13 = (f32[49,2,128]{2,1,0:T(2,128)S(1)}, f32[49,2,128]{2,1,0:T(2,128)S(1)}, u32[]{:S(2)}, u32[]{:S(2)}) collective-permute-start(f32[49,2,128]{2,1,0:T(2,128)S(1)} %get-tuple-element.130), channel_id=1, source_target_pairs={{0,4},{4,8},{8,12},{1,5},{5,9},{9,13},{2,6},{6,10},{10,14},{3,7},{... | collective-permute-start | bytes 150536 | tf_op jit(solution)/shard_map/ppermute | solution.py:25
  67.7 5.7 %collective-permute-start.14 = (f32[49,2,128]{2,1,0:T(2,128)S(1)}, f32[49,2,128]{2,1,0:T(2,128)S(1)}, u32[]{:S(2)}, u32[]{:S(2)}) collective-permute-start(f32[49,2,128]{2,1,0:T(2,128)S(1)} %get-tuple-element.131), channel_id=1, source_target_pairs={{4,0},{8,4},{12,8},{5,1},{9,5},{13,9},{6,2},{10,6},{14,10},{7,3},{... | collective-permute-start | bytes 150536 | tf_op jit(solution)/shard_map/ppermute | solution.py:25
  77.4 4.5 %collective-permute-start.15 = (f32[49,2,128]{2,1,0:T(2,128)S(1)}, f32[49,2,128]{2,1,0:T(2,128)S(1)}, u32[]{:S(2)}, u32[]{:S(2)}) collective-permute-start(f32[49,2,128]{2,1,0:T(2,128)S(1)} %get-tuple-element.128), channel_id=1, source_target_pairs={{0,4},{4,8},{8,12},{1,5},{5,9},{9,13},{2,6},{6,10},{10,14},{3,7},{... | collective-permute-start | bytes 150536 | tf_op jit(solution)/shard_map/ppermute | solution.py:25
  79.4 5.7 %collective-permute-start.16 = (f32[49,2,128]{2,1,0:T(2,128)S(1)}, f32[49,2,128]{2,1,0:T(2,128)S(1)}, u32[]{:S(2)}, u32[]{:S(2)}) collective-permute-start(f32[49,2,128]{2,1,0:T(2,128)S(1)} %get-tuple-element.129), channel_id=1, source_target_pairs={{4,0},{8,4},{12,8},{5,1},{9,5},{13,9},{6,2},{10,6},{14,10},{7,3},{... | collective-permute-start | bytes 150536 | tf_op jit(solution)/shard_map/ppermute | solution.py:25
  89.1 4.5 %collective-permute-start.17 = (f32[49,2,128]{2,1,0:T(2,128)S(1)}, f32[49,2,128]{2,1,0:T(2,128)S(1)}, u32[]{:S(2)}, u32[]{:S(2)}) collective-permute-start(f32[49,2,128]{2,1,0:T(2,128)S(1)} %get-tuple-element.126), channel_id=1, source_target_pairs={{0,4},{4,8},{8,12},{1,5},{5,9},{9,13},{2,6},{6,10},{10,14},{3,7},{... | collective-permute-start | bytes 150536 | tf_op jit(solution)/shard_map/ppermute | solution.py:25
  91.0 5.7 %collective-permute-start.18 = (f32[49,2,128]{2,1,0:T(2,128)S(1)}, f32[49,2,128]{2,1,0:T(2,128)S(1)}, u32[]{:S(2)}, u32[]{:S(2)}) collective-permute-start(f32[49,2,128]{2,1,0:T(2,128)S(1)} %get-tuple-element.127), channel_id=1, source_target_pairs={{4,0},{8,4},{12,8},{5,1},{9,5},{13,9},{6,2},{10,6},{14,10},{7,3},{... | collective-permute-start | bytes 150536 | tf_op jit(solution)/shard_map/ppermute | solution.py:25
  98.1 48.2 %collective-permute-start.19 = (f32[49,64,128]{2,1,0:T(8,128)}, f32[49,64,128]{2,1,0:T(8,128)}, u32[]{:S(2)}, u32[]{:S(2)}) collective-permute-start(f32[49,64,128]{2,1,0:T(8,128)} %fusion), channel_id=1, source_target_pairs={{1,0},{2,1},{3,2},{0,3},{5,4},{6,5},{7,6},{4,7},{9,8},{10,9},{11,1... | collective-permute-start | bytes 4816904 | tf_op jit(solution)/shard_map/ppermute | solution.py:31
where the time goes:
time: 153 us; the launch traced here: 150 us
  starting transfers between devices  47.4 us (31%)
  blocking collectives  44.8 us (29%)
  other arithmetic  25.3 us (17%)
  waiting for transfers between devices  22.7 us (15%)
  local copies, waits for them, and re-layouts  8.13 us (5%)
  between operations  1.86 us (1%)
    psum x1, blocking collectives, body(): drag_total = lax.psum(gradient, 'slab')  44.8 us
    ppermute x8, starting transfers between devices, shifted(): return lax.ppermute(block, axis, route)  17.5 us
    ppermute x5, starting transfers between devices, padded_2(): lax.ppermute(lax.slice_in_dim(block, block.shape[dim] - width, None, axis...  14 us
    ppermute x5, waiting for transfers between devices, padded_2(): lax.ppermute(lax.slice_in_dim(block, 0, width, axis=dim), axis, backward)  11.8 us
    ppermute x5, starting transfers between devices, padded_2(): lax.ppermute(lax.slice_in_dim(block, 0, width, axis=dim), axis, backward)  11.2 us
    ppermute x8, waiting for transfers between devices, shifted(): return lax.ppermute(block, axis, route)  10.8 us
    ppermute x2, starting transfers between devices, passed_along(): return lax.ppermute(block, axis, route)  4.62 us
    unnamed x12, local copies, waits for them, and re-layouts  3.94 us
  transfers between devices with their start and end apart: 20, of which 8 were waited for; matrix products, arithmetic and copies ran while one was open for 10% of the time, Pallas kernels for 0%

commit v1 on v0

v1 whole, which is shorter than its diff:
```python
import jax
import jax.numpy as jnp
from jax import lax
from jax.experimental import pallas as pl
from jax.experimental.pallas import tpu as pltpu
from jax.sharding import PartitionSpec as P

STEPS = 4
BLOCK = 8
HALO = 2 * STEPS
SAVED = 2 + 2 * STEPS


def shifted(block, axis, distance):
    devices = range(lax.axis_size(axis))
    route = [(i - distance, i) for i in devices if i - distance in devices]
    return lax.ppermute(block, axis, route)


def passed_along(block, axis, distance):
    devices = range(lax.axis_size(axis))
    route = [((i - distance) % len(devices), i) for i in devices]
    return lax.ppermute(block, axis, route)


def row_diff(values):
    return pltpu.roll(values, values.shape[0] - 1, 0) - pltpu.roll(values, 1, 0)


def column_diff(values):
    width = values.shape[1]
    lane = lax.broadcasted_iota(jnp.int32, values.shape, 1)
    after = jnp.where(lane < width - 1, pltpu.roll(values, width - 1, 1), 0.0)
    before = jnp.where(lane > 0, pltpu.roll(values, 1, 1), 0.0)
    return after - before


def over_blocks(rows, with_halo, visit, own, above, below):
    if with_halo:
        visit(pl.ds(0, BLOCK), above, pl.ds(0, BLOCK))

    def inner(index, carry):
        start = pl.multiple_of(index * BLOCK, BLOCK)
        visit(pl.ds(pl.multiple_of(start + HALO, BLOCK), BLOCK), own, pl.ds(start, BLOCK))
        return carry

    lax.fori_loop(0, rows // BLOCK, inner, 0)
    if with_halo:
        visit(pl.ds(HALO + rows, BLOCK), below, pl.ds(0, BLOCK))


def fill_padded(target, own, above, below):
    rows = own.shape[0]
    target[0:HALO] = above
    target[HALO : HALO + rows] = own
    target[HALO + rows : rows + 2 * HALO] = below


def drag_terms(u_bottom, v_bottom, thickness, drag, sea):
    speed = jnp.sqrt(u_bottom * u_bottom + v_bottom * v_bottom + 0.0025)
    denominator = thickness + 0.1 * drag * speed + 1.0 - sea
    return speed, denominator, thickness / denominator


def forward_kernel(state, above, below, depth, wet, drag, final, saved,
                   work, wet_pad, thick, drag_pad, eta, sum_u, sum_v, bot_u, bot_v, slope_x, slope_y, factor):
    fields, rows, _ = state.shape
    levels = (fields - 1) // 2
    fill_padded(wet_pad, wet[...], above[fields + 1], below[fields + 1])
    fill_padded(drag_pad, drag[...], above[fields + 2], below[fields + 2])
    fill_padded(thick, depth[...], above[fields], below[fields])
    fill_padded(eta, state[0], above[0], below[0])
    thick[...] = thick[...] / jnp.maximum(wet_pad[...], 1.0)

    def sums(at, source, source_at):
        wet_here = wet_pad[at]
        total_u = total_v = low_u = low_v = jnp.zeros_like(wet_here)
        for level in range(levels):
            active = wet_here > level
            bottom = wet_here == level + 1
            u = jnp.where(active, source[1 + level, source_at], 0.0)
            v = jnp.where(active, source[1 + levels + level, source_at], 0.0)
            total_u += u
            total_v += v
            low_u = jnp.where(bottom, u, low_u)
            low_v = jnp.where(bottom, v, low_v)
        sum_u[at] = total_u
        sum_v[at] = total_v
        bot_u[at] = low_u
        bot_v[at] = low_v

    over_blocks(rows, True, sums, state, above, below)
    saved[0] = bot_u[HALO : HALO + rows]
    saved[1] = bot_v[HALO : HALO + rows]

    for step in range(STEPS):
        first, last = step == 0, step == STEPS - 1
        sea = jnp.minimum(wet_pad[...], 1.0)
        flux_x = thick[...] * sum_u[...]
        flux_y = thick[...] * sum_v[...]
        surface = sea * (eta[...] - 0.2 * (row_diff(flux_x) + column_diff(flux_y)))
        eta[...] = surface
        slope_x[...] = 0.2 * row_diff(surface)
        slope_y[...] = 0.2 * column_diff(surface)
        factor[...] = drag_terms(bot_u[...], bot_v[...], thick[...], drag_pad[...], sea)[2]

        def update(at, source, source_at):
            wet_here = wet_pad[at]
            slow = factor[at]
            grad_x = slope_x[at]
            grad_y = slope_y[at]
            zero = jnp.zeros_like(wet_here)
            total_u = total_v = low_u = low_v = zero

            def fetch(level):
                if level == levels:
                    return zero, zero
                u = source[1 + level, source_at]
                v = source[1 + levels + level, source_at]
                if first:
                    u = jnp.where(wet_here > level, u, 0.0)
                    v = jnp.where(wet_here > level, v, 0.0)
                return u, v

            u_up = v_up = zero
            u, v = fetch(0)
            for level in range(levels):
                u_down, v_down = fetch(level + 1)
                inside = wet_here > level + 1
                bottom = wet_here == level + 1
                own = 1.0 if level == 0 else 0.9
                weight = jnp.where(inside, own - 0.1, own)
                retain = jnp.where(inside, 1.0, jnp.where(bottom, slow, 0.0))
                ut = weight * u + 0.1 * (v + u_up + u_down) - grad_x
                vt = weight * v + 0.1 * (v_up + v_down - u) - grad_y
                low_u = jnp.where(bottom, ut, low_u)
                low_v = jnp.where(bottom, vt, low_v)
                u_new = ut * retain
                v_new = vt * retain
                if last:
                    final[1 + level, source_at] = u_new
                    final[1 + levels + level, source_at] = v_new
                else:
                    work[1 + level, at] = u_new
                    work[1 + levels + level, at] = v_new
                    total_u += u_new
                    total_v += v_new
                u_up, v_up, u, v = u, v, u_down, v_down
            sum_u[at] = total_u
            sum_v[at] = total_v
            bot_u[at] = low_u
            bot_v[at] = low_v

        if first:
            over_blocks(rows, True, update, state, above, below)
        else:
            def inner(index, carry):
                start = pl.multiple_of(index * BLOCK, BLOCK)
                if last:
                    at = pl.ds(pl.multiple_of(start + HALO, BLOCK), BLOCK)
                    load = at
                else:
                    at = load = pl.ds(start, BLOCK)

                class Source:
                    def __getitem__(self, key):
                        return work[key[0], load]

                update(at, Source(), pl.ds(start, BLOCK))
                return carry

            lax.fori_loop(0, rows // BLOCK if last else (rows + 2 * HALO) // BLOCK, inner, 0)
        saved[2 + 2 * step] = bot_u[HALO : HALO + rows]
        saved[3 + 2 * step] = bot_v[HALO : HALO + rows]
        bot_u[...] = factor[...] * bot_u[...]
        bot_v[...] = factor[...] * bot_v[...]
    final[0] = eta[HALO : HALO + rows]


def adjoint_kernel(adjoint, misfit, saved, above, below, depth, wet, drag, stat_above, stat_below,
                   start, gradient,
                   work, kept, wet_pad, thick, drag_pad, eta, sum_u, sum_v, bot_u, bot_v,
                   push_x, push_y, push_low_x, push_low_y, factor, grad_pad):
    fields, rows, _ = adjoint.shape
    levels = (fields - 1) // 2
    miss_at, saved_at = fields, fields + STEPS
    fill_padded(wet_pad, wet[...], stat_above[1], stat_below[1])
    fill_padded(drag_pad, drag[...], stat_above[2], stat_below[2])
    fill_padded(thick, depth[...], stat_above[0], stat_below[0])
    thick[...] = thick[...] / jnp.maximum(wet_pad[...], 1.0)
    for item in range(SAVED):
        fill_padded(kept.at[item], saved[item], above[saved_at + item], below[saved_at + item])
    fill_padded(eta, adjoint[0], above[0], below[0])
    grad_pad[...] = jnp.zeros_like(grad_pad)
    sea = jnp.minimum(wet_pad[...], 1.0)

    before = [(kept[0], kept[1])]
    for step in range(STEPS - 1):
        slow = drag_terms(*before[step], thick[...], drag_pad[...], sea)[2]
        before.append((slow * kept[2 + 2 * step], slow * kept[3 + 2 * step]))

    def sums(at, source, source_at):
        wet_here = wet_pad[at]
        total_u = total_v = low_u = low_v = jnp.zeros_like(wet_here)
        for level in range(levels):
            active = wet_here > level
            bottom = wet_here == level + 1
            u = jnp.where(active, source[1 + level, source_at], 0.0)
            v = jnp.where(active, source[1 + levels + level, source_at], 0.0)
            total_u += u
            total_v += v
            low_u = jnp.where(bottom, u, low_u)
            low_v = jnp.where(bottom, v, low_v)
        sum_u[at] = total_u
        sum_v[at] = total_v
        bot_u[at] = low_u
        bot_v[at] = low_v

    over_blocks(rows, True, sums, adjoint, above, below)

    for step in reversed(range(STEPS)):
        first, last = step == STEPS - 1, step == 0
        sea = jnp.minimum(wet_pad[...], 1.0)
        fill_padded(push_x, misfit[step], above[miss_at + step], below[miss_at + step])
        u_before, v_before = before[step]
        speed, denominator, slow = drag_terms(u_before, v_before, thick[...], drag_pad[...], sea)
        factor[...] = slow
        low_u, low_v = bot_u[...], bot_v[...]
        on_factor = low_u * kept[2 + 2 * step] + low_v * kept[3 + 2 * step]
        on_denominator = -on_factor * slow / denominator
        grad_pad[...] += 0.1 * speed * on_denominator
        on_speed = 0.1 * drag_pad[...] * on_denominator / speed
        loss = 1.0 - slow
        total_x = sum_u[...] - loss * low_u
        total_y = sum_v[...] - loss * low_v
        surface = sea * (eta[...] + push_x[...] + 0.2 * (row_diff(total_x) + column_diff(total_y)))
        eta[...] = surface
        thin = 0.2 * thick[...]
        toward_x = thin * row_diff(surface)
        toward_y = thin * column_diff(surface)
        push_x[...] = toward_x
        push_y[...] = toward_y
        push_low_x[...] = toward_x + on_speed * u_before
        push_low_y[...] = toward_y + on_speed * v_before

        def update(at, source, source_at):
            wet_here = wet_pad[at]
            slow_here = factor[at]
            along_x, along_y = push_x[at], push_y[at]
            low_x, low_y = push_low_x[at], push_low_y[at]
            zero = jnp.zeros_like(wet_here)
            total_u = total_v = low_u = low_v = zero

            def fetch(level):
                if level == levels:
                    return zero, zero
                retain = jnp.where(wet_here > level + 1, 1.0, jnp.where(wet_here > level, slow_here, 0.0))
                return retain * source[1 + level, source_at], retain * source[1 + levels + level, source_at]

            p_up = q_up = zero
            p, q = fetch(0)
            for level in range(levels):
                p_down, q_down = fetch(level + 1)
                inside = wet_here > level + 1
                bottom = wet_here == level + 1
                active = wet_here > level
                own = 1.0 if level == 0 else 0.9
                weight = jnp.where(inside, own - 0.1, own)
                u = weight * p + 0.1 * (p_up + p_down - q) + jnp.where(inside, along_x, low_x)
                v = weight * q + 0.1 * (q_up + q_down + p) + jnp.where(inside, along_y, low_y)
                u = jnp.where(active, u, 0.0)
                v = jnp.where(active, v, 0.0)
                if last:
                    start[1 + level, source_at] = u
                    start[1 + levels + level, source_at] = v
                else:
                    work[1 + level, at] = u
                    work[1 + levels + level, at] = v
                    total_u += u
                    total_v += v
                    low_u = jnp.where(bottom, u, low_u)
                    low_v = jnp.where(bottom, v, low_v)
                p_up, q_up, p, q = p, q, p_down, q_down
            if not last:
                sum_u[at] = total_u
                sum_v[at] = total_v
                bot_u[at] = low_u
                bot_v[at] = low_v

        if first:
            over_blocks(rows, True, update, adjoint, above, below)
        else:
            def inner(index, carry):
                begin = pl.multiple_of(index * BLOCK, BLOCK)
                if last:
                    at = pl.ds(pl.multiple_of(begin + HALO, BLOCK), BLOCK)
                    load = at
                else:
                    at = load = pl.ds(begin, BLOCK)

                class Source:
                    def __getitem__(self, key):
                        return work[key[0], load]

                update(at, Source(), pl.ds(begin, BLOCK))
                return carry

            lax.fori_loop(0, rows // BLOCK if last else (rows + 2 * HALO) // BLOCK, inner, 0)
    start[0] = eta[HALO : HALO + rows]
    gradient[...] = grad_pad[HALO : HALO + rows]


def body(start_states, end_adjoints, misfits, water_depth, drag_coef, sea_mask, bottom_level):
    initial = start_states[0]
    adjoint = end_adjoints[0]
    misfit = misfits[0]
    fields, rows, width = initial.shape
    wet = (sea_mask * bottom_level).astype(jnp.float32)
    statics = jnp.stack([water_depth, wet, drag_coef])
    pad = pltpu.VMEM((rows + 2 * HALO, width), jnp.float32)
    work = pltpu.VMEM((fields, rows + 2 * HALO, width), jnp.float32)
    params = pltpu.CompilerParams(vmem_limit_bytes=32 << 20)
    cells = fields * rows * width

    above = shifted(jnp.concatenate([initial[:, -HALO:], statics[:, -HALO:]]), "tile", 1)
    below = shifted(jnp.concatenate([initial[:, :HALO], statics[:, :HALO]]), "tile", -1)
    final, saved = pl.pallas_call(
        forward_kernel,
        out_shape=(
            jax.ShapeDtypeStruct((fields, rows, width), jnp.float32),
            jax.ShapeDtypeStruct((SAVED, rows, width), jnp.float32),
        ),
        scratch_shapes=[work] + [pad] * 11,
        compiler_params=params,
        cost_estimate=pl.CostEstimate(flops=100 * cells, bytes_accessed=10 * cells, transcendentals=0),
        name="forward",
    )(initial, above, below, water_depth, wet, drag_coef)
    next_state = passed_along(final, "slab", 1)

    low = jnp.concatenate([adjoint[:, -HALO:], misfit[:, -HALO:], saved[:, -HALO:]])
    high = jnp.concatenate([adjoint[:, :HALO], misfit[:, :HALO], saved[:, :HALO]])
    start, gradient = pl.pallas_call(
        adjoint_kernel,
        out_shape=(
            jax.ShapeDtypeStruct((fields, rows, width), jnp.float32),
            jax.ShapeDtypeStruct((rows, width), jnp.float32),
        ),
        scratch_shapes=[work, pltpu.VMEM((SAVED, rows + 2 * HALO, width), jnp.float32)] + [pad] * 14,
        compiler_params=params,
        cost_estimate=pl.CostEstimate(flops=100 * cells, bytes_accessed=10 * cells, transcendentals=0),
        name="adjoint",
    )(adjoint, misfit, saved, shifted(low, "tile", 1), shifted(high, "tile", -1),
      water_depth, wet, drag_coef, above[fields:], below[fields:])
    next_adjoint = passed_along(start, "slab", -1)
    drag_total = lax.psum(gradient, "slab")
    return (next_state[None], next_adjoint[None], drag_total)


def solution(mesh):
    return jax.shard_map(
        body,
        mesh=mesh,
        in_specs=(
            P(("groups", "slab"), None, "tile", None),
            P(("groups", "slab"), None, "tile", None),
            P(("groups", "slab"), None, "tile", None),
            P(("groups", "tile"), None),
            P(("groups", "tile"), None),
            P(("groups", "tile"), None),
            P(("groups", "tile"), None),
        ),
        out_specs=(
            P(("groups", "slab"), None, "tile", None),
            P(("groups", "slab"), None, "tile", None),
            P(("groups", "tile"), None),
        ),
        check_vma=False,
    )
```

time: 153 us -> 112 us (0.73)
  the two profiles are of different devices: /device:TPU:1 before, /device:TPU:2 now
where the time goes in v1:
time: 112 us; the launch traced here: 111 us
  blocking collectives  71.6 us (64%)
  starting transfers between devices  15.2 us (14%)
  Pallas kernels  8.41 us (8%)
  local copies, waits for them, and re-layouts  7.8 us (7%)
  waiting for transfers between devices  5.83 us (5%)
  other arithmetic  1.59 us (1%)
    psum x1, blocking collectives, body(): drag_total = lax.psum(gradient, 'slab')  71.6 us
    ppermute x4, starting transfers between devices, shifted(): return lax.ppermute(block, axis, route)  9.9 us
    ppermute x4, waiting for transfers between devices, shifted(): return lax.ppermute(block, axis, route)  5.83 us
    unnamed x12, local copies, waits for them, and re-layouts  5.54 us
    ppermute x2, starting transfers between devices, passed_along(): return lax.ppermute(block, axis, route)  5.28 us
    pallas_call x1, Pallas kernels, body(): pl.pallas_call(adjoint_kernel, out_shape=(jax.ShapeDtypeStruct((fields, r...  4.52 us
    pallas_call x1, Pallas kernels, body(): pl.pallas_call(forward_kernel, out_shape=(jax.ShapeDtypeStruct((fields, r...  3.89 us
  transfers between devices with their start and end apart: 6, of which 3 were waited for; matrix products, arithmetic and copies ran while one was open for 1% of the time, Pallas kernels for 4%

profile of v1, /device:TPU:2, one launch (start us, length us, event | category | flops | bytes accessed | tf_op | source)
XLA Modules:
  0.0 111.2 jit_solution(5713053944327261253)
XLA Ops:
  0.6 0.0 copy-start
  0.6 0.0 copy-start.3
  0.7 0.0 copy-start.2
  0.7 0.0 copy-start.4
  0.7 1.2 %fusion.3 = (f32[49,8,128]{2,1,0:T(8,128)S(1)}, f32[49,8,128]{2,1,0:T(8,128)S(1)}) fusion(f32[49,64,128]{2,1,0:T(8,128)} %bitcast.8), kind=kLoop, calls=%fused_computation.10 | loop fusion | bytes 802816 | tf_op jit(solution)/shard_map/slice | solution.py:326
  1.9 0.8 multiply_convert_fusion.wet
  2.7 0.8 fusion
  3.4 1.9 %collective-permute-start.1 = (f32[52,8,128]{2,1,0:T(8,128)S(1)}, f32[52,8,128]{2,1,0:T(8,128)S(1)}, u32[]{:S(2)}, u32[]{:S(2)}) collective-permute-start(f32[52,8,128]{2,1,0:T(8,128)S(1)} %get-tuple-element.19), channel_id=1, source_target_pairs={{4,0},{8,4},{12,8},{5,1},{9,5},{13,9},{6,2},{10,6},{14,10},{7,3},{... | collective-permute-start | bytes 638984 | tf_op jit(solution)/shard_map/ppermute | solution.py:17
  5.3 2.4 %collective-permute-start = (f32[52,8,128]{2,1,0:T(8,128)S(1)}, f32[52,8,128]{2,1,0:T(8,128)S(1)}, u32[]{:S(2)}, u32[]{:S(2)}) collective-permute-start(f32[52,8,128]{2,1,0:T(8,128)S(1)} %get-tuple-element.20), channel_id=1, source_target_pairs={{0,4},{4,8},{8,12},{1,5},{5,9},{9,13},{2,6},{6,10},{10,14},{3,7},{... | collective-permute-start | bytes 638984 | tf_op jit(solution)/shard_map/ppermute | solution.py:17
  7.8 1.1 fusion.2
  8.8 0.0 copy-done.4
  8.9 0.0 copy-start.1
  8.9 0.0 collective-permute-done.1.below
  8.9 3.6 %collective-permute-done.above = f32[52,8,128]{2,1,0:T(8,128)S(1)} collective-permute-done((f32[52,8,128]{2,1,0:T(8,128)S(1)}, f32[52,8,128]{2,1,0:T(8,128)S(1)}, u32[]{:S(2)}, u32[]{:S(2)}) %collective-permute-start) | collective-permute-done | bytes 213024 | tf_op jit(solution)/shard_map/ppermute | solution.py:17
  12.5 0.0 copy-done
  12.5 0.0 copy-done.3
  12.5 0.0 copy-done.2
  12.5 3.9 %forward.1 = (f32[49,64,128]{2,1,0:T(8,128)S(1)}, f32[10,64,128]{2,1,0:T(8,128)S(1)}) custom-call(f32[49,64,128]{2,1,0:T(8,128)S(1)} %bitcast.9, f32[52,8,128]{2,1,0:T(8,128)S(1)} %collective-permute-done.above, f32[52,8,128]{2,1,0:T(8,128)S(1)} %collective-permute-done.1.below, f32[64,128]{1,0:T(8,128)S(1)} %copy-done.3, ...), custom_call_target="tpu_custom_call" | custom-call | flops 40140800 | bytes 4014080 | tf_op jit(solution)/shard_map/forward/pallas_call | solution.py:327
  16.5 1.9 %collective-permute-start.3 = (f32[63,8,128]{2,1,0:T(8,128)S(1)}, f32[63,8,128]{2,1,0:T(8,128)S(1)}, u32[]{:S(2)}, u32[]{:S(2)}) collective-permute-start(f32[63,8,128]{2,1,0:T(8,128)S(1)} %pad_maximum_fusion), channel_id=1, source_target_pairs={{0,4},{4,8},{8,12},{1,5},{5,9},{9,13},{2,6},{6,10},{10,14},{3,7},{... | collective-permute-start | bytes 774152 | tf_op jit(solution)/shard_map/ppermute | solution.py:17
  18.4 3.6 %collective-permute-start.4 = (f32[63,8,128]{2,1,0:T(8,128)S(1)}, f32[63,8,128]{2,1,0:T(8,128)S(1)}, u32[]{:S(2)}, u32[]{:S(2)}) collective-permute-start(f32[63,8,128]{2,1,0:T(8,128)S(1)} %pad_maximum_fusion.1), channel_id=1, source_target_pairs={{4,0},{8,4},{12,8},{5,1},{9,5},{13,9},{6,2},{10,6},{14,10},{7,3},{... | collective-permute-start | bytes 774152 | tf_op jit(solution)/shard_map/ppermute | solution.py:17
  22.1 1.6 %collective-permute-start.2 = (f32[49,64,128]{2,1,0:T(8,128)S(1)}, f32[49,64,128]{2,1,0:T(8,128)}, u32[]{:S(2)}, u32[]{:S(2)}) collective-permute-start(f32[49,64,128]{2,1,0:T(8,128)S(1)} %get-tuple-element.7), channel_id=1, source_target_pairs={{3,0},{0,1},{1,2},{2,3},{7,4},{4,5},{5,6},{6,7},{11,8},{8,9},{9,10... | collective-permute-start | bytes 4816904 | tf_op jit(solution)/shard_map/ppermute | solution.py:23
  23.7 0.4 collective-permute-done.3.above
  24.1 1.8 %collective-permute-done.4.below = f32[63,8,128]{2,1,0:T(8,128)S(1)} collective-permute-done((f32[63,8,128]{2,1,0:T(8,128)S(1)}, f32[63,8,128]{2,1,0:T(8,128)S(1)}, u32[]{:S(2)}, u32[]{:S(2)}) %collective-permute-start.4) | collective-permute-done | bytes 258080 | tf_op jit(solution)/shard_map/ppermute | solution.py:17
  25.9 0.0 copy-done.1
  25.9 4.5 %adjoint.1 = (f32[49,64,128]{2,1,0:T(8,128)S(1)}, f32[64,128]{1,0:T(8,128)S(1)}) custom-call(f32[49,64,128]{2,1,0:T(8,128)S(1)} %bitcast.11, f32[4,64,128]{2,1,0:T(8,128)S(1)} %bitcast.16, f32[10,64,128]{2,1,0:T(8,128)S(1)} %get-tuple-element.8.saved, f32[63,8,128]{2,1,0:T(8,128)S(1)} %collective-permute-done.3.above, ...), custom_call_target="tpu_custom_call" | custom-call | flops 40140800 | bytes 4014080 | tf_op jit(solution)/shard_map/adjoint/pallas_call | solution.py:342
  30.4 3.7 %collective-permute-start.5 = (f32[49,64,128]{2,1,0:T(8,128)S(1)}, f32[49,64,128]{2,1,0:T(8,128)}, u32[]{:S(2)}, u32[]{:S(2)}) collective-permute-start(f32[49,64,128]{2,1,0:T(8,128)S(1)} %get-tuple-element.9), channel_id=1, source_target_pairs={{1,0},{2,1},{3,2},{0,3},{5,4},{6,5},{7,6},{4,7},{9,8},{10,9},{11,1... | collective-permute-start | bytes 4816904 | tf_op jit(solution)/shard_map/ppermute | solution.py:23
  34.1 71.6 %psum.7 = f32[64,128]{1,0:T(8,128)} all-reduce(f32[64,128]{1,0:T(8,128)S(1)} %get-tuple-element.10), channel_id=1, replica_groups=mesh['groups'=2,'tile'=4,'slab'=4] {'slab'}, use_global_device_ids=true, to_apply=%region_0.0 | all-reduce | flops 8192 | bytes 65536 | tf_op jit(solution)/shard_map/psum | solution.py:355
  105.6 0.0 collective-permute-done.2
  105.7 0.0 collective-permute-done.5
  105.7 2.8 %copy.12 = f32[1,49,64,128]{3,2,1,0:T(8,128)} copy(f32[1,49,64,128]{3,2,1,0:T(8,128)} %bitcast.4) | data formatting | bytes 3211264
  108.4 2.8 %copy.13 = f32[1,49,64,128]{3,2,1,0:T(8,128)} copy(f32[1,49,64,128]{3,2,1,0:T(8,128)} %bitcast.7) | data formatting | bytes 3211264
  (6 shorter events, 0.1 us)
Async XLA Ops:
  0.6 11.9 %copy-start = (f32[1,49,64,128]{3,2,1,0:T(8,128)S(1)}, f32[1,49,64,128]{3,2,1,0:T(8,128)}, u32[]{:S(2)}) copy-start(f32[1,49,64,128]{3,2,1,0:T(8,128)} %param.7) | copy-start | bytes 4816900
  0.6 11.9 %copy-start.3 = (f32[64,128]{1,0:T(8,128)S(1)}, f32[64,128]{1,0:T(8,128)}, u32[]{:S(2)}) copy-start(f32[64,128]{1,0:T(8,128)} %depth.3) | copy-start | bytes 98308
  0.7 11.9 %copy-start.2 = (f32[64,128]{1,0:T(8,128)S(1)}, f32[64,128]{1,0:T(8,128)}, u32[]{:S(2)}) copy-start(f32[64,128]{1,0:T(8,128)} %drag.3) | copy-start | bytes 98308
  0.7 8.2 %copy-start.4 = (f32[1,4,64,128]{3,2,1,0:T(8,128)S(1)}, f32[1,4,64,128]{3,2,1,0:T(8,128)}, u32[]{:S(2)}) copy-start(f32[1,4,64,128]{3,2,1,0:T(8,128)} %param.9) | copy-start | bytes 393220
  3.4 5.4 %collective-permute-start.1 = (f32[52,8,128]{2,1,0:T(8,128)S(1)}, f32[52,8,128]{2,1,0:T(8,128)S(1)}, u32[]{:S(2)}, u32[]{:S(2)}) collective-permute-start(f32[52,8,128]{2,1,0:T(8,128)S(1)} %get-tuple-element.19), channel_id=1, source_target_pairs={{4,0},{8,4},{12,8},{5,1},{9,5},{13,9},{6,2},{10,6},{14,10},{7,3},{... | collective-permute-start | bytes 638984 | tf_op jit(solution)/shard_map/ppermute | solution.py:17
  5.3 7.2 %collective-permute-start = (f32[52,8,128]{2,1,0:T(8,128)S(1)}, f32[52,8,128]{2,1,0:T(8,128)S(1)}, u32[]{:S(2)}, u32[]{:S(2)}) collective-permute-start(f32[52,8,128]{2,1,0:T(8,128)S(1)} %get-tuple-element.20), channel_id=1, source_target_pairs={{0,4},{4,8},{8,12},{1,5},{5,9},{9,13},{2,6},{6,10},{10,14},{3,7},{... | collective-permute-start | bytes 638984 | tf_op jit(solution)/shard_map/ppermute | solution.py:17
  8.9 17.0 %copy-start.1 = (f32[1,49,64,128]{3,2,1,0:T(8,128)S(1)}, f32[1,49,64,128]{3,2,1,0:T(8,128)}, u32[]{:S(2)}) copy-start(f32[1,49,64,128]{3,2,1,0:T(8,128)} %param.8) | copy-start | bytes 4816900
  16.5 7.6 %collective-permute-start.3 = (f32[63,8,128]{2,1,0:T(8,128)S(1)}, f32[63,8,128]{2,1,0:T(8,128)S(1)}, u32[]{:S(2)}, u32[]{:S(2)}) collective-permute-start(f32[63,8,128]{2,1,0:T(8,128)S(1)} %pad_maximum_fusion), channel_id=1, source_target_pairs={{0,4},{4,8},{8,12},{1,5},{5,9},{9,13},{2,6},{6,10},{10,14},{3,7},{... | collective-permute-start | bytes 774152 | tf_op jit(solution)/shard_map/ppermute | solution.py:17
  18.4 7.5 %collective-permute-start.4 = (f32[63,8,128]{2,1,0:T(8,128)S(1)}, f32[63,8,128]{2,1,0:T(8,128)S(1)}, u32[]{:S(2)}, u32[]{:S(2)}) collective-permute-start(f32[63,8,128]{2,1,0:T(8,128)S(1)} %pad_maximum_fusion.1), channel_id=1, source_target_pairs={{4,0},{8,4},{12,8},{5,1},{9,5},{13,9},{6,2},{10,6},{14,10},{7,3},{... | collective-permute-start | bytes 774152 | tf_op jit(solution)/shard_map/ppermute | solution.py:17
  22.1 83.6 %collective-permute-start.2 = (f32[49,64,128]{2,1,0:T(8,128)S(1)}, f32[49,64,128]{2,1,0:T(8,128)}, u32[]{:S(2)}, u32[]{:S(2)}) collective-permute-start(f32[49,64,128]{2,1,0:T(8,128)S(1)} %get-tuple-element.7), channel_id=1, source_target_pairs={{3,0},{0,1},{1,2},{2,3},{7,4},{4,5},{5,6},{6,7},{11,8},{8,9},{9,10... | collective-permute-start | bytes 4816904 | tf_op jit(solution)/shard_map/ppermute | solution.py:23
  30.4 75.2 %collective-permute-start.5 = (f32[49,64,128]{2,1,0:T(8,128)S(1)}, f32[49,64,128]{2,1,0:T(8,128)}, u32[]{:S(2)}, u32[]{:S(2)}) collective-permute-start(f32[49,64,128]{2,1,0:T(8,128)S(1)} %get-tuple-element.9), channel_id=1, source_target_pairs={{1,0},{2,1},{3,2},{0,3},{5,4},{6,5},{7,6},{4,7},{9,8},{10,9},{11,1... | collective-permute-start | bytes 4816904 | tf_op jit(solution)/shard_map/ppermute | solution.py:23

commit v2 on v1

--- a/solution.py
+++ b/solution.py
@@ -8,7 +8,10 @@
 STEPS = 4
 BLOCK = 8
 HALO = 2 * STEPS
+REACH = 2 * HALO
 SAVED = 2 + 2 * STEPS
+POOL = 4 * BLOCK
+SLOTS = 29
 
 
 def shifted(block, axis, distance):
@@ -35,25 +38,244 @@
     return after - before
 
 
-def over_blocks(rows, with_halo, visit, own, above, below):
-    if with_halo:
-        visit(pl.ds(0, BLOCK), above, pl.ds(0, BLOCK))
-
-    def inner(index, carry):
-        start = pl.multiple_of(index * BLOCK, BLOCK)
-        visit(pl.ds(pl.multiple_of(start + HALO, BLOCK), BLOCK), own, pl.ds(start, BLOCK))
+def looped(count, visit):
+    def one(index, carry):
+        visit(pl.multiple_of(index * BLOCK, BLOCK))
         return carry
 
-    lax.fori_loop(0, rows // BLOCK, inner, 0)
-    if with_halo:
-        visit(pl.ds(HALO + rows, BLOCK), below, pl.ds(0, BLOCK))
+    lax.fori_loop(0, count // BLOCK, one, 0)
+
+
+def over_blocks(rows, halo, visit, own, above, below):
+    block = lambda start: pl.ds(start if isinstance(start, int) else pl.multiple_of(start, BLOCK), BLOCK)
+    looped(halo, lambda start: visit(block(start), above, block(start)))
+    looped(rows, lambda start: visit(block(start + halo), own, block(start)))
+    looped(halo, lambda start: visit(block(start + halo + rows), below, block(start)))
 
 
 def fill_padded(target, own, above, below):
-    rows = own.shape[0]
-    target[0:HALO] = above
-    target[HALO : HALO + rows] = own
-    target[HALO + rows : rows + 2 * HALO] = below
+    rows, halo = own.shape[0], above.shape[0]
+    target[0:halo] = above
+    target[halo : halo + rows] = own
+    target[halo + rows : rows + 2 * halo] = below
+
+
+class Shifted:
+    def __init__(self, ref, at):
+        self.ref, self.at = ref, at
+
+    def __getitem__(self, key):
+        return self.ref[key[0], self.at]
+
+
+class AdjointEdge:
+    def __init__(self, ref, fields):
+        self.ref, self.fields = ref, fields
+
+    def __getitem__(self, key):
+        plane, rows = edge_place(self.fields, key[0])
+        return self.ref[plane, rows]
+
+
+def edge_planes(fields):
+    return fields + 3 + (fields + STEPS + 1) // 2
+
+
+def edge_place(fields, item):
+    first = (fields + STEPS + 1) // 2
+    half = 0 if item < first else HALO
+    return fields + 3 + item - (first if half else 0), pl.ds(half, HALO)
+
+
+def lanes_of(values):
+    return lax.broadcasted_iota(jnp.int32, values.shape, values.ndim - 1)
+
+
+def take_lanes(values, index):
+    return jnp.take_along_axis(values, index, axis=1, mode="promise_in_bounds")
+
+
+def plan_kernel(mask, bottom, wet, order, place, deepest):
+    rows, width = mask.shape
+    half = width // 2
+    depth = mask[...] * bottom[...]
+    wet[...] = depth.astype(jnp.float32)
+    lane = lanes_of(depth)
+    even = (lax.broadcasted_iota(jnp.int32, depth.shape, 0) // BLOCK) % 2 == 0
+    key = (depth * width + lane).astype(jnp.float32)
+    rank = jnp.zeros_like(depth)
+    for shift in range(1, width):
+        rank = rank + jnp.where(pltpu.roll(key, shift, 1) > key, 1, 0)
+    ahead = jnp.where(rank < half, rank, width + half - 1 - rank)
+    behind = jnp.where(rank < half, rank + half, width - 1 - rank)
+    there = jnp.where(even, ahead, behind)
+    place[...] = there
+    moved = jnp.zeros_like(depth)
+    for shift in range(1, width):
+        moved = jnp.where(pltpu.roll(there, shift, 1) == lane, shift, moved)
+    origin = (lane - moved) & (width - 1)
+    order[...] = origin
+    most = jnp.zeros((BLOCK, width), jnp.float32)
+    for pool in range(rows // POOL):
+        ats = [slice(pool * POOL + block * BLOCK, pool * POOL + (block + 1) * BLOCK) for block in range(4)]
+        deep, shallow, swap = pair_up([take_lanes(wet[at], origin[at]) for at in ats])
+        most = jnp.maximum(most, deep[0] + jnp.where(swap, shallow[1], shallow[0]))
+        most = jnp.maximum(most, deep[1] + jnp.where(swap, shallow[0], shallow[1]))
+    deepest[0, 0] = jnp.max(most).astype(jnp.int32)
+
+
+def deep_and_shallow(blocks):
+    first = lanes_of(blocks[0]) < blocks[0].shape[1] // 2
+    deep = [jnp.where(first, blocks[0], blocks[1]), jnp.where(first, blocks[2], blocks[3])]
+    shallow = [jnp.where(first, blocks[1], blocks[0]), jnp.where(first, blocks[3], blocks[2])]
+    return deep, shallow
+
+
+def pair_up(depths):
+    deep, shallow = deep_and_shallow(depths)
+    swap = (deep[0] - deep[1]) * (shallow[0] - shallow[1]) > 0.0
+    return deep, shallow, swap
+
+
+def pool_rows(pool):
+    start = pl.multiple_of(pool * POOL, POOL)
+    return [pl.ds(pl.multiple_of(start + block * BLOCK, BLOCK), BLOCK) for block in range(4)]
+
+
+def pool_slots(pool):
+    start = pl.multiple_of(pool * (POOL // 2), POOL // 2)
+    return [pl.ds(pl.multiple_of(start + block * BLOCK, BLOCK), BLOCK) for block in range(2)]
+
+
+def pack(state, wet, order, packed):
+    fields, rows, _ = state.shape
+    levels = (fields - 1) // 2
+
+    def one_pool(pool, carry):
+        ats = pool_rows(pool)
+        slots = pool_slots(pool)
+        orders = [order[at, :] for at in ats]
+        deep_wet, _, swap = pair_up([take_lanes(wet[at, :], by) for at, by in zip(ats, orders)])
+        for base, target in ((1, 0), (1 + levels, SLOTS)):
+
+            def sorted_level(level):
+                parts = [take_lanes(state[base + level, at, :], by) for at, by in zip(ats, orders)]
+                deep, shallow = deep_and_shallow(parts)
+                return deep, (jnp.where(swap, shallow[1], shallow[0]), jnp.where(swap, shallow[0], shallow[1]))
+
+            for near in range((SLOTS + 1) // 2):
+                far = SLOTS - 1 - near
+                both = far < levels
+                deep, shallow = sorted_level(near)
+                far_deep, far_shallow = sorted_level(far) if both and far > near else (deep, shallow)
+                for half in range(2):
+                    value = deep[half]
+                    if both:
+                        value = jnp.where(deep_wet[half] > near, value, far_shallow[half])
+                    packed[target + near, slots[half], :] = value
+                    if far > near:
+                        value = shallow[half]
+                        if both:
+                            value = jnp.where(deep_wet[half] > far, far_deep[half], value)
+                        packed[target + far, slots[half], :] = value
+        for half in range(2):
+            for block in range(2):
+                packed[2 * SLOTS + half, slots[block], :] = state[0, ats[2 * half + block], :]
+        return carry
+
+    lax.fori_loop(0, rows // POOL, one_pool, 0)
+
+
+def pack_kernel(state, wet, order, packed):
+    pack(state, wet, order, packed)
+
+
+def unpack_kernel(deepest, packed, wet, order, place, whole, state):
+    levels = (state.shape[0] - 1) // 2
+    pool = pl.program_id(0)
+
+    @pl.when(deepest[0, 0] > SLOTS)
+    def _():
+        pltpu.sync_copy(whole.at[:, pl.ds(pl.multiple_of(pool * POOL, POOL), POOL), :], state)
+
+    @pl.when(deepest[0, 0] <= SLOTS)
+    def _():
+        ats = pool_rows(0)
+        slots = pool_slots(0)
+        wets = [wet[at, :] for at in ats]
+        places = [place[at, :] for at in ats]
+        _, _, swap = pair_up([take_lanes(depth, order[at, :]) for depth, at in zip(wets, ats)])
+        first = lanes_of(swap) < swap.shape[1] // 2
+        for base, source in ((1, 0), (1 + levels, SLOTS)):
+
+            def write_level(level, deep, ends):
+                shallow = jnp.where(swap, ends[1], ends[0]), jnp.where(swap, ends[0], ends[1])
+                for block in range(4):
+                    pair = deep[block // 2], shallow[block // 2]
+                    if block % 2:
+                        pair = pair[::-1]
+                    value = take_lanes(jnp.where(first, *pair), places[block])
+                    state[base + level, ats[block], :] = jnp.where(wets[block] > level, value, 0.0)
+
+            for near in range((SLOTS + 1) // 2):
+                far = SLOTS - 1 - near
+                head = [packed[source + near, slot, :] for slot in slots]
+                tail = [packed[source + far, slot, :] for slot in slots]
+                write_level(near, head, tail)
+                if near < far < levels:
+                    write_level(far, tail, head)
+        for half in range(2):
+            for block in range(2):
+                state[0, ats[2 * half + block], :] = packed[2 * SLOTS + half, slots[block], :]
+
+
+def edge_kernel(state, adjoint, misfit, depth, drag, mask, bottom, upward, downward, sems):
+    fields, rows, _ = state.shape
+    first = (fields + STEPS + 1) // 2
+    copies = []
+    for side, target in enumerate((upward, downward)):
+        wide = pl.ds(side * (rows - REACH), REACH)
+        narrow = pl.ds(side * (rows - HALO), HALO)
+        joint = fields + 3
+        copies += [
+            pltpu.make_async_copy(state.at[:, wide, :], target.at[pl.ds(0, fields)], sems.at[3 * side]),
+            pltpu.make_async_copy(
+                adjoint.at[pl.ds(0, first), narrow, :],
+                target.at[pl.ds(joint, first), pl.ds(0, HALO), :],
+                sems.at[3 * side + 1],
+            ),
+            pltpu.make_async_copy(
+                adjoint.at[pl.ds(first, fields - first), narrow, :],
+                target.at[pl.ds(joint, fields - first), pl.ds(HALO, HALO), :],
+                sems.at[3 * side + 2],
+            ),
+        ]
+    for copy in copies:
+        copy.start()
+    for side, target in enumerate((upward, downward)):
+        wide = pl.ds(side * (rows - REACH), REACH)
+        narrow = pl.ds(side * (rows - HALO), HALO)
+        target[fields] = depth[wide]
+        target[fields + 1] = (mask[wide] * bottom[wide]).astype(jnp.float32)
+        target[fields + 2] = drag[wide]
+        for step in range(STEPS):
+            plane, at = edge_place(fields, fields + step)
+            target[plane, at] = misfit[step, narrow]
+    for copy in copies:
+        copy.wait()
+
+
+def unpack_adjoint_kernel(deepest, packed, wet, order, place, whole, *rest):
+    *gradients, state, total = rest
+    unpack_kernel(deepest, packed, wet, order, place, whole, state)
+    summed = gradients[0][...]
+    for gradient in gradients[1:]:
+        summed = summed + gradient[...]
+    total[...] = summed
+
+
+def nothing_kernel(result):
+    pass
 
 
 def drag_terms(u_bottom, v_bottom, thickness, drag, sea):
@@ -62,7 +284,7 @@
     return speed, denominator, thickness / denominator
 
 
-def forward_kernel(state, above, below, depth, wet, drag, final, saved,
+def forward_kernel(state, above, below, depth, wet, drag, order, final, saved, packed,
                    work, wet_pad, thick, drag_pad, eta, sum_u, sum_v, bot_u, bot_v, slope_x, slope_y, factor):
     fields, rows, _ = state.shape
     levels = (fields - 1) // 2
@@ -89,9 +311,9 @@
         bot_u[at] = low_u
         bot_v[at] = low_v
 
-    over_blocks(rows, True, sums, state, above, below)
-    saved[0] = bot_u[HALO : HALO + rows]
-    saved[1] = bot_v[HALO : HALO + rows]
+    over_blocks(rows, REACH, sums, state, above, below)
+    saved[0] = bot_u[HALO : REACH + HALO + rows]
+    saved[1] = bot_v[HALO : REACH + HALO + rows]
 
     for step in range(STEPS):
         first, last = step == 0, step == STEPS - 1
@@ -104,7 +326,7 @@
         slope_y[...] = 0.2 * column_diff(surface)
         factor[...] = drag_terms(bot_u[...], bot_v[...], thick[...], drag_pad[...], sea)[2]
 
-        def update(at, source, source_at):
+        def update(at, source, source_at, into_final=False):
             wet_here = wet_pad[at]
             slow = factor[at]
             grad_x = slope_x[at]
@@ -137,7 +359,7 @@
                 low_v = jnp.where(bottom, vt, low_v)
                 u_new = ut * retain
                 v_new = vt * retain
-                if last:
+                if into_final:
                     final[1 + level, source_at] = u_new
                     final[1 + levels + level, source_at] = v_new
                 else:
@@ -152,45 +374,45 @@
             bot_v[at] = low_v
 
         if first:
-            over_blocks(rows, True, update, state, above, below)
+            over_blocks(rows, REACH, update, state, above, below)
+        elif last:
+
+            def into_final(start):
+                at = pl.ds(pl.multiple_of(start + REACH, BLOCK), BLOCK)
+                update(at, Shifted(work, at), pl.ds(start, BLOCK), True)
+
+            looped(rows, into_final)
+            for start in range(HALO, REACH, BLOCK):
+                for at in (pl.ds(start, BLOCK), pl.ds(start + HALO + rows, BLOCK)):
+                    update(at, work, at)
         else:
-            def inner(index, carry):
-                start = pl.multiple_of(index * BLOCK, BLOCK)
-                if last:
-                    at = pl.ds(pl.multiple_of(start + HALO, BLOCK), BLOCK)
-                    load = at
-                else:
-                    at = load = pl.ds(start, BLOCK)
-
-                class Source:
-                    def __getitem__(self, key):
-                        return work[key[0], load]
-
-                update(at, Source(), pl.ds(start, BLOCK))
-                return carry
-
-            lax.fori_loop(0, rows // BLOCK if last else (rows + 2 * HALO) // BLOCK, inner, 0)
-        saved[2 + 2 * step] = bot_u[HALO : HALO + rows]
-        saved[3 + 2 * step] = bot_v[HALO : HALO + rows]
+
+            def in_place(start):
+                at = pl.ds(start, BLOCK)
+                update(at, work, at)
+
+            looped(rows + 2 * REACH, in_place)
+        saved[2 + 2 * step] = bot_u[HALO : REACH + HALO + rows]
+        saved[3 + 2 * step] = bot_v[HALO : REACH + HALO + rows]
         bot_u[...] = factor[...] * bot_u[...]
         bot_v[...] = factor[...] * bot_v[...]
-    final[0] = eta[HALO : HALO + rows]
-
-
-def adjoint_kernel(adjoint, misfit, saved, above, below, depth, wet, drag, stat_above, stat_below,
+    final[0] = eta[REACH : REACH + rows]
+    pack(final, wet, order, packed)
+
+
+def adjoint_kernel(adjoint, misfit, kept, above, below, depth, wet, drag,
                    start, gradient,
-                   work, kept, wet_pad, thick, drag_pad, eta, sum_u, sum_v, bot_u, bot_v,
+                   work, wet_pad, thick, drag_pad, eta, sum_u, sum_v, bot_u, bot_v,
                    push_x, push_y, push_low_x, push_low_y, factor, grad_pad):
     fields, rows, _ = adjoint.shape
     levels = (fields - 1) // 2
-    miss_at, saved_at = fields, fields + STEPS
-    fill_padded(wet_pad, wet[...], stat_above[1], stat_below[1])
-    fill_padded(drag_pad, drag[...], stat_above[2], stat_below[2])
-    fill_padded(thick, depth[...], stat_above[0], stat_below[0])
+    fill_padded(wet_pad, wet[...], above[fields + 1, HALO:], below[fields + 1, :HALO])
+    fill_padded(drag_pad, drag[...], above[fields + 2, HALO:], below[fields + 2, :HALO])
+    fill_padded(thick, depth[...], above[fields, HALO:], below[fields, :HALO])
+    above = AdjointEdge(above, fields)
+    below = AdjointEdge(below, fields)
     thick[...] = thick[...] / jnp.maximum(wet_pad[...], 1.0)
-    for item in range(SAVED):
-        fill_padded(kept.at[item], saved[item], above[saved_at + item], below[saved_at + item])
-    fill_padded(eta, adjoint[0], above[0], below[0])
+    fill_padded(eta, adjoint[0], above[0, :], below[0, :])
     grad_pad[...] = jnp.zeros_like(grad_pad)
     sea = jnp.minimum(wet_pad[...], 1.0)
 
@@ -216,12 +438,12 @@
         bot_u[at] = low_u
         bot_v[at] = low_v
 
-    over_blocks(rows, True, sums, adjoint, above, below)
+    over_blocks(rows, HALO, sums, adjoint, above, below)
 
     for step in reversed(range(STEPS)):
         first, last = step == STEPS - 1, step == 0
         sea = jnp.minimum(wet_pad[...], 1.0)
-        fill_padded(push_x, misfit[step], above[miss_at + step], below[miss_at + step])
+        fill_padded(push_x, misfit[step], above[fields + step, :], below[fields + step, :])
         u_before, v_before = before[step]
         speed, denominator, slow = drag_terms(u_before, v_before, thick[...], drag_pad[...], sea)
         factor[...] = slow
@@ -243,7 +465,9 @@
         push_low_x[...] = toward_x + on_speed * u_before
         push_low_y[...] = toward_y + on_speed * v_before
 
-        def update(at, source, source_at):
+        def update(at, source, source_at, offset=0):
+            if offset:
+                at = source.at
             wet_here = wet_pad[at]
             slow_here = factor[at]
             along_x, along_y = push_x[at], push_y[at]
@@ -288,24 +512,21 @@
                 bot_v[at] = low_v
 
         if first:
-            over_blocks(rows, True, update, adjoint, above, below)
+            over_blocks(rows, HALO, update, adjoint, above, below)
+        elif last:
+
+            def into_start(begin):
+                update(pl.ds(begin, BLOCK), Shifted(work, pl.ds(pl.multiple_of(begin + HALO, BLOCK), BLOCK)),
+                       pl.ds(begin, BLOCK), HALO)
+
+            looped(rows, into_start)
         else:
-            def inner(index, carry):
-                begin = pl.multiple_of(index * BLOCK, BLOCK)
-                if last:
-                    at = pl.ds(pl.multiple_of(begin + HALO, BLOCK), BLOCK)
-                    load = at
-                else:
-                    at = load = pl.ds(begin, BLOCK)
-
-                class Source:
-                    def __getitem__(self, key):
-                        return work[key[0], load]
-
-                update(at, Source(), pl.ds(begin, BLOCK))
-                return carry
-
-            lax.fori_loop(0, rows // BLOCK if last else (rows + 2 * HALO) // BLOCK, inner, 0)
+
+            def in_place(begin):
+                at = pl.ds(begin, BLOCK)
+                update(at, work, at)
+
+            looped(rows + 2 * HALO, in_place)
     start[0] = eta[HALO : HALO + rows]
     gradient[...] = grad_pad[HALO : HALO + rows]
 
@@ -315,44 +536,89 @@
     adjoint = end_adjoints[0]
     misfit = misfits[0]
     fields, rows, width = initial.shape
-    wet = (sea_mask * bottom_level).astype(jnp.float32)
-    statics = jnp.stack([water_depth, wet, drag_coef])
-    pad = pltpu.VMEM((rows + 2 * HALO, width), jnp.float32)
-    work = pltpu.VMEM((fields, rows + 2 * HALO, width), jnp.float32)
+    floats = lambda *shape: jax.ShapeDtypeStruct(shape, jnp.float32)
+    whole_numbers = lambda *shape: jax.ShapeDtypeStruct(shape, jnp.int32)
+    pad = lambda halo: pltpu.VMEM((rows + 2 * halo, width), jnp.float32)
+    work = lambda halo: pltpu.VMEM((fields, rows + 2 * halo, width), jnp.float32)
     params = pltpu.CompilerParams(vmem_limit_bytes=32 << 20)
     cells = fields * rows * width
-
-    above = shifted(jnp.concatenate([initial[:, -HALO:], statics[:, -HALO:]]), "tile", 1)
-    below = shifted(jnp.concatenate([initial[:, :HALO], statics[:, :HALO]]), "tile", -1)
-    final, saved = pl.pallas_call(
+    cost = pl.CostEstimate(flops=100 * cells, bytes_accessed=10 * cells, transcendentals=0)
+    state_shape = floats(fields, rows, width)
+    packed_shape = floats(2 * SLOTS + 2, rows // 2, width)
+    edge_shape = floats(edge_planes(fields), REACH, width)
+    in_vmem = pl.BlockSpec(memory_space=pltpu.VMEM)
+    in_smem = pl.BlockSpec(memory_space=pltpu.SMEM)
+    anywhere = pl.BlockSpec(memory_space=pl.ANY)
+
+    upward, downward = pl.pallas_call(
+        edge_kernel,
+        in_specs=[anywhere] * 2 + [in_vmem] * 5,
+        out_shape=(edge_shape, edge_shape),
+        scratch_shapes=[pltpu.SemaphoreType.DMA((6,))],
+        cost_estimate=cost,
+        name="edges",
+    )(initial, adjoint, misfit, water_depth, drag_coef, sea_mask, bottom_level)
+    above = shifted(downward, "tile", 1)
+    below = shifted(upward, "tile", -1)
+
+    wet, order, place, deepest = pl.pallas_call(
+        plan_kernel,
+        out_specs=(in_vmem,) * 3 + (in_smem,),
+        out_shape=(floats(rows, width), whole_numbers(rows, width), whole_numbers(rows, width), whole_numbers(1, 1)),
+        cost_estimate=cost,
+        name="plan",
+    )(sea_mask, bottom_level)
+
+    final, saved, final_packed = pl.pallas_call(
         forward_kernel,
-        out_shape=(
-            jax.ShapeDtypeStruct((fields, rows, width), jnp.float32),
-            jax.ShapeDtypeStruct((SAVED, rows, width), jnp.float32),
-        ),
-        scratch_shapes=[work] + [pad] * 11,
+        out_shape=(state_shape, floats(SAVED, rows + 2 * HALO, width), packed_shape),
+        scratch_shapes=[work(REACH)] + [pad(REACH)] * 11,
         compiler_params=params,
-        cost_estimate=pl.CostEstimate(flops=100 * cells, bytes_accessed=10 * cells, transcendentals=0),
+        cost_estimate=cost,
         name="forward",
-    )(initial, above, below, water_depth, wet, drag_coef)
-    next_state = passed_along(final, "slab", 1)
-
-    low = jnp.concatenate([adjoint[:, -HALO:], misfit[:, -HALO:], saved[:, -HALO:]])
-    high = jnp.concatenate([adjoint[:, :HALO], misfit[:, :HALO], saved[:, :HALO]])
+    )(initial, above, below, water_depth, wet, drag_coef, order)
+    came_state = passed_along(final_packed, "slab", 1)
+
     start, gradient = pl.pallas_call(
         adjoint_kernel,
-        out_shape=(
-            jax.ShapeDtypeStruct((fields, rows, width), jnp.float32),
-            jax.ShapeDtypeStruct((rows, width), jnp.float32),
-        ),
-        scratch_shapes=[work, pltpu.VMEM((SAVED, rows + 2 * HALO, width), jnp.float32)] + [pad] * 14,
+        out_shape=(state_shape, floats(rows, width)),
+        scratch_shapes=[work(HALO)] + [pad(HALO)] * 14,
         compiler_params=params,
-        cost_estimate=pl.CostEstimate(flops=100 * cells, bytes_accessed=10 * cells, transcendentals=0),
+        cost_estimate=cost,
         name="adjoint",
-    )(adjoint, misfit, saved, shifted(low, "tile", 1), shifted(high, "tile", -1),
-      water_depth, wet, drag_coef, above[fields:], below[fields:])
-    next_adjoint = passed_along(start, "slab", -1)
-    drag_total = lax.psum(gradient, "slab")
+    )(adjoint, misfit, saved, above, below, water_depth, wet, drag_coef)
+    slabs = lax.axis_size("slab")
+    if slabs > 4:
+        gradients = [lax.psum(gradient, "slab")]
+    else:
+        gradients = [gradient] + [passed_along(gradient, "slab", distance) for distance in range(1, slabs)]
+    start_packed = pl.pallas_call(
+        pack_kernel, out_shape=packed_shape, compiler_params=params, cost_estimate=cost, name="pack"
+    )(start, wet, order)
+    came_adjoint = passed_along(start_packed, "slab", -1)
+
+    def received(kernel, packed, sent, distance, *extra):
+        fallback = lax.cond(
+            deepest[0, 0] > SLOTS,
+            lambda sent: passed_along(sent, "slab", distance),
+            lambda sent: pl.pallas_call(nothing_kernel, out_specs=anywhere, out_shape=state_shape, name="nothing")(),
+            sent,
+        )
+        pool = pl.BlockSpec((POOL, width), lambda i: (i, 0))
+        return pl.pallas_call(
+            kernel,
+            grid=(rows // POOL,),
+            in_specs=[in_smem, pl.BlockSpec((2 * SLOTS + 2, POOL // 2, width), lambda i: (0, i, 0)),
+                      pool, pool, pool, anywhere] + [pool] * len(extra),
+            out_specs=[pl.BlockSpec((fields, POOL, width), lambda i: (0, i, 0))] + [pool] * bool(extra),
+            out_shape=[state_shape] + [floats(rows, width)] * bool(extra),
+            compiler_params=params,
+            cost_estimate=cost,
+            name="unpack",
+        )(deepest, packed, wet, order, place, fallback, *extra)
+
+    (next_state,) = received(unpack_kernel, came_state, final, 1)
+    next_adjoint, drag_total = received(unpack_adjoint_kernel, came_adjoint, start, -1, *gradients)
     return (next_state[None], next_adjoint[None], drag_total)
 
 

time: 112 us -> 76.8 us (0.69)
  the two profiles are of different devices: /device:TPU:2 before, /device:TPU:1 now
where the time goes in v2:
time: 76.8 us; the launch traced here: 75.6 us
  waiting for transfers between devices  29.7 us (39%)
  Pallas kernels  29.6 us (39%)
  starting transfers between devices  13.3 us (17%)
  local copies, waits for them, and re-layouts  1.54 us (2%)
  between operations  1.44 us (2%)
    ppermute x5, waiting for transfers between devices, passed_along(): return lax.ppermute(block, axis, route)  23.3 us
    pallas_call x1, Pallas kernels, body(): pl.pallas_call(forward_kernel, out_shape=(state_shape, floats(SAVED, rows...  8.18 us
    ppermute x5, starting transfers between devices, passed_along(): return lax.ppermute(block, axis, route)  6.72 us
    ppermute x2, starting transfers between devices, shifted(): return lax.ppermute(block, axis, route)  6.56 us
    ppermute x2, waiting for transfers between devices, shifted(): return lax.ppermute(block, axis, route)  6.42 us
    pallas_call x2, Pallas kernels, received(): pl.pallas_call(kernel, grid=(rows // POOL,), in_specs=[in_smem, pl.BlockS...  6.22 us
    pallas_call x1, Pallas kernels, body(): pl.pallas_call(adjoint_kernel, out_shape=(state_shape, floats(rows, width...  5.79 us
    pallas_call x1, Pallas kernels, body(): pl.pallas_call(plan_kernel, out_specs=(in_vmem,) * 3 + (in_smem,), out_sh...  3.78 us
  transfers between devices with their start and end apart: 7, of which 5 were waited for; matrix products, arithmetic and copies ran while one was open for 0% of the time, Pallas kernels for 20%

profile of v2, /device:TPU:1, one launch (start us, length us, event | category | flops | bytes accessed | tf_op | source)
XLA Modules:
  0.0 75.6 jit_solution(5697785539035504526)
XLA Ops:
  0.6 0.0 copy-start.1
  0.6 0.0 copy-start.7
  0.7 0.0 copy-start.8
  0.7 0.0 copy-start.6
  0.7 3.4 %edges.1 = (f32[79,16,128]{2,1,0:T(8,128)}, f32[79,16,128]{2,1,0:T(8,128)}) custom-call(f32[49,64,128]{2,1,0:T(8,128)} %bitcast.8, f32[49,64,128]{2,1,0:T(8,128)} %bitcast.6, f32[4,64,128]{2,1,0:T(8,128)} %bitcast.10, f32[64,128]{1,0:T(8,128)} %depth.5, f32[64,128]{1,0:T(8,128)} %drag.5, s32[64,128]{1,0:T(8,128)} %mask.3, s32[64,128]{1,0:T(8,128)} %bottom.3), custom_call_target="tpu_custom_call" | custom-call | flops 40140800 | bytes 4014080 | tf_op jit(solution)/shard_map/edges/pallas_call | solution.py:553
  4.1 0.0 copy-start
  4.1 4.6 %collective-permute-start.2 = (f32[79,16,128]{2,1,0:T(8,128)}, f32[79,16,128]{2,1,0:T(8,128)}, u32[]{:S(2)}, u32[]{:S(2)}) collective-permute-start(f32[79,16,128]{2,1,0:T(8,128)} %get-tuple-element.25), channel_id=1, source_target_pairs={{0,4},{4,8},{8,12},{1,5},{5,9},{9,13},{2,6},{6,10},{10,14},{3,7},{... | collective-permute-start | bytes 1941512 | tf_op jit(solution)/shard_map/ppermute | solution.py:20
  8.8 1.9 %collective-permute-start.3 = (f32[79,16,128]{2,1,0:T(8,128)}, f32[79,16,128]{2,1,0:T(8,128)}, u32[]{:S(2)}, u32[]{:S(2)}) collective-permute-start(f32[79,16,128]{2,1,0:T(8,128)} %get-tuple-element.26), channel_id=1, source_target_pairs={{4,0},{8,4},{12,8},{5,1},{9,5},{13,9},{6,2},{10,6},{14,10},{7,3},{... | collective-permute-start | bytes 1941512 | tf_op jit(solution)/shard_map/ppermute | solution.py:20
  10.7 3.8 %plan.1 = (f32[64,128]{1,0:T(8,128)}, s32[64,128]{1,0:T(8,128)}, s32[64,128]{1,0:T(8,128)}, s32[1,1]{1,0:T(1,128)}) custom-call(s32[64,128]{1,0:T(8,128)} %mask.3, s32[64,128]{1,0:T(8,128)} %bottom.3), custom_call_target="tpu_custom_call" | custom-call | flops 40140800 | bytes 4014080 | tf_op jit(solution)/shard_map/plan/pallas_call | solution.py:564
  14.5 2.0 %collective-permute-done.2.above = f32[79,16,128]{2,1,0:T(8,128)} collective-permute-done((f32[79,16,128]{2,1,0:T(8,128)}, f32[79,16,128]{2,1,0:T(8,128)}, u32[]{:S(2)}, u32[]{:S(2)}) %collective-permute-start.2) | collective-permute-done | bytes 647200 | tf_op jit(solution)/shard_map/ppermute | solution.py:20
  16.5 4.4 %collective-permute-done.3.below = f32[79,16,128]{2,1,0:T(8,128)} collective-permute-done((f32[79,16,128]{2,1,0:T(8,128)}, f32[79,16,128]{2,1,0:T(8,128)}, u32[]{:S(2)}, u32[]{:S(2)}) %collective-permute-start.3) | collective-permute-done | bytes 647200 | tf_op jit(solution)/shard_map/ppermute | solution.py:20
  20.9 0.0 copy-done.1
  20.9 0.0 copy-done.7
  20.9 0.0 copy-done.8
  20.9 0.0 copy-start.2
  20.9 0.7 copy-done.2
  21.7 0.8 copy-done.4
  22.4 8.2 %forward.1 = (f32[49,64,128]{2,1,0:T(8,128)}, f32[10,80,128]{2,1,0:T(8,128)S(1)}, f32[60,32,128]{2,1,0:T(8,128)}) custom-call(f32[49,64,128]{2,1,0:T(8,128)S(1)} %bitcast.9, f32[79,16,128]{2,1,0:T(8,128)} %collective-permute-done.2.above, f32[79,16,128]{2,1,0:T(8,128)} %collective-permute-done.3.below, f32[64,128]{1,0:T(8,128)S(1)} %copy-done.7, ...), custom_call_target="tpu_custom_call" | custom-call | flops 40140800 | bytes 4014080 | tf_op jit(solution)/shard_map/forward/pallas_call | solution.py:572
  30.6 1.3 %collective-permute-start.4 = (f32[60,32,128]{2,1,0:T(8,128)}, f32[60,32,128]{2,1,0:T(8,128)S(1)}, u32[]{:S(2)}, u32[]{:S(2)}) collective-permute-start(f32[60,32,128]{2,1,0:T(8,128)} %get-tuple-element.29), channel_id=1, source_target_pairs={{3,0},{0,1},{1,2},{2,3},{7,4},{4,5},{5,6},{6,7},{11,8},{8,9},{9,10... | collective-permute-start | bytes 2949128 | tf_op jit(solution)/shard_map/ppermute | solution.py:26
  31.9 5.8 %adjoint.1 = (f32[49,64,128]{2,1,0:T(8,128)S(1)}, f32[64,128]{1,0:T(8,128)S(1)}) custom-call(f32[49,64,128]{2,1,0:T(8,128)S(1)} %bitcast.7, f32[4,64,128]{2,1,0:T(8,128)S(1)} %bitcast.11, f32[10,80,128]{2,1,0:T(8,128)S(1)} %get-tuple-element.32.kept, f32[79,16,128]{2,1,0:T(8,128)} %collective-permute-done.2.above, ...), custom_call_target="tpu_custom_call" | custom-call | flops 40140800 | bytes 4014080 | tf_op jit(solution)/shard_map/adjoint/pallas_call | solution.py:582
  37.7 2.2 %pack.1 = f32[60,32,128]{2,1,0:T(8,128)} custom-call(f32[49,64,128]{2,1,0:T(8,128)S(1)} %get-tuple-element.33.state, f32[64,128]{1,0:T(8,128)S(1)} %copy-done.2, s32[64,128]{1,0:T(8,128)S(1)} %copy-done.4), custom_call_target="tpu_custom_call" | custom-call | flops 40140800 | bytes 4014080 | tf_op jit(solution)/shard_map/pack/pallas_call | solution.py:595
  39.9 2.0 %collective-permute-start.5 = (f32[60,32,128]{2,1,0:T(8,128)}, f32[60,32,128]{2,1,0:T(8,128)S(1)}, u32[]{:S(2)}, u32[]{:S(2)}) collective-permute-start(f32[60,32,128]{2,1,0:T(8,128)} %pack.1), channel_id=1, source_target_pairs={{1,0},{2,1},{3,2},{0,3},{5,4},{6,5},{7,6},{4,7},{9,8},{10,9},{11,1... | collective-permute-start | bytes 2949128 | tf_op jit(solution)/shard_map/ppermute | solution.py:26
  42.6 0.1 collective-permute-start.6
  42.7 1.7 %collective-permute-start.7 = (f32[64,128]{1,0:T(8,128)S(1)}, f32[64,128]{1,0:T(8,128)S(1)}, u32[]{:S(2)}, u32[]{:S(2)}) collective-permute-start(f32[64,128]{1,0:T(8,128)S(1)} %get-tuple-element.34.rest_0_), channel_id=1, source_target_pairs={{2,0},{3,1},{0,2},{1,3},{6,4},{7,5},{4,6},{5,7},{10,8},{11,9},{8,1... | collective-permute-start | bytes 98312 | tf_op jit(solution)/shard_map/ppermute | solution.py:26
  44.5 1.6 %collective-permute-start.8 = (f32[64,128]{1,0:T(8,128)S(1)}, f32[64,128]{1,0:T(8,128)S(1)}, u32[]{:S(2)}, u32[]{:S(2)}) collective-permute-start(f32[64,128]{1,0:T(8,128)S(1)} %get-tuple-element.34.rest_0_), channel_id=1, source_target_pairs={{1,0},{2,1},{3,2},{0,3},{5,4},{6,5},{7,6},{4,7},{9,8},{10,9},{11,1... | collective-permute-start | bytes 98312 | tf_op jit(solution)/shard_map/ppermute | solution.py:26
  46.1 10.2 %collective-permute-done.4.packed = f32[60,32,128]{2,1,0:T(8,128)S(1)} collective-permute-done((f32[60,32,128]{2,1,0:T(8,128)}, f32[60,32,128]{2,1,0:T(8,128)S(1)}, u32[]{:S(2)}, u32[]{:S(2)}) %collective-permute-start.4) | collective-permute-done | bytes 983072 | tf_op jit(solution)/shard_map/ppermute | solution.py:26
  56.3 3.1 %unpack.2 = f32[49,64,128]{2,1,0:T(8,128)} custom-call(s32[1,1]{1,0:T(1,128)} %get-tuple-element.24.deepest, f32[60,32,128]{2,1,0:T(8,128)S(1)} %collective-permute-done.4.packed, f32[64,128]{1,0:T(8,128)S(1)} %copy-done.3, s32[64,128]{1,0:T(8,128)S(1)} %copy-done.5, s32[64,128]{1,0:T(8,128)S(1)} %copy-done.9, f32[49,64,128]{2,1,0:T(8,128)} %get-tuple-element.37.whole), custom_call_target="tpu_custom_call" | custom-call | flops 40140800 | bytes 4014080 | tf_op jit(solution)/shard_map/unpack/pallas_call | solution.py:608
  59.4 12.2 %collective-permute-done.6.rest_1_ = f32[64,128]{1,0:T(8,128)S(1)} collective-permute-done((f32[64,128]{1,0:T(8,128)S(1)}, f32[64,128]{1,0:T(8,128)S(1)}, u32[]{:S(2)}, u32[]{:S(2)}) %collective-permute-start.6) | collective-permute-done | bytes 32800 | tf_op jit(solution)/shard_map/ppermute | solution.py:26
  71.6 0.9 %collective-permute-done.7.rest_2_ = f32[64,128]{1,0:T(8,128)S(1)} collective-permute-done((f32[64,128]{1,0:T(8,128)S(1)}, f32[64,128]{1,0:T(8,128)S(1)}, u32[]{:S(2)}, u32[]{:S(2)}) %collective-permute-start.7) | collective-permute-done | bytes 32800 | tf_op jit(solution)/shard_map/ppermute | solution.py:26
  72.4 0.0 collective-permute-done.8.rest_3_
  72.4 0.0 collective-permute-done.5.packed
  72.4 3.1 %unpack.3 = (f32[49,64,128]{2,1,0:T(8,128)}, f32[64,128]{1,0:T(8,128)}) custom-call(s32[1,1]{1,0:T(1,128)} %get-tuple-element.24.deepest, f32[60,32,128]{2,1,0:T(8,128)S(1)} %collective-permute-done.5.packed, f32[64,128]{1,0:T(8,128)S(1)} %copy-done.3, s32[64,128]{1,0:T(8,128)S(1)} %copy-done.5, s32[64,128]{1,0:T(8,128)S(1)} %copy-done.9, ...), custom_call_target="tpu_custom_call" | custom-call | flops 40140800 | bytes 4014080 | tf_op jit(solution)/shard_map/unpack/pallas_call | solution.py:608
  (13 shorter events, 0.0 us)
Async XLA Ops:
  0.6 20.3 %copy-start.1 = (f32[1,49,64,128]{3,2,1,0:T(8,128)S(1)}, f32[1,49,64,128]{3,2,1,0:T(8,128)}, u32[]{:S(2)}) copy-start(f32[1,49,64,128]{3,2,1,0:T(8,128)} %param.11) | copy-start | bytes 4816900
  0.6 20.3 %copy-start.7 = (f32[64,128]{1,0:T(8,128)S(1)}, f32[64,128]{1,0:T(8,128)}, u32[]{:S(2)}) copy-start(f32[64,128]{1,0:T(8,128)} %depth.5) | copy-start | bytes 98308
  0.7 20.3 %copy-start.8 = (f32[64,128]{1,0:T(8,128)S(1)}, f32[64,128]{1,0:T(8,128)}, u32[]{:S(2)}) copy-start(f32[64,128]{1,0:T(8,128)} %drag.5) | copy-start | bytes 98308
  0.7 31.3 %copy-start.6 = (f32[1,4,64,128]{3,2,1,0:T(8,128)S(1)}, f32[1,4,64,128]{3,2,1,0:T(8,128)}, u32[]{:S(2)}) copy-start(f32[1,4,64,128]{3,2,1,0:T(8,128)} %param.13) | copy-start | bytes 393220
  4.1 27.8 %copy-start = (f32[1,49,64,128]{3,2,1,0:T(8,128)S(1)}, f32[1,49,64,128]{3,2,1,0:T(8,128)}, u32[]{:S(2)}) copy-start(f32[1,49,64,128]{3,2,1,0:T(8,128)} %param.12) | copy-start | bytes 4816900
  4.1 12.4 %collective-permute-start.2 = (f32[79,16,128]{2,1,0:T(8,128)}, f32[79,16,128]{2,1,0:T(8,128)}, u32[]{:S(2)}, u32[]{:S(2)}) collective-permute-start(f32[79,16,128]{2,1,0:T(8,128)} %get-tuple-element.25), channel_id=1, source_target_pairs={{0,4},{4,8},{8,12},{1,5},{5,9},{9,13},{2,6},{6,10},{10,14},{3,7},{... | collective-permute-start | bytes 1941512 | tf_op jit(solution)/shard_map/ppermute | solution.py:20
  8.8 12.1 %collective-permute-start.3 = (f32[79,16,128]{2,1,0:T(8,128)}, f32[79,16,128]{2,1,0:T(8,128)}, u32[]{:S(2)}, u32[]{:S(2)}) collective-permute-start(f32[79,16,128]{2,1,0:T(8,128)} %get-tuple-element.26), channel_id=1, source_target_pairs={{4,0},{8,4},{12,8},{5,1},{9,5},{13,9},{6,2},{10,6},{14,10},{7,3},{... | collective-permute-start | bytes 1941512 | tf_op jit(solution)/shard_map/ppermute | solution.py:20
  20.9 0.8 %copy-start.2 = (f32[64,128]{1,0:T(8,128)S(1)}, f32[64,128]{1,0:T(8,128)}, u32[]{:S(2)}) copy-start(f32[64,128]{1,0:T(8,128)} %get-tuple-element.27.wet) | copy-start | bytes 98308
  21.7 0.8 %copy-start.4 = (s32[64,128]{1,0:T(8,128)S(1)}, s32[64,128]{1,0:T(8,128)}, u32[]{:S(2)}) copy-start(s32[64,128]{1,0:T(8,128)} %get-tuple-element.28.order) | copy-start | bytes 98308
  30.6 25.7 %collective-permute-start.4 = (f32[60,32,128]{2,1,0:T(8,128)}, f32[60,32,128]{2,1,0:T(8,128)S(1)}, u32[]{:S(2)}, u32[]{:S(2)}) collective-permute-start(f32[60,32,128]{2,1,0:T(8,128)} %get-tuple-element.29), channel_id=1, source_target_pairs={{3,0},{0,1},{1,2},{2,3},{7,4},{4,5},{5,6},{6,7},{11,8},{8,9},{9,10... | collective-permute-start | bytes 2949128 | tf_op jit(solution)/shard_map/ppermute | solution.py:26
  39.9 32.6 %collective-permute-start.5 = (f32[60,32,128]{2,1,0:T(8,128)}, f32[60,32,128]{2,1,0:T(8,128)S(1)}, u32[]{:S(2)}, u32[]{:S(2)}) collective-permute-start(f32[60,32,128]{2,1,0:T(8,128)} %pack.1), channel_id=1, source_target_pairs={{1,0},{2,1},{3,2},{0,3},{5,4},{6,5},{7,6},{4,7},{9,8},{10,9},{11,1... | collective-permute-start | bytes 2949128 | tf_op jit(solution)/shard_map/ppermute | solution.py:26
  42.6 29.0 %collective-permute-start.6 = (f32[64,128]{1,0:T(8,128)S(1)}, f32[64,128]{1,0:T(8,128)S(1)}, u32[]{:S(2)}, u32[]{:S(2)}) collective-permute-start(f32[64,128]{1,0:T(8,128)S(1)} %get-tuple-element.34.rest_0_), channel_id=1, source_target_pairs={{3,0},{0,1},{1,2},{2,3},{7,4},{4,5},{5,6},{6,7},{11,8},{8,9},{9,10... | collective-permute-start | bytes 98312 | tf_op jit(solution)/shard_map/ppermute | solution.py:26
  42.7 29.8 %collective-permute-start.7 = (f32[64,128]{1,0:T(8,128)S(1)}, f32[64,128]{1,0:T(8,128)S(1)}, u32[]{:S(2)}, u32[]{:S(2)}) collective-permute-start(f32[64,128]{1,0:T(8,128)S(1)} %get-tuple-element.34.rest_0_), channel_id=1, source_target_pairs={{2,0},{3,1},{0,2},{1,3},{6,4},{7,5},{4,6},{5,7},{10,8},{11,9},{8,1... | collective-permute-start | bytes 98312 | tf_op jit(solution)/shard_map/ppermute | solution.py:26
  44.4 11.9 %copy-start.3 = (f32[64,128]{1,0:T(8,128)S(1)}, f32[64,128]{1,0:T(8,128)}, u32[]{:S(2)}) copy-start(f32[64,128]{1,0:T(8,128)} %get-tuple-element.27.wet) | copy-start | bytes 98308
  44.4 11.9 %copy-start.5 = (s32[64,128]{1,0:T(8,128)S(1)}, s32[64,128]{1,0:T(8,128)}, u32[]{:S(2)}) copy-start(s32[64,128]{1,0:T(8,128)} %get-tuple-element.28.order) | copy-start | bytes 98308
  44.4 11.9 %copy-start.9 = (s32[64,128]{1,0:T(8,128)S(1)}, s32[64,128]{1,0:T(8,128)}, u32[]{:S(2)}) copy-start(s32[64,128]{1,0:T(8,128)} %get-tuple-element.30.place) | copy-start | bytes 98308
  44.5 28.0 %collective-permute-start.8 = (f32[64,128]{1,0:T(8,128)S(1)}, f32[64,128]{1,0:T(8,128)S(1)}, u32[]{:S(2)}, u32[]{:S(2)}) collective-permute-start(f32[64,128]{1,0:T(8,128)S(1)} %get-tuple-element.34.rest_0_), channel_id=1, source_target_pairs={{1,0},{2,1},{3,2},{0,3},{5,4},{6,5},{7,6},{4,7},{9,8},{10,9},{11,1... | collective-permute-start | bytes 98312 | tf_op jit(solution)/shard_map/ppermute | solution.py:26

commit v3 on v2

--- a/solution.py
+++ b/solution.py
@@ -148,8 +148,7 @@
 
 
 def pack(state, wet, order, packed):
-    fields, rows, _ = state.shape
-    levels = (fields - 1) // 2
+    levels = (state.shape[0] - 1) // 2
 
     def one_pool(pool, carry):
         ats = pool_rows(pool)
@@ -178,20 +177,45 @@
                         if both:
                             value = jnp.where(deep_wet[half] > far, far_deep[half], value)
                         packed[target + far, slots[half], :] = value
-        for half in range(2):
-            for block in range(2):
-                packed[2 * SLOTS + half, slots[block], :] = state[0, ats[2 * half + block], :]
         return carry
 
-    lax.fori_loop(0, rows // POOL, one_pool, 0)
+    lax.fori_loop(0, packed.shape[1] // (POOL // 2), one_pool, 0)
 
 
 def pack_kernel(state, wet, order, packed):
     pack(state, wet, order, packed)
 
 
-def unpack_kernel(deepest, packed, wet, order, place, whole, state):
+def unpack_pool(packed, wet, order, place, state, pool):
     levels = (state.shape[0] - 1) // 2
+    ats = pool_rows(pool)
+    slots = pool_slots(pool)
+    wets = [wet[at, :] for at in ats]
+    places = [place[at, :] for at in ats]
+    _, _, swap = pair_up([take_lanes(depth, order[at, :]) for depth, at in zip(wets, ats)])
+    first = lanes_of(swap) < swap.shape[1] // 2
+    for base, source in ((1, 0), (1 + levels, SLOTS)):
+
+        def write_level(level, deep, ends):
+            shallow = jnp.where(swap, ends[1], ends[0]), jnp.where(swap, ends[0], ends[1])
+            for block in range(4):
+                pair = deep[block // 2], shallow[block // 2]
+                if block % 2:
+                    pair = pair[::-1]
+                value = take_lanes(jnp.where(first, *pair), places[block])
+                state[base + level, ats[block], :] = jnp.where(wets[block] > level, value, 0.0)
+
+        for near in range((SLOTS + 1) // 2):
+            far = SLOTS - 1 - near
+            head = [packed[source + near, slot, :] for slot in slots]
+            tail = [packed[source + far, slot, :] for slot in slots]
+            write_level(near, head, tail)
+            if near < far < levels:
+                write_level(far, tail, head)
+
+
+def unpack_kernel(deepest, packed, wet, order, place, whole, *rest):
+    *gradients, state, total = rest
     pool = pl.program_id(0)
 
     @pl.when(deepest[0, 0] > SLOTS)
@@ -200,80 +224,107 @@
 
     @pl.when(deepest[0, 0] <= SLOTS)
     def _():
-        ats = pool_rows(0)
-        slots = pool_slots(0)
-        wets = [wet[at, :] for at in ats]
-        places = [place[at, :] for at in ats]
-        _, _, swap = pair_up([take_lanes(depth, order[at, :]) for depth, at in zip(wets, ats)])
-        first = lanes_of(swap) < swap.shape[1] // 2
-        for base, source in ((1, 0), (1 + levels, SLOTS)):
-
-            def write_level(level, deep, ends):
-                shallow = jnp.where(swap, ends[1], ends[0]), jnp.where(swap, ends[0], ends[1])
-                for block in range(4):
-                    pair = deep[block // 2], shallow[block // 2]
-                    if block % 2:
-                        pair = pair[::-1]
-                    value = take_lanes(jnp.where(first, *pair), places[block])
-                    state[base + level, ats[block], :] = jnp.where(wets[block] > level, value, 0.0)
-
-            for near in range((SLOTS + 1) // 2):
-                far = SLOTS - 1 - near
-                head = [packed[source + near, slot, :] for slot in slots]
-                tail = [packed[source + far, slot, :] for slot in slots]
-                write_level(near, head, tail)
-                if near < far < levels:
-                    write_level(far, tail, head)
+        unpack_pool(packed, wet, order, place, state, 0)
         for half in range(2):
-            for block in range(2):
-                state[0, ats[2 * half + block], :] = packed[2 * SLOTS + half, slots[block], :]
-
-
-def edge_kernel(state, adjoint, misfit, depth, drag, mask, bottom, upward, downward, sems):
-    fields, rows, _ = state.shape
-    first = (fields + STEPS + 1) // 2
-    copies = []
-    for side, target in enumerate((upward, downward)):
-        wide = pl.ds(side * (rows - REACH), REACH)
-        narrow = pl.ds(side * (rows - HALO), HALO)
-        joint = fields + 3
-        copies += [
-            pltpu.make_async_copy(state.at[:, wide, :], target.at[pl.ds(0, fields)], sems.at[3 * side]),
-            pltpu.make_async_copy(
-                adjoint.at[pl.ds(0, first), narrow, :],
-                target.at[pl.ds(joint, first), pl.ds(0, HALO), :],
-                sems.at[3 * side + 1],
-            ),
-            pltpu.make_async_copy(
-                adjoint.at[pl.ds(first, fields - first), narrow, :],
-                target.at[pl.ds(joint, fields - first), pl.ds(HALO, HALO), :],
-                sems.at[3 * side + 2],
-            ),
-        ]
-    for copy in copies:
-        copy.start()
-    for side, target in enumerate((upward, downward)):
-        wide = pl.ds(side * (rows - REACH), REACH)
-        narrow = pl.ds(side * (rows - HALO), HALO)
-        target[fields] = depth[wide]
-        target[fields + 1] = (mask[wide] * bottom[wide]).astype(jnp.float32)
-        target[fields + 2] = drag[wide]
-        for step in range(STEPS):
-            plane, at = edge_place(fields, fields + step)
-            target[plane, at] = misfit[step, narrow]
-    for copy in copies:
-        copy.wait()
-
-
-def unpack_adjoint_kernel(deepest, packed, wet, order, place, whole, *rest):
-    *gradients, state, total = rest
-    unpack_kernel(deepest, packed, wet, order, place, whole, state)
+            state[0, half * (POOL // 2) : (half + 1) * (POOL // 2)] = packed[2 * SLOTS + half]
+
     summed = gradients[0][...]
     for gradient in gradients[1:]:
         summed = summed + gradient[...]
     total[...] = summed
 
 
+def replay_kernel(deepest, packed, wet, order, place, depth, drag, surfaces, whole, final,
+                  thick, bot_u, bot_v, slope_x, slope_y, factor):
+    fields, rows, width = final.shape
+    levels = (fields - 1) // 2
+
+    @pl.when(deepest[0, 0] > SLOTS)
+    def _():
+        pltpu.sync_copy(whole, final)
+        for level in range(levels):
+            active = wet[...] > level
+            for at in (1 + level, 1 + levels + level):
+                final[at] = jnp.where(active, final[at], 0.0)
+
+    @pl.when(deepest[0, 0] <= SLOTS)
+    def _():
+        def one_pool(pool, carry):
+            unpack_pool(packed, wet, order, place, final, pool)
+            return carry
+
+        lax.fori_loop(0, rows // POOL, one_pool, 0)
+
+    def lowest(start):
+        at = pl.ds(start, BLOCK)
+        wet_here = wet[at, :]
+        low_u = low_v = jnp.zeros_like(wet_here)
+        for level in range(levels):
+            bottom = wet_here == level + 1
+            low_u = jnp.where(bottom, final[1 + level, at, :], low_u)
+            low_v = jnp.where(bottom, final[1 + levels + level, at, :], low_v)
+        bot_u[at, :] = low_u
+        bot_v[at, :] = low_v
+
+    looped(rows, lowest)
+    sea = jnp.minimum(wet[...], 1.0)
+    thick[...] = depth[...] / jnp.maximum(wet[...], 1.0)
+    for step in range(STEPS):
+        surface = surfaces[step]
+        slope_x[...] = 0.2 * row_diff(surface)[HALO : HALO + rows]
+        slope_y[...] = 0.2 * column_diff(surface[HALO : HALO + rows])
+        factor[...] = drag_terms(bot_u[...], bot_v[...], thick[...], drag[...], sea)[2]
+
+        def update(start):
+            at = pl.ds(start, BLOCK)
+
+            def store(level, u, v):
+                final[1 + level, at, :] = u
+                final[1 + levels + level, at, :] = v
+
+            slow = factor[at, :]
+            fetch = lambda level: (final[1 + level, at, :], final[1 + levels + level, at, :])
+            _, low, _ = column_step(levels, wet[at, :], slow, slope_x[at, :], slope_y[at, :], fetch, store)
+            bot_u[at, :] = slow * low[0]
+            bot_v[at, :] = slow * low[1]
+
+        looped(rows, update)
+    final[0] = surfaces[STEPS - 1, HALO : HALO + rows]
+
+
+def edge_kernel(state, adjoint, misfit, depth, drag, mask, bottom, upward, downward, sea_rows, level_rows, sems):
+    fields, rows, _ = state.shape
+    first = (fields + STEPS + 1) // 2
+    joint = fields + 3
+    copies = []
+
+    def bring(source, target):
+        copies.append(pltpu.make_async_copy(source, target, sems.at[len(copies)]))
+
+    for side, target in enumerate((upward, downward)):
+        wide = pl.ds(side * (rows - REACH), REACH)
+        narrow = pl.ds(side * (rows - HALO), HALO)
+        bring(state.at[:, wide, :], target.at[pl.ds(0, fields)])
+        bring(adjoint.at[pl.ds(0, first), narrow, :], target.at[pl.ds(joint, first), pl.ds(0, HALO), :])
+        bring(
+            adjoint.at[pl.ds(first, fields - first), narrow, :],
+            target.at[pl.ds(joint, fields - first), pl.ds(HALO, HALO), :],
+        )
+        for step in range(STEPS):
+            plane, at = edge_place(fields, fields + step)
+            bring(misfit.at[step, narrow, :], target.at[plane, at, :])
+        bring(depth.at[wide, :], target.at[fields])
+        bring(drag.at[wide, :], target.at[fields + 2])
+        bring(mask.at[wide, :], sea_rows.at[side])
+        bring(bottom.at[wide, :], level_rows.at[side])
+    for copy in copies:
+        copy.start()
+    for copy in copies:
+        copy.wait()
+    for side, target in enumerate((upward, downward)):
+        target[fields + 1] = (sea_rows[side] * level_rows[side]).astype(jnp.float32)
+
+
 def nothing_kernel(result):
     pass
 
@@ -284,10 +335,37 @@
     return speed, denominator, thickness / denominator
 
 
-def forward_kernel(state, above, below, depth, wet, drag, order, final, saved, packed,
-                   work, wet_pad, thick, drag_pad, eta, sum_u, sum_v, bot_u, bot_v, slope_x, slope_y, factor):
+def column_step(levels, wet_here, slow, grad_x, grad_y, fetch, store):
+    zero = jnp.zeros_like(wet_here)
+    total = low = second = (zero, zero)
+    u_up = v_up = zero
+    u, v = fetch(0)
+    for level in range(levels):
+        u_down, v_down = fetch(level + 1) if level + 1 < levels else (zero, zero)
+        inside = wet_here > level + 1
+        bottom = wet_here == level + 1
+        above_bottom = wet_here == level + 2
+        own = 1.0 if level == 0 else 0.9
+        weight = jnp.where(inside, own - 0.1, own)
+        retain = jnp.where(inside, 1.0, jnp.where(bottom, slow, 0.0))
+        ut = weight * u + 0.1 * (v + u_up + u_down) - grad_x
+        vt = weight * v + 0.1 * (v_up + v_down - u) - grad_y
+        low = jnp.where(bottom, ut, low[0]), jnp.where(bottom, vt, low[1])
+        u_new = ut * retain
+        v_new = vt * retain
+        second = jnp.where(above_bottom, u_new, second[0]), jnp.where(above_bottom, v_new, second[1])
+        store(level, u_new, v_new)
+        total = total[0] + u_new, total[1] + v_new
+        u_up, v_up, u, v = u, v, u_down, v_down
+    return total, low, second
+
+
+def forward_kernel(state, above, below, depth, wet, drag, saved, surfaces,
+                   work, wet_pad, thick, drag_pad, eta, sum_u, sum_v, bot_u, bot_v, next_u, next_v,
+                   slope_x, slope_y, factor):
     fields, rows, _ = state.shape
     levels = (fields - 1) // 2
+    kept_rows = slice(HALO, REACH + HALO + rows)
     fill_padded(wet_pad, wet[...], above[fields + 1], below[fields + 1])
     fill_padded(drag_pad, drag[...], above[fields + 2], below[fields + 2])
     fill_padded(thick, depth[...], above[fields], below[fields])
@@ -312,96 +390,64 @@
         bot_v[at] = low_v
 
     over_blocks(rows, REACH, sums, state, above, below)
-    saved[0] = bot_u[HALO : REACH + HALO + rows]
-    saved[1] = bot_v[HALO : REACH + HALO + rows]
+    saved[0] = bot_u[kept_rows]
+    saved[1] = bot_v[kept_rows]
 
     for step in range(STEPS):
-        first, last = step == 0, step == STEPS - 1
         sea = jnp.minimum(wet_pad[...], 1.0)
         flux_x = thick[...] * sum_u[...]
         flux_y = thick[...] * sum_v[...]
         surface = sea * (eta[...] - 0.2 * (row_diff(flux_x) + column_diff(flux_y)))
         eta[...] = surface
+        surfaces[step] = eta[kept_rows]
         slope_x[...] = 0.2 * row_diff(surface)
         slope_y[...] = 0.2 * column_diff(surface)
-        factor[...] = drag_terms(bot_u[...], bot_v[...], thick[...], drag_pad[...], sea)[2]
-
-        def update(at, source, source_at, into_final=False):
-            wet_here = wet_pad[at]
-            slow = factor[at]
-            grad_x = slope_x[at]
-            grad_y = slope_y[at]
-            zero = jnp.zeros_like(wet_here)
-            total_u = total_v = low_u = low_v = zero
-
-            def fetch(level):
-                if level == levels:
-                    return zero, zero
-                u = source[1 + level, source_at]
-                v = source[1 + levels + level, source_at]
-                if first:
-                    u = jnp.where(wet_here > level, u, 0.0)
-                    v = jnp.where(wet_here > level, v, 0.0)
-                return u, v
-
-            u_up = v_up = zero
-            u, v = fetch(0)
-            for level in range(levels):
-                u_down, v_down = fetch(level + 1)
-                inside = wet_here > level + 1
-                bottom = wet_here == level + 1
-                own = 1.0 if level == 0 else 0.9
-                weight = jnp.where(inside, own - 0.1, own)
-                retain = jnp.where(inside, 1.0, jnp.where(bottom, slow, 0.0))
-                ut = weight * u + 0.1 * (v + u_up + u_down) - grad_x
-                vt = weight * v + 0.1 * (v_up + v_down - u) - grad_y
-                low_u = jnp.where(bottom, ut, low_u)
-                low_v = jnp.where(bottom, vt, low_v)
-                u_new = ut * retain
-                v_new = vt * retain
-                if into_final:
-                    final[1 + level, source_at] = u_new
-                    final[1 + levels + level, source_at] = v_new
-                else:
-                    work[1 + level, at] = u_new
-                    work[1 + levels + level, at] = v_new
-                    total_u += u_new
-                    total_v += v_new
-                u_up, v_up, u, v = u, v, u_down, v_down
-            sum_u[at] = total_u
-            sum_v[at] = total_v
-            bot_u[at] = low_u
-            bot_v[at] = low_v
-
-        if first:
-            over_blocks(rows, REACH, update, state, above, below)
-        elif last:
-
-            def into_final(start):
-                at = pl.ds(pl.multiple_of(start + REACH, BLOCK), BLOCK)
-                update(at, Shifted(work, at), pl.ds(start, BLOCK), True)
-
-            looped(rows, into_final)
-            for start in range(HALO, REACH, BLOCK):
-                for at in (pl.ds(start, BLOCK), pl.ds(start + HALO + rows, BLOCK)):
-                    update(at, work, at)
+        if step == STEPS - 1:
+            weight = jnp.where(wet_pad[...] > 1.0, 0.9, 1.0)
+            low_u, low_v = bot_u[...], bot_v[...]
+            floor = wet_pad[...] > 0.0
+            last_u = weight * low_u + 0.1 * (low_v + next_u[...]) - slope_x[...]
+            last_v = weight * low_v + 0.1 * (next_v[...] - low_u) - slope_y[...]
+            bot_u[...] = jnp.where(floor, last_u, 0.0)
+            bot_v[...] = jnp.where(floor, last_v, 0.0)
         else:
-
-            def in_place(start):
-                at = pl.ds(start, BLOCK)
-                update(at, work, at)
-
-            looped(rows + 2 * REACH, in_place)
-        saved[2 + 2 * step] = bot_u[HALO : REACH + HALO + rows]
-        saved[3 + 2 * step] = bot_v[HALO : REACH + HALO + rows]
-        bot_u[...] = factor[...] * bot_u[...]
-        bot_v[...] = factor[...] * bot_v[...]
-    final[0] = eta[REACH : REACH + rows]
-    pack(final, wet, order, packed)
-
-
-def adjoint_kernel(adjoint, misfit, kept, above, below, depth, wet, drag,
-                   start, gradient,
+            factor[...] = drag_terms(bot_u[...], bot_v[...], thick[...], drag_pad[...], sea)[2]
+
+            def update(at, source, source_at):
+                wet_here = wet_pad[at]
+
+                def fetch(level):
+                    u = source[1 + level, source_at]
+                    v = source[1 + levels + level, source_at]
+                    if step == 0:
+                        u = jnp.where(wet_here > level, u, 0.0)
+                        v = jnp.where(wet_here > level, v, 0.0)
+                    return u, v
+
+                def store(level, u, v):
+                    work[1 + level, at] = u
+                    work[1 + levels + level, at] = v
+
+                total, low, second = column_step(
+                    levels, wet_here, factor[at], slope_x[at], slope_y[at], fetch, store
+                )
+                sum_u[at], sum_v[at] = total
+                bot_u[at], bot_v[at] = low
+                next_u[at], next_v[at] = second
+
+            if step == 0:
+                over_blocks(rows, REACH, update, state, above, below)
+            else:
+                looped(rows + 2 * REACH, lambda start: update(pl.ds(start, BLOCK), work, pl.ds(start, BLOCK)))
+        saved[2 + 2 * step] = bot_u[kept_rows]
+        saved[3 + 2 * step] = bot_v[kept_rows]
+        if step < STEPS - 1:
+            bot_u[...] = factor[...] * bot_u[...]
+            bot_v[...] = factor[...] * bot_v[...]
+
+
+def adjoint_kernel(adjoint, misfit, kept, above, below, depth, wet, drag, order,
+                   output, gradient, packed, start, sem,
                    work, wet_pad, thick, drag_pad, eta, sum_u, sum_v, bot_u, bot_v,
                    push_x, push_y, push_low_x, push_low_y, factor, grad_pad):
     fields, rows, _ = adjoint.shape
@@ -529,6 +575,14 @@
             looped(rows + 2 * HALO, in_place)
     start[0] = eta[HALO : HALO + rows]
     gradient[...] = grad_pad[HALO : HALO + rows]
+    copy = pltpu.make_async_copy(start, output, sem)
+    copy.start()
+    pack(start, wet, order, packed)
+    for pool in range(rows // POOL):
+        for half in range(2):
+            at = pool * POOL + half * (POOL // 2)
+            packed[2 * SLOTS + half, pool * (POOL // 2) : (pool + 1) * (POOL // 2)] = start[0, at : at + POOL // 2]
+    copy.wait()
 
 
 def body(start_states, end_adjoints, misfits, water_depth, drag_coef, sea_mask, bottom_level):
@@ -540,7 +594,7 @@
     whole_numbers = lambda *shape: jax.ShapeDtypeStruct(shape, jnp.int32)
     pad = lambda halo: pltpu.VMEM((rows + 2 * halo, width), jnp.float32)
     work = lambda halo: pltpu.VMEM((fields, rows + 2 * halo, width), jnp.float32)
-    params = pltpu.CompilerParams(vmem_limit_bytes=32 << 20)
+    params = pltpu.CompilerParams(vmem_limit_bytes=16 << 20)
     cells = fields * rows * width
     cost = pl.CostEstimate(flops=100 * cells, bytes_accessed=10 * cells, transcendentals=0)
     state_shape = floats(fields, rows, width)
@@ -552,9 +606,11 @@
 
     upward, downward = pl.pallas_call(
         edge_kernel,
-        in_specs=[anywhere] * 2 + [in_vmem] * 5,
+        in_specs=[anywhere] * 7,
+        out_specs=(in_vmem, in_vmem),
         out_shape=(edge_shape, edge_shape),
-        scratch_shapes=[pltpu.SemaphoreType.DMA((6,))],
+        scratch_shapes=[pltpu.VMEM((2, REACH, width), jnp.int32)] * 2 + [pltpu.SemaphoreType.DMA((22,))],
+        compiler_params=params,
         cost_estimate=cost,
         name="edges",
     )(initial, adjoint, misfit, water_depth, drag_coef, sea_mask, bottom_level)
@@ -565,60 +621,80 @@
         plan_kernel,
         out_specs=(in_vmem,) * 3 + (in_smem,),
         out_shape=(floats(rows, width), whole_numbers(rows, width), whole_numbers(rows, width), whole_numbers(1, 1)),
+        compiler_params=params,
         cost_estimate=cost,
         name="plan",
     )(sea_mask, bottom_level)
 
-    final, saved, final_packed = pl.pallas_call(
+    raw = pl.pallas_call(
+        pack_kernel,
+        out_shape=floats(2 * SLOTS, rows // 2, width),
+        compiler_params=params,
+        cost_estimate=cost,
+        name="pack",
+    )(initial, wet, order)
+    came_raw = passed_along(raw, "slab", 1)
+
+    saved, surfaces = pl.pallas_call(
         forward_kernel,
-        out_shape=(state_shape, floats(SAVED, rows + 2 * HALO, width), packed_shape),
-        scratch_shapes=[work(REACH)] + [pad(REACH)] * 11,
+        out_shape=(floats(SAVED, rows + 2 * HALO, width), floats(STEPS, rows + 2 * HALO, width)),
+        scratch_shapes=[work(REACH)] + [pad(REACH)] * 13,
         compiler_params=params,
         cost_estimate=cost,
         name="forward",
-    )(initial, above, below, water_depth, wet, drag_coef, order)
-    came_state = passed_along(final_packed, "slab", 1)
-
-    start, gradient = pl.pallas_call(
+    )(initial, above, below, water_depth, wet, drag_coef)
+    came_surfaces = passed_along(surfaces, "slab", 1)
+
+    start, gradient, start_packed = pl.pallas_call(
         adjoint_kernel,
-        out_shape=(state_shape, floats(rows, width)),
-        scratch_shapes=[work(HALO)] + [pad(HALO)] * 14,
+        out_specs=(anywhere, in_vmem, in_vmem),
+        out_shape=(state_shape, floats(rows, width), packed_shape),
+        scratch_shapes=[work(0), pltpu.SemaphoreType.DMA(()), work(HALO)] + [pad(HALO)] * 14,
         compiler_params=params,
         cost_estimate=cost,
         name="adjoint",
-    )(adjoint, misfit, saved, above, below, water_depth, wet, drag_coef)
+    )(adjoint, misfit, saved, above, below, water_depth, wet, drag_coef, order)
     slabs = lax.axis_size("slab")
     if slabs > 4:
         gradients = [lax.psum(gradient, "slab")]
     else:
         gradients = [gradient] + [passed_along(gradient, "slab", distance) for distance in range(1, slabs)]
-    start_packed = pl.pallas_call(
-        pack_kernel, out_shape=packed_shape, compiler_params=params, cost_estimate=cost, name="pack"
-    )(start, wet, order)
+    start_packed, came_raw, came_surfaces = lax.optimization_barrier((start_packed, came_raw, came_surfaces))
     came_adjoint = passed_along(start_packed, "slab", -1)
 
-    def received(kernel, packed, sent, distance, *extra):
-        fallback = lax.cond(
+    def unless_packed(sent, distance):
+        return lax.cond(
             deepest[0, 0] > SLOTS,
             lambda sent: passed_along(sent, "slab", distance),
-            lambda sent: pl.pallas_call(nothing_kernel, out_specs=anywhere, out_shape=state_shape, name="nothing")(),
+            lambda sent: pl.pallas_call(
+                nothing_kernel, out_specs=anywhere, out_shape=state_shape, compiler_params=params, name="nothing"
+            )(),
             sent,
         )
-        pool = pl.BlockSpec((POOL, width), lambda i: (i, 0))
-        return pl.pallas_call(
-            kernel,
-            grid=(rows // POOL,),
-            in_specs=[in_smem, pl.BlockSpec((2 * SLOTS + 2, POOL // 2, width), lambda i: (0, i, 0)),
-                      pool, pool, pool, anywhere] + [pool] * len(extra),
-            out_specs=[pl.BlockSpec((fields, POOL, width), lambda i: (0, i, 0))] + [pool] * bool(extra),
-            out_shape=[state_shape] + [floats(rows, width)] * bool(extra),
-            compiler_params=params,
-            cost_estimate=cost,
-            name="unpack",
-        )(deepest, packed, wet, order, place, fallback, *extra)
-
-    (next_state,) = received(unpack_kernel, came_state, final, 1)
-    next_adjoint, drag_total = received(unpack_adjoint_kernel, came_adjoint, start, -1, *gradients)
+
+    next_state = pl.pallas_call(
+        replay_kernel,
+        in_specs=[in_smem] + [in_vmem] * 7 + [anywhere],
+        out_shape=state_shape,
+        scratch_shapes=[pad(0)] * 6,
+        compiler_params=params,
+        cost_estimate=cost,
+        name="replay",
+    )(deepest, came_raw, wet, order, place, water_depth, drag_coef, came_surfaces,
+      unless_packed(initial, 1))
+
+    pool = pl.BlockSpec((POOL, width), lambda i: (i, 0))
+    next_adjoint, drag_total = pl.pallas_call(
+        unpack_kernel,
+        grid=(rows // POOL,),
+        in_specs=[in_smem, pl.BlockSpec((2 * SLOTS + 2, POOL // 2, width), lambda i: (0, i, 0)),
+                  pool, pool, pool, anywhere] + [pool] * len(gradients),
+        out_specs=[pl.BlockSpec((fields, POOL, width), lambda i: (0, i, 0)), pool],
+        out_shape=[state_shape, floats(rows, width)],
+        compiler_params=params,
+        cost_estimate=cost,
+        name="unpack",
+    )(deepest, came_adjoint, wet, order, place, unless_packed(start, -1), *gradients)
     return (next_state[None], next_adjoint[None], drag_total)
 
 

time: 76.8 us -> 65.3 us (0.85); the launches traced: 75.6 us -> 65.1 us
  waiting for transfers between devices: 29.7 us -> 21.1 us
  Pallas kernels: 29.6 us -> 26.2 us
  starting transfers between devices: 13.3 us -> 14.7 us
    ppermute x5 -> x6, waiting for transfers between devices: 23.3 us -> 10.9 us  [passed_along(): return lax.ppermute(block, axis, route)]
    ppermute x2, waiting for transfers between devices: 6.42 us -> 10.2 us  [shifted(): return lax.ppermute(block, axis, route)]
    pallas_call x8, Pallas kernels: 25.8 us -> 23.2 us  [the longest x1 6.01 us: body(): pl.pallas_call(replay_kernel, in_specs=[in_smem] + [in_vmem] * 7 + [anywh...]
    ppermute x5 -> x6, starting transfers between devices: 6.72 us -> 8.81 us  [passed_along(): return lax.ppermute(block, axis, route)]
    pallas_call x1, Pallas kernels: 3.78 us -> 3 us  [body(): pl.pallas_call(plan_kernel, out_specs=(in_vmem,) * 3 + (in_smem,), out_sh...]
    unnamed x20 -> x14, local copies, waits for them, and re-layouts: 1.54 us -> 1.65 us
  transfers between devices with their start and end apart: 7 -> 8, of which waited for: 5 -> 4; matrix products, arithmetic and copies ran while one was open for 0% -> 0% of each run, Pallas kernels for 20% -> 27%
where the time goes in v3:
time: 65.3 us; the launch traced here: 65.1 us
  Pallas kernels  26.2 us (40%)
  waiting for transfers between devices  21.1 us (32%)
  starting transfers between devices  14.7 us (23%)
  local copies, waits for them, and re-layouts  1.65 us (3%)
  between operations  1.41 us (2%)
    ppermute x6, waiting for transfers between devices, passed_along(): return lax.ppermute(block, axis, route)  10.9 us
    ppermute x2, waiting for transfers between devices, shifted(): return lax.ppermute(block, axis, route)  10.2 us
    ppermute x6, starting transfers between devices, passed_along(): return lax.ppermute(block, axis, route)  8.81 us
    pallas_call x1, Pallas kernels, body(): pl.pallas_call(replay_kernel, in_specs=[in_smem] + [in_vmem] * 7 + [anywh...  6.01 us
    ppermute x2, starting transfers between devices, shifted(): return lax.ppermute(block, axis, route)  5.88 us
    pallas_call x1, Pallas kernels, body(): pl.pallas_call(adjoint_kernel, out_specs=(anywhere, in_vmem, in_vmem), ou...  5.77 us
    pallas_call x1, Pallas kernels, body(): pl.pallas_call(forward_kernel, out_shape=(floats(SAVED, rows + 2 * HALO,...  4.22 us
    pallas_call x1, Pallas kernels, body(): pl.pallas_call(unpack_kernel, grid=(rows // POOL,), in_specs=[in_smem, pl...  3.08 us
  transfers between devices with their start and end apart: 8, of which 4 were waited for; matrix products, arithmetic and copies ran while one was open for 0% of the time, Pallas kernels for 27%

profile of v3, /device:TPU:1, one launch (start us, length us, event | category | flops | bytes accessed | tf_op | source)
XLA Modules:
  0.0 65.1 jit_solution(17556969840710822848)
XLA Ops:
  0.6 0.0 copy-start
  0.6 0.0 copy-start.3
  0.7 0.0 copy-start.1
  0.7 0.0 copy-start.4
  0.7 0.9 %copy-done.4 = s32[64,128]{1,0:T(8,128)S(1)} copy-done((s32[64,128]{1,0:T(8,128)S(1)}, s32[64,128]{1,0:T(8,128)}, u32[]{:S(2)}) %copy-start.4) | copy-done | bytes 32792
  1.5 0.8 %copy-done.5 = s32[64,128]{1,0:T(8,128)S(1)} copy-done((s32[64,128]{1,0:T(8,128)S(1)}, s32[64,128]{1,0:T(8,128)}, u32[]{:S(2)}) %copy-start.5) | copy-done | bytes 32792
  2.3 3.0 %plan.1 = (f32[64,128]{1,0:T(8,128)S(1)}, s32[64,128]{1,0:T(8,128)S(1)}, s32[64,128]{1,0:T(8,128)S(1)}, s32[1,1]{1,0:T(1,128)}) custom-call(s32[64,128]{1,0:T(8,128)S(1)} %copy-done.4, s32[64,128]{1,0:T(8,128)S(1)} %copy-done.5), custom_call_target="tpu_custom_call" | custom-call | flops 40140800 | bytes 4014080 | tf_op jit(solution)/shard_map/plan/pallas_call | solution.py:620
  5.3 2.6 %pack.1 = f32[58,32,128]{2,1,0:T(8,128)S(1)} custom-call(f32[49,64,128]{2,1,0:T(8,128)} %bitcast.10, f32[64,128]{1,0:T(8,128)S(1)} %get-tuple-element.30.wet, s32[64,128]{1,0:T(8,128)S(1)} %get-tuple-element.32.order), custom_call_target="tpu_custom_call" | custom-call | flops 40140800 | bytes 4014080 | tf_op jit(solution)/shard_map/pack/pallas_call | solution.py:629
  8.0 2.2 %collective-permute-start.4 = (f32[58,32,128]{2,1,0:T(8,128)S(1)}, f32[58,32,128]{2,1,0:T(8,128)S(1)}, u32[]{:S(2)}, u32[]{:S(2)}) collective-permute-start(f32[58,32,128]{2,1,0:T(8,128)S(1)} %pack.1), channel_id=1, source_target_pairs={{3,0},{0,1},{1,2},{2,3},{7,4},{4,5},{5,6},{6,7},{11,8},{8,9},{9,10... | collective-permute-start | bytes 2850824 | tf_op jit(solution)/shard_map/ppermute | solution.py:26
  10.1 0.0 copy-done.3
  10.1 0.0 copy-done.2
  10.1 0.0 copy-start.6
  10.2 1.5 %edges.1 = (f32[79,16,128]{2,1,0:T(8,128)S(1)}, f32[79,16,128]{2,1,0:T(8,128)S(1)}) custom-call(f32[49,64,128]{2,1,0:T(8,128)} %bitcast.11, f32[49,64,128]{2,1,0:T(8,128)S(1)} %bitcast.6, f32[4,64,128]{2,1,0:T(8,128)S(1)} %bitcast.8, f32[64,128]{1,0:T(8,128)S(1)} %copy-done.1, f32[64,128]{1,0:T(8,128)S(1)} %copy-done.2, s32[64,128]{1,0:T(8,128)S(1)} %copy-done.4, ...), custom_call_target="tpu_custom_call" | custom-call | flops 40140800 | bytes 4014080 | tf_op jit(solution)/shard_map/edges/pallas_call | solution.py:607
  11.6 4.0 %collective-permute-start.2 = (f32[79,16,128]{2,1,0:T(8,128)S(1)}, f32[79,16,128]{2,1,0:T(8,128)S(1)}, u32[]{:S(2)}, u32[]{:S(2)}) collective-permute-start(f32[79,16,128]{2,1,0:T(8,128)S(1)} %get-tuple-element.28), channel_id=1, source_target_pairs={{0,4},{4,8},{8,12},{1,5},{5,9},{9,13},{2,6},{6,10},{10,14},{3,7},{... | collective-permute-start | bytes 1941512 | tf_op jit(solution)/shard_map/ppermute | solution.py:20
  15.6 1.9 %collective-permute-start.3 = (f32[79,16,128]{2,1,0:T(8,128)S(1)}, f32[79,16,128]{2,1,0:T(8,128)S(1)}, u32[]{:S(2)}, u32[]{:S(2)}) collective-permute-start(f32[79,16,128]{2,1,0:T(8,128)S(1)} %get-tuple-element.29), channel_id=1, source_target_pairs={{4,0},{8,4},{12,8},{5,1},{9,5},{13,9},{6,2},{10,6},{14,10},{7,3},{... | collective-permute-start | bytes 1941512 | tf_op jit(solution)/shard_map/ppermute | solution.py:20
  17.5 5.5 %collective-permute-done.2.above = f32[79,16,128]{2,1,0:T(8,128)S(1)} collective-permute-done((f32[79,16,128]{2,1,0:T(8,128)S(1)}, f32[79,16,128]{2,1,0:T(8,128)S(1)}, u32[]{:S(2)}, u32[]{:S(2)}) %collective-permute-start.2) | collective-permute-done | bytes 647200 | tf_op jit(solution)/shard_map/ppermute | solution.py:20
  23.0 4.7 %collective-permute-done.3.below = f32[79,16,128]{2,1,0:T(8,128)S(1)} collective-permute-done((f32[79,16,128]{2,1,0:T(8,128)S(1)}, f32[79,16,128]{2,1,0:T(8,128)S(1)}, u32[]{:S(2)}, u32[]{:S(2)}) %collective-permute-start.3) | collective-permute-done | bytes 647200 | tf_op jit(solution)/shard_map/ppermute | solution.py:20
  27.7 4.2 %forward.1 = (f32[10,80,128]{2,1,0:T(8,128)S(1)}, f32[4,80,128]{2,1,0:T(8,128)S(1)}) custom-call(f32[49,64,128]{2,1,0:T(8,128)S(1)} %bitcast.12, f32[79,16,128]{2,1,0:T(8,128)S(1)} %collective-permute-done.2.above, f32[79,16,128]{2,1,0:T(8,128)S(1)} %collective-permute-done.3.below, f32[64,128]{1,0:T(8,128)S(1)} %copy-done.1, ...), custom_call_target="tpu_custom_call" | custom-call | flops 40140800 | bytes 4014080 | tf_op jit(solution)/shard_map/forward/pallas_call | solution.py:638
  31.9 1.3 %collective-permute-start.5 = (f32[4,80,128]{2,1,0:T(8,128)S(1)}, f32[4,80,128]{2,1,0:T(8,128)S(1)}, u32[]{:S(2)}, u32[]{:S(2)}) collective-permute-start(f32[4,80,128]{2,1,0:T(8,128)S(1)} %get-tuple-element.34), channel_id=1, source_target_pairs={{3,0},{0,1},{1,2},{2,3},{7,4},{4,5},{5,6},{6,7},{11,8},{8,9},{9,10... | collective-permute-start | bytes 491528 | tf_op jit(solution)/shard_map/ppermute | solution.py:26
  33.3 5.8 %adjoint.1 = (f32[49,64,128]{2,1,0:T(8,128)}, f32[64,128]{1,0:T(8,128)S(1)}, f32[60,32,128]{2,1,0:T(8,128)S(1)}) custom-call(f32[49,64,128]{2,1,0:T(8,128)S(1)} %bitcast.7, f32[4,64,128]{2,1,0:T(8,128)S(1)} %bitcast.9, f32[10,80,128]{2,1,0:T(8,128)S(1)} %get-tuple-element.31.kept, f32[79,16,128]{2,1,0:T(8,128)S(1)} %collective-permute-done.2.above, ...), custom_call_target="tpu_custom_call" | custom-call | flops 40140800 | bytes 4014080 | tf_op jit(solution)/shard_map/adjoint/pallas_call | solution.py:648
  39.1 0.0 collective-permute-done.5.surfaces
  39.1 0.0 collective-permute-done.4.packed
  39.1 2.0 %collective-permute-start.6 = (f32[60,32,128]{2,1,0:T(8,128)S(1)}, f32[60,32,128]{2,1,0:T(8,128)S(1)}, u32[]{:S(2)}, u32[]{:S(2)}) collective-permute-start(f32[60,32,128]{2,1,0:T(8,128)S(1)} %get-tuple-element.38), channel_id=1, source_target_pairs={{1,0},{2,1},{3,2},{0,3},{5,4},{6,5},{7,6},{4,7},{9,8},{10,9},{11,1... | collective-permute-start | bytes 2949128 | tf_op jit(solution)/shard_map/ppermute | solution.py:26
  41.1 0.0 collective-permute-start.7
  41.1 0.5 collective-permute-start.8
  41.6 2.7 %collective-permute-start.9 = (f32[64,128]{1,0:T(8,128)S(1)}, f32[64,128]{1,0:T(8,128)S(1)}, u32[]{:S(2)}, u32[]{:S(2)}) collective-permute-start(f32[64,128]{1,0:T(8,128)S(1)} %get-tuple-element.40.rest_0_), channel_id=1, source_target_pairs={{1,0},{2,1},{3,2},{0,3},{5,4},{6,5},{7,6},{4,7},{9,8},{10,9},{11,1... | collective-permute-start | bytes 98312 | tf_op jit(solution)/shard_map/ppermute | solution.py:26
  45.1 6.0 %replay.1 = f32[49,64,128]{2,1,0:T(8,128)} custom-call(s32[1,1]{1,0:T(1,128)} %get-tuple-element.27.deepest, f32[58,32,128]{2,1,0:T(8,128)S(1)} %collective-permute-done.4.packed, f32[64,128]{1,0:T(8,128)S(1)} %get-tuple-element.30.wet, s32[64,128]{1,0:T(8,128)S(1)} %get-tuple-element.32.order, s32[64,128]{1,0:T(8,128)S(1)} %get-tuple-element.36.place, ...), custom_call_target="tpu_custom_call" | custom-call | flops 40140800 | bytes 4014080 | tf_op jit(solution)/shard_map/replay/pallas_call | solution.py:675
  51.1 10.4 %collective-permute-done.7.rest_1_ = f32[64,128]{1,0:T(8,128)S(1)} collective-permute-done((f32[64,128]{1,0:T(8,128)S(1)}, f32[64,128]{1,0:T(8,128)S(1)}, u32[]{:S(2)}, u32[]{:S(2)}) %collective-permute-start.7) | collective-permute-done | bytes 32800 | tf_op jit(solution)/shard_map/ppermute | solution.py:26
  61.5 0.0 collective-permute-done.8.rest_2_
  61.5 0.5 collective-permute-done.9.rest_3_
  62.0 0.0 collective-permute-done.6.packed
  62.0 3.1 %unpack.1 = (f32[49,64,128]{2,1,0:T(8,128)}, f32[64,128]{1,0:T(8,128)}) custom-call(s32[1,1]{1,0:T(1,128)} %get-tuple-element.27.deepest, f32[60,32,128]{2,1,0:T(8,128)S(1)} %collective-permute-done.6.packed, f32[64,128]{1,0:T(8,128)S(1)} %get-tuple-element.30.wet, s32[64,128]{1,0:T(8,128)S(1)} %get-tuple-element.32.order, ...), custom_call_target="tpu_custom_call" | custom-call | flops 40140800 | bytes 4014080 | tf_op jit(solution)/shard_map/unpack/pallas_call | solution.py:687
  (9 shorter events, 0.1 us)
Async XLA Ops:
  0.6 9.5 %copy-start = (f32[1,49,64,128]{3,2,1,0:T(8,128)S(1)}, f32[1,49,64,128]{3,2,1,0:T(8,128)}, u32[]{:S(2)}) copy-start(f32[1,49,64,128]{3,2,1,0:T(8,128)} %param.12) | copy-start | bytes 4816900
  0.6 9.5 %copy-start.3 = (f32[1,4,64,128]{3,2,1,0:T(8,128)S(1)}, f32[1,4,64,128]{3,2,1,0:T(8,128)}, u32[]{:S(2)}) copy-start(f32[1,4,64,128]{3,2,1,0:T(8,128)} %param.13) | copy-start | bytes 393220
  0.7 9.5 %copy-start.1 = (f32[64,128]{1,0:T(8,128)S(1)}, f32[64,128]{1,0:T(8,128)}, u32[]{:S(2)}) copy-start(f32[64,128]{1,0:T(8,128)} %depth.7) | copy-start | bytes 98308
  0.7 0.9 %copy-start.4 = (s32[64,128]{1,0:T(8,128)S(1)}, s32[64,128]{1,0:T(8,128)}, u32[]{:S(2)}) copy-start(s32[64,128]{1,0:T(8,128)} %mask.3) | copy-start | bytes 98308
  1.5 0.8 %copy-start.5 = (s32[64,128]{1,0:T(8,128)S(1)}, s32[64,128]{1,0:T(8,128)}, u32[]{:S(2)}) copy-start(s32[64,128]{1,0:T(8,128)} %bottom.3) | copy-start | bytes 98308
  2.3 7.8 %copy-start.2 = (f32[64,128]{1,0:T(8,128)S(1)}, f32[64,128]{1,0:T(8,128)}, u32[]{:S(2)}) copy-start(f32[64,128]{1,0:T(8,128)} %drag.7) | copy-start | bytes 98308
  8.0 31.1 %collective-permute-start.4 = (f32[58,32,128]{2,1,0:T(8,128)S(1)}, f32[58,32,128]{2,1,0:T(8,128)S(1)}, u32[]{:S(2)}, u32[]{:S(2)}) collective-permute-start(f32[58,32,128]{2,1,0:T(8,128)S(1)} %pack.1), channel_id=1, source_target_pairs={{3,0},{0,1},{1,2},{2,3},{7,4},{4,5},{5,6},{6,7},{11,8},{8,9},{9,10... | collective-permute-start | bytes 2850824 | tf_op jit(solution)/shard_map/ppermute | solution.py:26
  10.1 17.6 %copy-start.6 = (f32[1,49,64,128]{3,2,1,0:T(8,128)S(1)}, f32[1,49,64,128]{3,2,1,0:T(8,128)}, u32[]{:S(2)}) copy-start(f32[1,49,64,128]{3,2,1,0:T(8,128)} %param.11) | copy-start | bytes 4816900
  11.6 11.4 %collective-permute-start.2 = (f32[79,16,128]{2,1,0:T(8,128)S(1)}, f32[79,16,128]{2,1,0:T(8,128)S(1)}, u32[]{:S(2)}, u32[]{:S(2)}) collective-permute-start(f32[79,16,128]{2,1,0:T(8,128)S(1)} %get-tuple-element.28), channel_id=1, source_target_pairs={{0,4},{4,8},{8,12},{1,5},{5,9},{9,13},{2,6},{6,10},{10,14},{3,7},{... | collective-permute-start | bytes 1941512 | tf_op jit(solution)/shard_map/ppermute | solution.py:20
  15.6 12.1 %collective-permute-start.3 = (f32[79,16,128]{2,1,0:T(8,128)S(1)}, f32[79,16,128]{2,1,0:T(8,128)S(1)}, u32[]{:S(2)}, u32[]{:S(2)}) collective-permute-start(f32[79,16,128]{2,1,0:T(8,128)S(1)} %get-tuple-element.29), channel_id=1, source_target_pairs={{4,0},{8,4},{12,8},{5,1},{9,5},{13,9},{6,2},{10,6},{14,10},{7,3},{... | collective-permute-start | bytes 1941512 | tf_op jit(solution)/shard_map/ppermute | solution.py:20
  31.9 7.1 %collective-permute-start.5 = (f32[4,80,128]{2,1,0:T(8,128)S(1)}, f32[4,80,128]{2,1,0:T(8,128)S(1)}, u32[]{:S(2)}, u32[]{:S(2)}) collective-permute-start(f32[4,80,128]{2,1,0:T(8,128)S(1)} %get-tuple-element.34), channel_id=1, source_target_pairs={{3,0},{0,1},{1,2},{2,3},{7,4},{4,5},{5,6},{6,7},{11,8},{8,9},{9,10... | collective-permute-start | bytes 491528 | tf_op jit(solution)/shard_map/ppermute | solution.py:26
  39.1 22.9 %collective-permute-start.6 = (f32[60,32,128]{2,1,0:T(8,128)S(1)}, f32[60,32,128]{2,1,0:T(8,128)S(1)}, u32[]{:S(2)}, u32[]{:S(2)}) collective-permute-start(f32[60,32,128]{2,1,0:T(8,128)S(1)} %get-tuple-element.38), channel_id=1, source_target_pairs={{1,0},{2,1},{3,2},{0,3},{5,4},{6,5},{7,6},{4,7},{9,8},{10,9},{11,1... | collective-permute-start | bytes 2949128 | tf_op jit(solution)/shard_map/ppermute | solution.py:26
  41.1 20.4 %collective-permute-start.7 = (f32[64,128]{1,0:T(8,128)S(1)}, f32[64,128]{1,0:T(8,128)S(1)}, u32[]{:S(2)}, u32[]{:S(2)}) collective-permute-start(f32[64,128]{1,0:T(8,128)S(1)} %get-tuple-element.40.rest_0_), channel_id=1, source_target_pairs={{3,0},{0,1},{1,2},{2,3},{7,4},{4,5},{5,6},{6,7},{11,8},{8,9},{9,10... | collective-permute-start | bytes 98312 | tf_op jit(solution)/shard_map/ppermute | solution.py:26
  41.1 20.4 %collective-permute-start.8 = (f32[64,128]{1,0:T(8,128)S(1)}, f32[64,128]{1,0:T(8,128)S(1)}, u32[]{:S(2)}, u32[]{:S(2)}) collective-permute-start(f32[64,128]{1,0:T(8,128)S(1)} %get-tuple-element.40.rest_0_), channel_id=1, source_target_pairs={{2,0},{3,1},{0,2},{1,3},{6,4},{7,5},{4,6},{5,7},{10,8},{11,9},{8,1... | collective-permute-start | bytes 98312 | tf_op jit(solution)/shard_map/ppermute | solution.py:26
  41.6 20.3 %collective-permute-start.9 = (f32[64,128]{1,0:T(8,128)S(1)}, f32[64,128]{1,0:T(8,128)S(1)}, u32[]{:S(2)}, u32[]{:S(2)}) collective-permute-start(f32[64,128]{1,0:T(8,128)S(1)} %get-tuple-element.40.rest_0_), channel_id=1, source_target_pairs={{1,0},{2,1},{3,2},{0,3},{5,4},{6,5},{7,6},{4,7},{9,8},{10,9},{11,1... | collective-permute-start | bytes 98312 | tf_op jit(solution)/shard_map/ppermute | solution.py:26

commit v4 on v3

--- a/solution.py
+++ b/solution.py
@@ -12,6 +12,7 @@
 SAVED = 2 + 2 * STEPS
 POOL = 4 * BLOCK
 SLOTS = 29
+LEVELS = 24
 
 
 def shifted(block, axis, distance):
@@ -102,10 +103,20 @@
     wet[...] = depth.astype(jnp.float32)
     lane = lanes_of(depth)
     even = (lax.broadcasted_iota(jnp.int32, depth.shape, 0) // BLOCK) % 2 == 0
-    key = (depth * width + lane).astype(jnp.float32)
-    rank = jnp.zeros_like(depth)
-    for shift in range(1, width):
-        rank = rank + jnp.where(pltpu.roll(key, shift, 1) > key, 1, 0)
+    most_levels = LEVELS
+    before = lax.broadcasted_iota(jnp.int32, (width, 2 * width), 0) < lax.broadcasted_iota(jnp.int32, (width, 2 * width), 1)
+    same = [jnp.where(depth == level, 1.0, 0.0) for level in range(most_levels, -1, -1)]
+    counts = jnp.dot(
+        jnp.concatenate(same).astype(jnp.bfloat16),
+        jnp.where(before, 1.0, 0.0).astype(jnp.bfloat16),
+        preferred_element_type=jnp.float32,
+    )
+    deeper = rank = jnp.zeros(depth.shape, jnp.float32)
+    for index, level in enumerate(range(most_levels, -1, -1)):
+        here = counts[index * rows : (index + 1) * rows]
+        rank = jnp.where(depth == level, deeper + here[:, :width], rank)
+        deeper = deeper + here[:, width:]
+    rank = rank.astype(jnp.int32)
     ahead = jnp.where(rank < half, rank, width + half - 1 - rank)
     behind = jnp.where(rank < half, rank + half, width - 1 - rank)
     there = jnp.where(even, ahead, behind)
@@ -214,8 +225,8 @@
                 write_level(far, tail, head)
 
 
-def unpack_kernel(deepest, packed, wet, order, place, whole, *rest):
-    *gradients, state, total = rest
+def unpack_kernel(deepest, packed, wet, order, place, whole, state, done):
+    done[...] = jnp.zeros_like(done)
     pool = pl.program_id(0)
 
     @pl.when(deepest[0, 0] > SLOTS)
@@ -227,11 +238,6 @@
         unpack_pool(packed, wet, order, place, state, 0)
         for half in range(2):
             state[0, half * (POOL // 2) : (half + 1) * (POOL // 2)] = packed[2 * SLOTS + half]
-
-    summed = gradients[0][...]
-    for gradient in gradients[1:]:
-        summed = summed + gradient[...]
-    total[...] = summed
 
 
 def replay_kernel(deepest, packed, wet, order, place, depth, drag, surfaces, whole, final,
@@ -270,9 +276,13 @@
     sea = jnp.minimum(wet[...], 1.0)
     thick[...] = depth[...] / jnp.maximum(wet[...], 1.0)
     for step in range(STEPS):
-        surface = surfaces[step]
-        slope_x[...] = 0.2 * row_diff(surface)[HALO : HALO + rows]
-        slope_y[...] = 0.2 * column_diff(surface[HALO : HALO + rows])
+        surface = surfaces[step * rows : (step + 1) * rows]
+        edges = surfaces[STEPS * rows : STEPS * rows + HALO]
+        row = lax.broadcasted_iota(jnp.int32, surface.shape, 0)
+        before = jnp.where(row == 0, edges[2 * step : 2 * step + 1], pltpu.roll(surface, 1, 0))
+        after = jnp.where(row == rows - 1, edges[2 * step + 1 : 2 * step + 2], pltpu.roll(surface, rows - 1, 0))
+        slope_x[...] = 0.2 * (after - before)
+        slope_y[...] = 0.2 * column_diff(surface)
         factor[...] = drag_terms(bot_u[...], bot_v[...], thick[...], drag[...], sea)[2]
 
         def update(start):
@@ -289,7 +299,7 @@
             bot_v[at, :] = slow * low[1]
 
         looped(rows, update)
-    final[0] = surfaces[STEPS - 1, HALO : HALO + rows]
+    final[0] = surfaces[(STEPS - 1) * rows : STEPS * rows]
 
 
 def edge_kernel(state, adjoint, misfit, depth, drag, mask, bottom, upward, downward, sea_rows, level_rows, sems):
@@ -323,6 +333,14 @@
         copy.wait()
     for side, target in enumerate((upward, downward)):
         target[fields + 1] = (sea_rows[side] * level_rows[side]).astype(jnp.float32)
+
+
+def total_kernel(done, *refs):
+    *gradients, total = refs
+    summed = gradients[0][...]
+    for gradient in gradients[1:]:
+        summed = summed + gradient[...]
+    total[...] = summed
 
 
 def nothing_kernel(result):
@@ -399,7 +417,9 @@
         flux_y = thick[...] * sum_v[...]
         surface = sea * (eta[...] - 0.2 * (row_diff(flux_x) + column_diff(flux_y)))
         eta[...] = surface
-        surfaces[step] = eta[kept_rows]
+        surfaces[step * rows : (step + 1) * rows] = eta[REACH : REACH + rows]
+        surfaces[STEPS * rows + 2 * step : STEPS * rows + 2 * step + 1] = eta[REACH - 1 : REACH]
+        surfaces[STEPS * rows + 2 * step + 1 : STEPS * rows + 2 * step + 2] = eta[REACH + rows : REACH + rows + 1]
         slope_x[...] = 0.2 * row_diff(surface)
         slope_y[...] = 0.2 * column_diff(surface)
         if step == STEPS - 1:
@@ -637,7 +657,7 @@
 
     saved, surfaces = pl.pallas_call(
         forward_kernel,
-        out_shape=(floats(SAVED, rows + 2 * HALO, width), floats(STEPS, rows + 2 * HALO, width)),
+        out_shape=(floats(SAVED, rows + 2 * HALO, width), floats(STEPS * rows + HALO, width)),
         scratch_shapes=[work(REACH)] + [pad(REACH)] * 13,
         compiler_params=params,
         cost_estimate=cost,
@@ -684,17 +704,21 @@
       unless_packed(initial, 1))
 
     pool = pl.BlockSpec((POOL, width), lambda i: (i, 0))
-    next_adjoint, drag_total = pl.pallas_call(
+    next_adjoint, done = pl.pallas_call(
         unpack_kernel,
         grid=(rows // POOL,),
         in_specs=[in_smem, pl.BlockSpec((2 * SLOTS + 2, POOL // 2, width), lambda i: (0, i, 0)),
-                  pool, pool, pool, anywhere] + [pool] * len(gradients),
-        out_specs=[pl.BlockSpec((fields, POOL, width), lambda i: (0, i, 0)), pool],
-        out_shape=[state_shape, floats(rows, width)],
+                  pool, pool, pool, anywhere],
+        out_specs=[pl.BlockSpec((fields, POOL, width), lambda i: (0, i, 0)),
+                   pl.BlockSpec((BLOCK, width), lambda i: (0, 0))],
+        out_shape=[state_shape, floats(BLOCK, width)],
         compiler_params=params,
         cost_estimate=cost,
         name="unpack",
-    )(deepest, came_adjoint, wet, order, place, unless_packed(start, -1), *gradients)
+    )(deepest, came_adjoint, wet, order, place, unless_packed(start, -1))
+    drag_total = pl.pallas_call(
+        total_kernel, out_shape=floats(rows, width), compiler_params=params, cost_estimate=cost, name="total"
+    )(done, *gradients)
     return (next_state[None], next_adjoint[None], drag_total)
 
 

time: 65.3 us -> 64.5 us (0.988)
  waiting for transfers between devices: 21.1 us -> 20.4 us
    pallas_call x1, Pallas kernels: 3 us -> 2.25 us  [body(): pl.pallas_call(plan_kernel, out_specs=(in_vmem,) * 3 + (in_smem,), out_sh...]
    ppermute x6, waiting for transfers between devices: 10.9 us -> 10.2 us  [passed_along(): return lax.ppermute(block, axis, route)]
  transfers between devices with their start and end apart: 8 -> 8, of which waited for: 4 -> 3; matrix products, arithmetic and copies ran while one was open for 0% -> 0% of each run, Pallas kernels for 27% -> 32%
where the time goes in v4:
time: 64.5 us; the launch traced here: 64.3 us
  Pallas kernels  26.1 us (40%)
  waiting for transfers between devices  20.4 us (32%)
  starting transfers between devices  14.7 us (23%)
  local copies, waits for them, and re-layouts  1.65 us (3%)
  between operations  1.43 us (2%)
    ppermute x6, waiting for transfers between devices, passed_along(): return lax.ppermute(block, axis, route)  10.2 us
    ppermute x2, waiting for transfers between devices, shifted(): return lax.ppermute(block, axis, route)  10.2 us
    ppermute x6, starting transfers between devices, passed_along(): return lax.ppermute(block, axis, route)  8.8 us
    pallas_call x1, Pallas kernels, body(): pl.pallas_call(replay_kernel, in_specs=[in_smem] + [in_vmem] * 7 + [anywh...  6.04 us
    ppermute x2, starting transfers between devices, shifted(): return lax.ppermute(block, axis, route)  5.88 us
    pallas_call x1, Pallas kernels, body(): pl.pallas_call(adjoint_kernel, out_specs=(anywhere, in_vmem, in_vmem), ou...  5.78 us
    pallas_call x1, Pallas kernels, body(): pl.pallas_call(forward_kernel, out_shape=(floats(SAVED, rows + 2 * HALO,...  4.23 us
    pallas_call x1, Pallas kernels, body(): pl.pallas_call(unpack_kernel, grid=(rows // POOL,), in_specs=[in_smem, pl...  3.05 us
  transfers between devices with their start and end apart: 8, of which 3 were waited for; matrix products, arithmetic and copies ran while one was open for 0% of the time, Pallas kernels for 32%

profile of v4, /device:TPU:1, one launch (start us, length us, event | category | flops | bytes accessed | tf_op | source)
XLA Modules:
  0.0 64.3 jit_solution(15498690009095264902)
XLA Ops:
  0.6 0.0 copy-start
  0.6 0.0 copy-start.3
  0.7 0.0 copy-start.1
  0.7 0.0 copy-start.4
  0.7 0.9 %copy-done.4 = s32[64,128]{1,0:T(8,128)S(1)} copy-done((s32[64,128]{1,0:T(8,128)S(1)}, s32[64,128]{1,0:T(8,128)}, u32[]{:S(2)}) %copy-start.4) | copy-done | bytes 32792
  1.5 0.8 %copy-done.5 = s32[64,128]{1,0:T(8,128)S(1)} copy-done((s32[64,128]{1,0:T(8,128)S(1)}, s32[64,128]{1,0:T(8,128)}, u32[]{:S(2)}) %copy-start.5) | copy-done | bytes 32792
  2.3 2.3 %plan.1 = (f32[64,128]{1,0:T(8,128)S(1)}, s32[64,128]{1,0:T(8,128)S(1)}, s32[64,128]{1,0:T(8,128)S(1)}, s32[1,1]{1,0:T(1,128)}) custom-call(s32[64,128]{1,0:T(8,128)S(1)} %copy-done.4, s32[64,128]{1,0:T(8,128)S(1)} %copy-done.5), custom_call_target="tpu_custom_call" | custom-call | flops 40140800 | bytes 4014080 | tf_op jit(solution)/shard_map/plan/pallas_call | solution.py:640
  4.6 2.6 %pack.1 = f32[58,32,128]{2,1,0:T(8,128)S(1)} custom-call(f32[49,64,128]{2,1,0:T(8,128)} %bitcast.10, f32[64,128]{1,0:T(8,128)S(1)} %get-tuple-element.30.wet, s32[64,128]{1,0:T(8,128)S(1)} %get-tuple-element.32.order), custom_call_target="tpu_custom_call" | custom-call | flops 40140800 | bytes 4014080 | tf_op jit(solution)/shard_map/pack/pallas_call | solution.py:649
  7.2 2.2 %collective-permute-start.4 = (f32[58,32,128]{2,1,0:T(8,128)S(1)}, f32[58,32,128]{2,1,0:T(8,128)S(1)}, u32[]{:S(2)}, u32[]{:S(2)}) collective-permute-start(f32[58,32,128]{2,1,0:T(8,128)S(1)} %pack.1), channel_id=1, source_target_pairs={{3,0},{0,1},{1,2},{2,3},{7,4},{4,5},{5,6},{6,7},{11,8},{8,9},{9,10... | collective-permute-start | bytes 2850824 | tf_op jit(solution)/shard_map/ppermute | solution.py:27
  9.4 0.0 copy-done.2
  9.4 0.0 copy-start.6
  9.4 1.5 %edges.1 = (f32[79,16,128]{2,1,0:T(8,128)S(1)}, f32[79,16,128]{2,1,0:T(8,128)S(1)}) custom-call(f32[49,64,128]{2,1,0:T(8,128)} %bitcast.11, f32[49,64,128]{2,1,0:T(8,128)S(1)} %bitcast.6, f32[4,64,128]{2,1,0:T(8,128)S(1)} %bitcast.8, f32[64,128]{1,0:T(8,128)S(1)} %copy-done.1, f32[64,128]{1,0:T(8,128)S(1)} %copy-done.2, s32[64,128]{1,0:T(8,128)S(1)} %copy-done.4, ...), custom_call_target="tpu_custom_call" | custom-call | flops 40140800 | bytes 4014080 | tf_op jit(solution)/shard_map/edges/pallas_call | solution.py:627
  10.9 4.0 %collective-permute-start.2 = (f32[79,16,128]{2,1,0:T(8,128)S(1)}, f32[79,16,128]{2,1,0:T(8,128)S(1)}, u32[]{:S(2)}, u32[]{:S(2)}) collective-permute-start(f32[79,16,128]{2,1,0:T(8,128)S(1)} %get-tuple-element.28), channel_id=1, source_target_pairs={{0,4},{4,8},{8,12},{1,5},{5,9},{9,13},{2,6},{6,10},{10,14},{3,7},{... | collective-permute-start | bytes 1941512 | tf_op jit(solution)/shard_map/ppermute | solution.py:21
  14.8 1.9 %collective-permute-start.3 = (f32[79,16,128]{2,1,0:T(8,128)S(1)}, f32[79,16,128]{2,1,0:T(8,128)S(1)}, u32[]{:S(2)}, u32[]{:S(2)}) collective-permute-start(f32[79,16,128]{2,1,0:T(8,128)S(1)} %get-tuple-element.29), channel_id=1, source_target_pairs={{4,0},{8,4},{12,8},{5,1},{9,5},{13,9},{6,2},{10,6},{14,10},{7,3},{... | collective-permute-start | bytes 1941512 | tf_op jit(solution)/shard_map/ppermute | solution.py:21
  16.8 5.5 %collective-permute-done.2.above = f32[79,16,128]{2,1,0:T(8,128)S(1)} collective-permute-done((f32[79,16,128]{2,1,0:T(8,128)S(1)}, f32[79,16,128]{2,1,0:T(8,128)S(1)}, u32[]{:S(2)}, u32[]{:S(2)}) %collective-permute-start.2) | collective-permute-done | bytes 647200 | tf_op jit(solution)/shard_map/ppermute | solution.py:21
  22.3 4.7 %collective-permute-done.3.below = f32[79,16,128]{2,1,0:T(8,128)S(1)} collective-permute-done((f32[79,16,128]{2,1,0:T(8,128)S(1)}, f32[79,16,128]{2,1,0:T(8,128)S(1)}, u32[]{:S(2)}, u32[]{:S(2)}) %collective-permute-start.3) | collective-permute-done | bytes 647200 | tf_op jit(solution)/shard_map/ppermute | solution.py:21
  27.0 4.2 %forward.1 = (f32[10,80,128]{2,1,0:T(8,128)S(1)}, f32[264,128]{1,0:T(8,128)S(1)}) custom-call(f32[49,64,128]{2,1,0:T(8,128)S(1)} %bitcast.12, f32[79,16,128]{2,1,0:T(8,128)S(1)} %collective-permute-done.2.above, f32[79,16,128]{2,1,0:T(8,128)S(1)} %collective-permute-done.3.below, f32[64,128]{1,0:T(8,128)S(1)} %copy-done.1, ...), custom_call_target="tpu_custom_call" | custom-call | flops 40140800 | bytes 4014080 | tf_op jit(solution)/shard_map/forward/pallas_call | solution.py:658
  31.2 1.3 %collective-permute-start.5 = (f32[264,128]{1,0:T(8,128)S(1)}, f32[264,128]{1,0:T(8,128)S(1)}, u32[]{:S(2)}, u32[]{:S(2)}) collective-permute-start(f32[264,128]{1,0:T(8,128)S(1)} %get-tuple-element.34), channel_id=1, source_target_pairs={{3,0},{0,1},{1,2},{2,3},{7,4},{4,5},{5,6},{6,7},{11,8},{8,9},{9,10... | collective-permute-start | bytes 405512 | tf_op jit(solution)/shard_map/ppermute | solution.py:27
  32.5 5.8 %adjoint.1 = (f32[49,64,128]{2,1,0:T(8,128)}, f32[64,128]{1,0:T(8,128)S(1)}, f32[60,32,128]{2,1,0:T(8,128)S(1)}) custom-call(f32[49,64,128]{2,1,0:T(8,128)S(1)} %bitcast.7, f32[4,64,128]{2,1,0:T(8,128)S(1)} %bitcast.9, f32[10,80,128]{2,1,0:T(8,128)S(1)} %get-tuple-element.31.kept, f32[79,16,128]{2,1,0:T(8,128)S(1)} %collective-permute-done.2.above, ...), custom_call_target="tpu_custom_call" | custom-call | flops 40140800 | bytes 4014080 | tf_op jit(solution)/shard_map/adjoint/pallas_call | solution.py:668
  38.3 0.0 collective-permute-done.5.surfaces
  38.3 0.0 collective-permute-done.4.packed
  38.4 2.0 %collective-permute-start.6 = (f32[60,32,128]{2,1,0:T(8,128)S(1)}, f32[60,32,128]{2,1,0:T(8,128)S(1)}, u32[]{:S(2)}, u32[]{:S(2)}) collective-permute-start(f32[60,32,128]{2,1,0:T(8,128)S(1)} %get-tuple-element.38), channel_id=1, source_target_pairs={{1,0},{2,1},{3,2},{0,3},{5,4},{6,5},{7,6},{4,7},{9,8},{10,9},{11,1... | collective-permute-start | bytes 2949128 | tf_op jit(solution)/shard_map/ppermute | solution.py:27
  40.4 0.0 collective-permute-start.7
  40.4 0.6 collective-permute-start.8
  40.9 2.7 %collective-permute-start.9 = (f32[64,128]{1,0:T(8,128)S(1)}, f32[64,128]{1,0:T(8,128)S(1)}, u32[]{:S(2)}, u32[]{:S(2)}) collective-permute-start(f32[64,128]{1,0:T(8,128)S(1)} %get-tuple-element.42.refs_0_), channel_id=1, source_target_pairs={{1,0},{2,1},{3,2},{0,3},{5,4},{6,5},{7,6},{4,7},{9,8},{10,9},{11,1... | collective-permute-start | bytes 98312 | tf_op jit(solution)/shard_map/ppermute | solution.py:27
  44.4 6.0 %replay.1 = f32[49,64,128]{2,1,0:T(8,128)} custom-call(s32[1,1]{1,0:T(1,128)} %get-tuple-element.27.deepest, f32[58,32,128]{2,1,0:T(8,128)S(1)} %collective-permute-done.4.packed, f32[64,128]{1,0:T(8,128)S(1)} %get-tuple-element.30.wet, s32[64,128]{1,0:T(8,128)S(1)} %get-tuple-element.32.order, s32[64,128]{1,0:T(8,128)S(1)} %get-tuple-element.36.place, ...), custom_call_target="tpu_custom_call" | custom-call | flops 40140800 | bytes 4014080 | tf_op jit(solution)/shard_map/replay/pallas_call | solution.py:695
  50.4 10.2 %collective-permute-done.6.packed = f32[60,32,128]{2,1,0:T(8,128)S(1)} collective-permute-done((f32[60,32,128]{2,1,0:T(8,128)S(1)}, f32[60,32,128]{2,1,0:T(8,128)S(1)}, u32[]{:S(2)}, u32[]{:S(2)}) %collective-permute-start.6) | collective-permute-done | bytes 983072 | tf_op jit(solution)/shard_map/ppermute | solution.py:27
  60.6 3.0 %unpack.1 = (f32[49,64,128]{2,1,0:T(8,128)}, f32[8,128]{1,0:T(8,128)S(1)}) custom-call(s32[1,1]{1,0:T(1,128)} %get-tuple-element.27.deepest, f32[60,32,128]{2,1,0:T(8,128)S(1)} %collective-permute-done.6.packed, f32[64,128]{1,0:T(8,128)S(1)} %get-tuple-element.30.wet, s32[64,128]{1,0:T(8,128)S(1)} %get-tuple-element.32.order, ...), custom_call_target="tpu_custom_call" | custom-call | flops 40140800 | bytes 4014080 | tf_op jit(solution)/shard_map/unpack/pallas_call | solution.py:707
  63.6 0.0 collective-permute-done.7.refs_1_
  63.6 0.0 collective-permute-done.8.refs_2_
  63.6 0.0 collective-permute-done.9.refs_3_
  63.6 0.6 total.1
  (10 shorter events, 0.1 us)
Async XLA Ops:
  0.6 8.8 %copy-start = (f32[1,49,64,128]{3,2,1,0:T(8,128)S(1)}, f32[1,49,64,128]{3,2,1,0:T(8,128)}, u32[]{:S(2)}) copy-start(f32[1,49,64,128]{3,2,1,0:T(8,128)} %param.12) | copy-start | bytes 4816900
  0.6 8.7 %copy-start.3 = (f32[1,4,64,128]{3,2,1,0:T(8,128)S(1)}, f32[1,4,64,128]{3,2,1,0:T(8,128)}, u32[]{:S(2)}) copy-start(f32[1,4,64,128]{3,2,1,0:T(8,128)} %param.13) | copy-start | bytes 393220
  0.7 8.7 %copy-start.1 = (f32[64,128]{1,0:T(8,128)S(1)}, f32[64,128]{1,0:T(8,128)}, u32[]{:S(2)}) copy-start(f32[64,128]{1,0:T(8,128)} %depth.7) | copy-start | bytes 98308
  0.7 0.9 %copy-start.4 = (s32[64,128]{1,0:T(8,128)S(1)}, s32[64,128]{1,0:T(8,128)}, u32[]{:S(2)}) copy-start(s32[64,128]{1,0:T(8,128)} %mask.3) | copy-start | bytes 98308
  1.5 0.8 %copy-start.5 = (s32[64,128]{1,0:T(8,128)S(1)}, s32[64,128]{1,0:T(8,128)}, u32[]{:S(2)}) copy-start(s32[64,128]{1,0:T(8,128)} %bottom.3) | copy-start | bytes 98308
  2.3 7.1 %copy-start.2 = (f32[64,128]{1,0:T(8,128)S(1)}, f32[64,128]{1,0:T(8,128)}, u32[]{:S(2)}) copy-start(f32[64,128]{1,0:T(8,128)} %drag.7) | copy-start | bytes 98308
  7.2 31.1 %collective-permute-start.4 = (f32[58,32,128]{2,1,0:T(8,128)S(1)}, f32[58,32,128]{2,1,0:T(8,128)S(1)}, u32[]{:S(2)}, u32[]{:S(2)}) collective-permute-start(f32[58,32,128]{2,1,0:T(8,128)S(1)} %pack.1), channel_id=1, source_target_pairs={{3,0},{0,1},{1,2},{2,3},{7,4},{4,5},{5,6},{6,7},{11,8},{8,9},{9,10... | collective-permute-start | bytes 2850824 | tf_op jit(solution)/shard_map/ppermute | solution.py:27
  9.4 17.6 %copy-start.6 = (f32[1,49,64,128]{3,2,1,0:T(8,128)S(1)}, f32[1,49,64,128]{3,2,1,0:T(8,128)}, u32[]{:S(2)}) copy-start(f32[1,49,64,128]{3,2,1,0:T(8,128)} %param.11) | copy-start | bytes 4816900
  10.9 11.4 %collective-permute-start.2 = (f32[79,16,128]{2,1,0:T(8,128)S(1)}, f32[79,16,128]{2,1,0:T(8,128)S(1)}, u32[]{:S(2)}, u32[]{:S(2)}) collective-permute-start(f32[79,16,128]{2,1,0:T(8,128)S(1)} %get-tuple-element.28), channel_id=1, source_target_pairs={{0,4},{4,8},{8,12},{1,5},{5,9},{9,13},{2,6},{6,10},{10,14},{3,7},{... | collective-permute-start | bytes 1941512 | tf_op jit(solution)/shard_map/ppermute | solution.py:21
  14.8 12.1 %collective-permute-start.3 = (f32[79,16,128]{2,1,0:T(8,128)S(1)}, f32[79,16,128]{2,1,0:T(8,128)S(1)}, u32[]{:S(2)}, u32[]{:S(2)}) collective-permute-start(f32[79,16,128]{2,1,0:T(8,128)S(1)} %get-tuple-element.29), channel_id=1, source_target_pairs={{4,0},{8,4},{12,8},{5,1},{9,5},{13,9},{6,2},{10,6},{14,10},{7,3},{... | collective-permute-start | bytes 1941512 | tf_op jit(solution)/shard_map/ppermute | solution.py:21
  31.2 7.1 %collective-permute-start.5 = (f32[264,128]{1,0:T(8,128)S(1)}, f32[264,128]{1,0:T(8,128)S(1)}, u32[]{:S(2)}, u32[]{:S(2)}) collective-permute-start(f32[264,128]{1,0:T(8,128)S(1)} %get-tuple-element.34), channel_id=1, source_target_pairs={{3,0},{0,1},{1,2},{2,3},{7,4},{4,5},{5,6},{6,7},{11,8},{8,9},{9,10... | collective-permute-start | bytes 405512 | tf_op jit(solution)/shard_map/ppermute | solution.py:27
  38.4 22.2 %collective-permute-start.6 = (f32[60,32,128]{2,1,0:T(8,128)S(1)}, f32[60,32,128]{2,1,0:T(8,128)S(1)}, u32[]{:S(2)}, u32[]{:S(2)}) collective-permute-start(f32[60,32,128]{2,1,0:T(8,128)S(1)} %get-tuple-element.38), channel_id=1, source_target_pairs={{1,0},{2,1},{3,2},{0,3},{5,4},{6,5},{7,6},{4,7},{9,8},{10,9},{11,1... | collective-permute-start | bytes 2949128 | tf_op jit(solution)/shard_map/ppermute | solution.py:27
  40.4 23.2 %collective-permute-start.7 = (f32[64,128]{1,0:T(8,128)S(1)}, f32[64,128]{1,0:T(8,128)S(1)}, u32[]{:S(2)}, u32[]{:S(2)}) collective-permute-start(f32[64,128]{1,0:T(8,128)S(1)} %get-tuple-element.42.refs_0_), channel_id=1, source_target_pairs={{3,0},{0,1},{1,2},{2,3},{7,4},{4,5},{5,6},{6,7},{11,8},{8,9},{9,10... | collective-permute-start | bytes 98312 | tf_op jit(solution)/shard_map/ppermute | solution.py:27
  40.4 23.2 %collective-permute-start.8 = (f32[64,128]{1,0:T(8,128)S(1)}, f32[64,128]{1,0:T(8,128)S(1)}, u32[]{:S(2)}, u32[]{:S(2)}) collective-permute-start(f32[64,128]{1,0:T(8,128)S(1)} %get-tuple-element.42.refs_0_), channel_id=1, source_target_pairs={{2,0},{3,1},{0,2},{1,3},{6,4},{7,5},{4,6},{5,7},{10,8},{11,9},{8,1... | collective-permute-start | bytes 98312 | tf_op jit(solution)/shard_map/ppermute | solution.py:27
  40.9 22.7 %collective-permute-start.9 = (f32[64,128]{1,0:T(8,128)S(1)}, f32[64,128]{1,0:T(8,128)S(1)}, u32[]{:S(2)}, u32[]{:S(2)}) collective-permute-start(f32[64,128]{1,0:T(8,128)S(1)} %get-tuple-element.42.refs_0_), channel_id=1, source_target_pairs={{1,0},{2,1},{3,2},{0,3},{5,4},{6,5},{7,6},{4,7},{9,8},{10,9},{11,1... | collective-permute-start | bytes 98312 | tf_op jit(solution)/shard_map/ppermute | solution.py:27

commit v5 on v4

--- a/solution.py
+++ b/solution.py
@@ -96,10 +96,10 @@
     return jnp.take_along_axis(values, index, axis=1, mode="promise_in_bounds")
 
 
-def plan_kernel(mask, bottom, wet, order, place, deepest):
-    rows, width = mask.shape
+def plan_kernel(wet_levels, wet, order, place, deepest):
+    rows, width = wet_levels.shape
     half = width // 2
-    depth = mask[...] * bottom[...]
+    depth = wet_levels[...]
     wet[...] = depth.astype(jnp.float32)
     lane = lanes_of(depth)
     even = (lax.broadcasted_iota(jnp.int32, depth.shape, 0) // BLOCK) % 2 == 0
@@ -302,7 +302,7 @@
     final[0] = surfaces[(STEPS - 1) * rows : STEPS * rows]
 
 
-def edge_kernel(state, adjoint, misfit, depth, drag, mask, bottom, upward, downward, sea_rows, level_rows, sems):
+def edge_kernel(state, adjoint, misfit, depth, drag, wet_levels, upward, downward, level_rows, sems):
     fields, rows, _ = state.shape
     first = (fields + STEPS + 1) // 2
     joint = fields + 3
@@ -325,14 +325,13 @@
             bring(misfit.at[step, narrow, :], target.at[plane, at, :])
         bring(depth.at[wide, :], target.at[fields])
         bring(drag.at[wide, :], target.at[fields + 2])
-        bring(mask.at[wide, :], sea_rows.at[side])
-        bring(bottom.at[wide, :], level_rows.at[side])
+        bring(wet_levels.at[wide, :], level_rows.at[side])
     for copy in copies:
         copy.start()
     for copy in copies:
         copy.wait()
     for side, target in enumerate((upward, downward)):
-        target[fields + 1] = (sea_rows[side] * level_rows[side]).astype(jnp.float32)
+        target[fields + 1] = level_rows[side].astype(jnp.float32)
 
 
 def total_kernel(done, *refs):
@@ -609,6 +608,7 @@
     initial = start_states[0]
     adjoint = end_adjoints[0]
     misfit = misfits[0]
+    wet_levels = sea_mask * bottom_level
     fields, rows, width = initial.shape
     floats = lambda *shape: jax.ShapeDtypeStruct(shape, jnp.float32)
     whole_numbers = lambda *shape: jax.ShapeDtypeStruct(shape, jnp.int32)
@@ -626,14 +626,14 @@
 
     upward, downward = pl.pallas_call(
         edge_kernel,
-        in_specs=[anywhere] * 7,
+        in_specs=[anywhere] * 6,
         out_specs=(in_vmem, in_vmem),
         out_shape=(edge_shape, edge_shape),
-        scratch_shapes=[pltpu.VMEM((2, REACH, width), jnp.int32)] * 2 + [pltpu.SemaphoreType.DMA((22,))],
+        scratch_shapes=[pltpu.VMEM((2, REACH, width), jnp.int32), pltpu.SemaphoreType.DMA((20,))],
         compiler_params=params,
         cost_estimate=cost,
         name="edges",
-    )(initial, adjoint, misfit, water_depth, drag_coef, sea_mask, bottom_level)
+    )(initial, adjoint, misfit, water_depth, drag_coef, wet_levels)
     above = shifted(downward, "tile", 1)
     below = shifted(upward, "tile", -1)
 
@@ -644,10 +644,14 @@
         compiler_params=params,
         cost_estimate=cost,
         name="plan",
-    )(sea_mask, bottom_level)
-
+    )(wet_levels)
+
+    pool = pl.BlockSpec((POOL, width), lambda i: (i, 0))
     raw = pl.pallas_call(
         pack_kernel,
+        grid=(rows // POOL,),
+        in_specs=[pl.BlockSpec((fields, POOL, width), lambda i: (0, i, 0)), pool, pool],
+        out_specs=pl.BlockSpec((2 * SLOTS, POOL // 2, width), lambda i: (0, i, 0)),
         out_shape=floats(2 * SLOTS, rows // 2, width),
         compiler_params=params,
         cost_estimate=cost,

time: 64.5 us -> 63.6 us (0.986)
  local copies, waits for them, and re-layouts: 1.65 us -> 0.02 us
  other arithmetic: 0 us -> 0.9 us
    unnamed x14 -> x10, local copies, waits for them, and re-layouts: 1.65 us -> 0.02 us
    mul x0 -> x1, other arithmetic: none -> 0.9 us  [body(): wet_levels = sea_mask * bottom_level]
where the time goes in v5:
time: 63.6 us; the launch traced here: 63.3 us
  Pallas kernels  25.9 us (41%)
  waiting for transfers between devices  20.4 us (32%)
  starting transfers between devices  14.7 us (23%)
  between operations  1.43 us (2%)
  other arithmetic  0.9 us (1%)
    ppermute x6, waiting for transfers between devices, passed_along(): return lax.ppermute(block, axis, route)  10.2 us
    ppermute x2, waiting for transfers between devices, shifted(): return lax.ppermute(block, axis, route)  10.2 us
    ppermute x6, starting transfers between devices, passed_along(): return lax.ppermute(block, axis, route)  8.81 us
    pallas_call x1, Pallas kernels, body(): pl.pallas_call(replay_kernel, in_specs=[in_smem] + [in_vmem] * 7 + [anywh...  6.04 us
    ppermute x2, starting transfers between devices, shifted(): return lax.ppermute(block, axis, route)  5.89 us
    pallas_call x1, Pallas kernels, body(): pl.pallas_call(adjoint_kernel, out_specs=(anywhere, in_vmem, in_vmem), ou...  5.78 us
    pallas_call x1, Pallas kernels, body(): pl.pallas_call(forward_kernel, out_shape=(floats(SAVED, rows + 2 * HALO,...  4.23 us
    pallas_call x1, Pallas kernels, body(): pl.pallas_call(unpack_kernel, grid=(rows // POOL,), in_specs=[in_smem, pl...  3.05 us
  transfers between devices with their start and end apart: 8, of which 3 were waited for; matrix products, arithmetic and copies ran while one was open for 0% of the time, Pallas kernels for 32%

profile of v5, /device:TPU:1, one launch (start us, length us, event | category | flops | bytes accessed | tf_op | source)
XLA Modules:
  0.0 63.3 jit_solution(17751736295018837782)
XLA Ops:
  0.6 0.0 copy-start
  0.6 0.0 copy-start.3
  0.7 0.0 copy-start.1
  0.7 0.0 copy-start.2
  0.7 0.9 %mul.3.wet_levels = s32[64,128]{1,0:T(8,128)S(1)} multiply(s32[64,128]{1,0:T(8,128)} %param.16, s32[64,128]{1,0:T(8,128)} %param.17) | non-fusion elementwise | flops 8192 | bytes 98304 | tf_op jit(solution)/shard_map/mul | solution.py:611
  1.6 2.2 %plan.1 = (f32[64,128]{1,0:T(8,128)S(1)}, s32[64,128]{1,0:T(8,128)S(1)}, s32[64,128]{1,0:T(8,128)S(1)}, s32[1,1]{1,0:T(1,128)}) custom-call(s32[64,128]{1,0:T(8,128)S(1)} %mul.3.wet_levels), custom_call_target="tpu_custom_call" | custom-call | flops 40140800 | bytes 4014080 | tf_op jit(solution)/shard_map/plan/pallas_call | solution.py:640
  3.8 2.4 %pack.1 = f32[58,32,128]{2,1,0:T(8,128)S(1)} custom-call(f32[49,64,128]{2,1,0:T(8,128)} %bitcast.10, f32[64,128]{1,0:T(8,128)S(1)} %get-tuple-element.30.wet, s32[64,128]{1,0:T(8,128)S(1)} %get-tuple-element.32.order), custom_call_target="tpu_custom_call" | custom-call | flops 40140800 | bytes 4014080 | tf_op jit(solution)/shard_map/pack/pallas_call | solution.py:650
  6.3 2.2 %collective-permute-start.4 = (f32[58,32,128]{2,1,0:T(8,128)S(1)}, f32[58,32,128]{2,1,0:T(8,128)S(1)}, u32[]{:S(2)}, u32[]{:S(2)}) collective-permute-start(f32[58,32,128]{2,1,0:T(8,128)S(1)} %pack.1), channel_id=1, source_target_pairs={{3,0},{0,1},{1,2},{2,3},{7,4},{4,5},{5,6},{6,7},{11,8},{8,9},{9,10... | collective-permute-start | bytes 2850824 | tf_op jit(solution)/shard_map/ppermute | solution.py:27
  8.5 0.0 copy-done
  8.5 0.0 copy-done.3
  8.5 0.0 copy-start.4
  8.5 1.4 %edges.1 = (f32[79,16,128]{2,1,0:T(8,128)S(1)}, f32[79,16,128]{2,1,0:T(8,128)S(1)}) custom-call(f32[49,64,128]{2,1,0:T(8,128)} %bitcast.11, f32[49,64,128]{2,1,0:T(8,128)S(1)} %bitcast.6, f32[4,64,128]{2,1,0:T(8,128)S(1)} %bitcast.8, f32[64,128]{1,0:T(8,128)S(1)} %copy-done.1, f32[64,128]{1,0:T(8,128)S(1)} %copy-done.2, s32[64,128]{1,0:T(8,128)S(1)} %mul.3.wet_levels), custom_call_target="tpu_custom_call" | custom-call | flops 40140800 | bytes 4014080 | tf_op jit(solution)/shard_map/edges/pallas_call | solution.py:627
  9.9 4.0 %collective-permute-start.2 = (f32[79,16,128]{2,1,0:T(8,128)S(1)}, f32[79,16,128]{2,1,0:T(8,128)S(1)}, u32[]{:S(2)}, u32[]{:S(2)}) collective-permute-start(f32[79,16,128]{2,1,0:T(8,128)S(1)} %get-tuple-element.28), channel_id=1, source_target_pairs={{0,4},{4,8},{8,12},{1,5},{5,9},{9,13},{2,6},{6,10},{10,14},{3,7},{... | collective-permute-start | bytes 1941512 | tf_op jit(solution)/shard_map/ppermute | solution.py:21
  13.9 1.9 %collective-permute-start.3 = (f32[79,16,128]{2,1,0:T(8,128)S(1)}, f32[79,16,128]{2,1,0:T(8,128)S(1)}, u32[]{:S(2)}, u32[]{:S(2)}) collective-permute-start(f32[79,16,128]{2,1,0:T(8,128)S(1)} %get-tuple-element.29), channel_id=1, source_target_pairs={{4,0},{8,4},{12,8},{5,1},{9,5},{13,9},{6,2},{10,6},{14,10},{7,3},{... | collective-permute-start | bytes 1941512 | tf_op jit(solution)/shard_map/ppermute | solution.py:21
  15.8 5.5 %collective-permute-done.2.above = f32[79,16,128]{2,1,0:T(8,128)S(1)} collective-permute-done((f32[79,16,128]{2,1,0:T(8,128)S(1)}, f32[79,16,128]{2,1,0:T(8,128)S(1)}, u32[]{:S(2)}, u32[]{:S(2)}) %collective-permute-start.2) | collective-permute-done | bytes 647200 | tf_op jit(solution)/shard_map/ppermute | solution.py:21
  21.3 4.7 %collective-permute-done.3.below = f32[79,16,128]{2,1,0:T(8,128)S(1)} collective-permute-done((f32[79,16,128]{2,1,0:T(8,128)S(1)}, f32[79,16,128]{2,1,0:T(8,128)S(1)}, u32[]{:S(2)}, u32[]{:S(2)}) %collective-permute-start.3) | collective-permute-done | bytes 647200 | tf_op jit(solution)/shard_map/ppermute | solution.py:21
  26.0 4.2 %forward.1 = (f32[10,80,128]{2,1,0:T(8,128)S(1)}, f32[264,128]{1,0:T(8,128)S(1)}) custom-call(f32[49,64,128]{2,1,0:T(8,128)S(1)} %bitcast.12, f32[79,16,128]{2,1,0:T(8,128)S(1)} %collective-permute-done.2.above, f32[79,16,128]{2,1,0:T(8,128)S(1)} %collective-permute-done.3.below, f32[64,128]{1,0:T(8,128)S(1)} %copy-done.1, ...), custom_call_target="tpu_custom_call" | custom-call | flops 40140800 | bytes 4014080 | tf_op jit(solution)/shard_map/forward/pallas_call | solution.py:662
  30.3 1.3 %collective-permute-start.5 = (f32[264,128]{1,0:T(8,128)S(1)}, f32[264,128]{1,0:T(8,128)S(1)}, u32[]{:S(2)}, u32[]{:S(2)}) collective-permute-start(f32[264,128]{1,0:T(8,128)S(1)} %get-tuple-element.34), channel_id=1, source_target_pairs={{3,0},{0,1},{1,2},{2,3},{7,4},{4,5},{5,6},{6,7},{11,8},{8,9},{9,10... | collective-permute-start | bytes 405512 | tf_op jit(solution)/shard_map/ppermute | solution.py:27
  31.6 5.8 %adjoint.1 = (f32[49,64,128]{2,1,0:T(8,128)}, f32[64,128]{1,0:T(8,128)S(1)}, f32[60,32,128]{2,1,0:T(8,128)S(1)}) custom-call(f32[49,64,128]{2,1,0:T(8,128)S(1)} %bitcast.7, f32[4,64,128]{2,1,0:T(8,128)S(1)} %bitcast.9, f32[10,80,128]{2,1,0:T(8,128)S(1)} %get-tuple-element.31.kept, f32[79,16,128]{2,1,0:T(8,128)S(1)} %collective-permute-done.2.above, ...), custom_call_target="tpu_custom_call" | custom-call | flops 40140800 | bytes 4014080 | tf_op jit(solution)/shard_map/adjoint/pallas_call | solution.py:672
  37.4 0.0 collective-permute-done.5.surfaces
  37.4 0.0 collective-permute-done.4.packed
  37.4 2.0 %collective-permute-start.6 = (f32[60,32,128]{2,1,0:T(8,128)S(1)}, f32[60,32,128]{2,1,0:T(8,128)S(1)}, u32[]{:S(2)}, u32[]{:S(2)}) collective-permute-start(f32[60,32,128]{2,1,0:T(8,128)S(1)} %get-tuple-element.38), channel_id=1, source_target_pairs={{1,0},{2,1},{3,2},{0,3},{5,4},{6,5},{7,6},{4,7},{9,8},{10,9},{11,1... | collective-permute-start | bytes 2949128 | tf_op jit(solution)/shard_map/ppermute | solution.py:27
  39.4 0.0 collective-permute-start.7
  39.4 0.5 collective-permute-start.8
  40.0 2.7 %collective-permute-start.9 = (f32[64,128]{1,0:T(8,128)S(1)}, f32[64,128]{1,0:T(8,128)S(1)}, u32[]{:S(2)}, u32[]{:S(2)}) collective-permute-start(f32[64,128]{1,0:T(8,128)S(1)} %get-tuple-element.42.refs_0_), channel_id=1, source_target_pairs={{1,0},{2,1},{3,2},{0,3},{5,4},{6,5},{7,6},{4,7},{9,8},{10,9},{11,1... | collective-permute-start | bytes 98312 | tf_op jit(solution)/shard_map/ppermute | solution.py:27
  43.4 6.0 %replay.1 = f32[49,64,128]{2,1,0:T(8,128)} custom-call(s32[1,1]{1,0:T(1,128)} %get-tuple-element.27.deepest, f32[58,32,128]{2,1,0:T(8,128)S(1)} %collective-permute-done.4.packed, f32[64,128]{1,0:T(8,128)S(1)} %get-tuple-element.30.wet, s32[64,128]{1,0:T(8,128)S(1)} %get-tuple-element.32.order, s32[64,128]{1,0:T(8,128)S(1)} %get-tuple-element.36.place, ...), custom_call_target="tpu_custom_call" | custom-call | flops 40140800 | bytes 4014080 | tf_op jit(solution)/shard_map/replay/pallas_call | solution.py:699
  49.5 10.2 %collective-permute-done.6.packed = f32[60,32,128]{2,1,0:T(8,128)S(1)} collective-permute-done((f32[60,32,128]{2,1,0:T(8,128)S(1)}, f32[60,32,128]{2,1,0:T(8,128)S(1)}, u32[]{:S(2)}, u32[]{:S(2)}) %collective-permute-start.6) | collective-permute-done | bytes 983072 | tf_op jit(solution)/shard_map/ppermute | solution.py:27
  59.6 3.0 %unpack.1 = (f32[49,64,128]{2,1,0:T(8,128)}, f32[8,128]{1,0:T(8,128)S(1)}) custom-call(s32[1,1]{1,0:T(1,128)} %get-tuple-element.27.deepest, f32[60,32,128]{2,1,0:T(8,128)S(1)} %collective-permute-done.6.packed, f32[64,128]{1,0:T(8,128)S(1)} %get-tuple-element.30.wet, s32[64,128]{1,0:T(8,128)S(1)} %get-tuple-element.32.order, ...), custom_call_target="tpu_custom_call" | custom-call | flops 40140800 | bytes 4014080 | tf_op jit(solution)/shard_map/unpack/pallas_call | solution.py:711
  62.7 0.0 collective-permute-done.7.refs_1_
  62.7 0.0 collective-permute-done.8.refs_2_
  62.7 0.0 collective-permute-done.9.refs_3_
  62.7 0.6 total.1
  (7 shorter events, 0.1 us)
Async XLA Ops:
  0.6 7.8 %copy-start = (f32[1,49,64,128]{3,2,1,0:T(8,128)S(1)}, f32[1,49,64,128]{3,2,1,0:T(8,128)}, u32[]{:S(2)}) copy-start(f32[1,49,64,128]{3,2,1,0:T(8,128)} %param.12) | copy-start | bytes 4816900
  0.6 7.8 %copy-start.3 = (f32[1,4,64,128]{3,2,1,0:T(8,128)S(1)}, f32[1,4,64,128]{3,2,1,0:T(8,128)}, u32[]{:S(2)}) copy-start(f32[1,4,64,128]{3,2,1,0:T(8,128)} %param.13) | copy-start | bytes 393220
  0.7 7.8 %copy-start.1 = (f32[64,128]{1,0:T(8,128)S(1)}, f32[64,128]{1,0:T(8,128)}, u32[]{:S(2)}) copy-start(f32[64,128]{1,0:T(8,128)} %depth.7) | copy-start | bytes 98308
  0.7 7.8 %copy-start.2 = (f32[64,128]{1,0:T(8,128)S(1)}, f32[64,128]{1,0:T(8,128)}, u32[]{:S(2)}) copy-start(f32[64,128]{1,0:T(8,128)} %drag.7) | copy-start | bytes 98308
  6.3 31.1 %collective-permute-start.4 = (f32[58,32,128]{2,1,0:T(8,128)S(1)}, f32[58,32,128]{2,1,0:T(8,128)S(1)}, u32[]{:S(2)}, u32[]{:S(2)}) collective-permute-start(f32[58,32,128]{2,1,0:T(8,128)S(1)} %pack.1), channel_id=1, source_target_pairs={{3,0},{0,1},{1,2},{2,3},{7,4},{4,5},{5,6},{6,7},{11,8},{8,9},{9,10... | collective-permute-start | bytes 2850824 | tf_op jit(solution)/shard_map/ppermute | solution.py:27
  8.5 17.6 %copy-start.4 = (f32[1,49,64,128]{3,2,1,0:T(8,128)S(1)}, f32[1,49,64,128]{3,2,1,0:T(8,128)}, u32[]{:S(2)}) copy-start(f32[1,49,64,128]{3,2,1,0:T(8,128)} %param.11) | copy-start | bytes 4816900
  9.9 11.4 %collective-permute-start.2 = (f32[79,16,128]{2,1,0:T(8,128)S(1)}, f32[79,16,128]{2,1,0:T(8,128)S(1)}, u32[]{:S(2)}, u32[]{:S(2)}) collective-permute-start(f32[79,16,128]{2,1,0:T(8,128)S(1)} %get-tuple-element.28), channel_id=1, source_target_pairs={{0,4},{4,8},{8,12},{1,5},{5,9},{9,13},{2,6},{6,10},{10,14},{3,7},{... | collective-permute-start | bytes 1941512 | tf_op jit(solution)/shard_map/ppermute | solution.py:21
  13.9 12.1 %collective-permute-start.3 = (f32[79,16,128]{2,1,0:T(8,128)S(1)}, f32[79,16,128]{2,1,0:T(8,128)S(1)}, u32[]{:S(2)}, u32[]{:S(2)}) collective-permute-start(f32[79,16,128]{2,1,0:T(8,128)S(1)} %get-tuple-element.29), channel_id=1, source_target_pairs={{4,0},{8,4},{12,8},{5,1},{9,5},{13,9},{6,2},{10,6},{14,10},{7,3},{... | collective-permute-start | bytes 1941512 | tf_op jit(solution)/shard_map/ppermute | solution.py:21
  30.3 7.1 %collective-permute-start.5 = (f32[264,128]{1,0:T(8,128)S(1)}, f32[264,128]{1,0:T(8,128)S(1)}, u32[]{:S(2)}, u32[]{:S(2)}) collective-permute-start(f32[264,128]{1,0:T(8,128)S(1)} %get-tuple-element.34), channel_id=1, source_target_pairs={{3,0},{0,1},{1,2},{2,3},{7,4},{4,5},{5,6},{6,7},{11,8},{8,9},{9,10... | collective-permute-start | bytes 405512 | tf_op jit(solution)/shard_map/ppermute | solution.py:27
  37.4 22.2 %collective-permute-start.6 = (f32[60,32,128]{2,1,0:T(8,128)S(1)}, f32[60,32,128]{2,1,0:T(8,128)S(1)}, u32[]{:S(2)}, u32[]{:S(2)}) collective-permute-start(f32[60,32,128]{2,1,0:T(8,128)S(1)} %get-tuple-element.38), channel_id=1, source_target_pairs={{1,0},{2,1},{3,2},{0,3},{5,4},{6,5},{7,6},{4,7},{9,8},{10,9},{11,1... | collective-permute-start | bytes 2949128 | tf_op jit(solution)/shard_map/ppermute | solution.py:27
  39.4 23.3 %collective-permute-start.7 = (f32[64,128]{1,0:T(8,128)S(1)}, f32[64,128]{1,0:T(8,128)S(1)}, u32[]{:S(2)}, u32[]{:S(2)}) collective-permute-start(f32[64,128]{1,0:T(8,128)S(1)} %get-tuple-element.42.refs_0_), channel_id=1, source_target_pairs={{3,0},{0,1},{1,2},{2,3},{7,4},{4,5},{5,6},{6,7},{11,8},{8,9},{9,10... | collective-permute-start | bytes 98312 | tf_op jit(solution)/shard_map/ppermute | solution.py:27
  39.4 23.3 %collective-permute-start.8 = (f32[64,128]{1,0:T(8,128)S(1)}, f32[64,128]{1,0:T(8,128)S(1)}, u32[]{:S(2)}, u32[]{:S(2)}) collective-permute-start(f32[64,128]{1,0:T(8,128)S(1)} %get-tuple-element.42.refs_0_), channel_id=1, source_target_pairs={{2,0},{3,1},{0,2},{1,3},{6,4},{7,5},{4,6},{5,7},{10,8},{11,9},{8,1... | collective-permute-start | bytes 98312 | tf_op jit(solution)/shard_map/ppermute | solution.py:27
  40.0 22.7 %collective-permute-start.9 = (f32[64,128]{1,0:T(8,128)S(1)}, f32[64,128]{1,0:T(8,128)S(1)}, u32[]{:S(2)}, u32[]{:S(2)}) collective-permute-start(f32[64,128]{1,0:T(8,128)S(1)} %get-tuple-element.42.refs_0_), channel_id=1, source_target_pairs={{1,0},{2,1},{3,2},{0,3},{5,4},{6,5},{7,6},{4,7},{9,8},{10,9},{11,1... | collective-permute-start | bytes 98312 | tf_op jit(solution)/shard_map/ppermute | solution.py:27

commit v6 on v5

--- a/solution.py
+++ b/solution.py
@@ -197,9 +197,10 @@
     pack(state, wet, order, packed)
 
 
-def unpack_pool(packed, wet, order, place, state, pool):
+def unpack_pool(packed, wet, order, place, state, pool, state_pool):
     levels = (state.shape[0] - 1) // 2
     ats = pool_rows(pool)
+    state_ats = pool_rows(state_pool)
     slots = pool_slots(pool)
     wets = [wet[at, :] for at in ats]
     places = [place[at, :] for at in ats]
@@ -214,7 +215,7 @@
                 if block % 2:
                     pair = pair[::-1]
                 value = take_lanes(jnp.where(first, *pair), places[block])
-                state[base + level, ats[block], :] = jnp.where(wets[block] > level, value, 0.0)
+                state[base + level, state_ats[block], :] = jnp.where(wets[block] > level, value, 0.0)
 
         for near in range((SLOTS + 1) // 2):
             far = SLOTS - 1 - near
@@ -235,9 +236,10 @@
 
     @pl.when(deepest[0, 0] <= SLOTS)
     def _():
-        unpack_pool(packed, wet, order, place, state, 0)
+        unpack_pool(packed, wet, order, place, state, pool, 0)
         for half in range(2):
-            state[0, half * (POOL // 2) : (half + 1) * (POOL // 2)] = packed[2 * SLOTS + half]
+            at = pl.ds(pl.multiple_of(pool * (POOL // 2), POOL // 2), POOL // 2)
+            state[0, half * (POOL // 2) : (half + 1) * (POOL // 2)] = packed[2 * SLOTS + half, at, :]
 
 
 def replay_kernel(deepest, packed, wet, order, place, depth, drag, surfaces, whole, final,
@@ -256,7 +258,7 @@
     @pl.when(deepest[0, 0] <= SLOTS)
     def _():
         def one_pool(pool, carry):
-            unpack_pool(packed, wet, order, place, final, pool)
+            unpack_pool(packed, wet, order, place, final, pool, pool)
             return carry
 
         lax.fori_loop(0, rows // POOL, one_pool, 0)
@@ -711,8 +713,7 @@
     next_adjoint, done = pl.pallas_call(
         unpack_kernel,
         grid=(rows // POOL,),
-        in_specs=[in_smem, pl.BlockSpec((2 * SLOTS + 2, POOL // 2, width), lambda i: (0, i, 0)),
-                  pool, pool, pool, anywhere],
+        in_specs=[in_smem] + [in_vmem] * 4 + [anywhere],
         out_specs=[pl.BlockSpec((fields, POOL, width), lambda i: (0, i, 0)),
                    pl.BlockSpec((BLOCK, width), lambda i: (0, 0))],
         out_shape=[state_shape, floats(BLOCK, width)],

time: 63.6 us -> 63.5 us (level)
  no operation moved by 1% of the time
where the time goes in v6:
time: 63.5 us; the launch traced here: 63.2 us
  Pallas kernels  25.8 us (41%)
  waiting for transfers between devices  20.4 us (32%)
  starting transfers between devices  14.7 us (23%)
  between operations  1.43 us (2%)
  other arithmetic  0.9 us (1%)
    ppermute x6, waiting for transfers between devices, passed_along(): return lax.ppermute(block, axis, route)  10.2 us
    ppermute x2, waiting for transfers between devices, shifted(): return lax.ppermute(block, axis, route)  10.2 us
    ppermute x6, starting transfers between devices, passed_along(): return lax.ppermute(block, axis, route)  8.81 us
    pallas_call x1, Pallas kernels, body(): pl.pallas_call(replay_kernel, in_specs=[in_smem] + [in_vmem] * 7 + [anywh...  6.04 us
    ppermute x2, starting transfers between devices, shifted(): return lax.ppermute(block, axis, route)  5.89 us
    pallas_call x1, Pallas kernels, body(): pl.pallas_call(adjoint_kernel, out_specs=(anywhere, in_vmem, in_vmem), ou...  5.78 us
    pallas_call x1, Pallas kernels, body(): pl.pallas_call(forward_kernel, out_shape=(floats(SAVED, rows + 2 * HALO,...  4.23 us
    pallas_call x1, Pallas kernels, body(): pl.pallas_call(unpack_kernel, grid=(rows // POOL,), in_specs=[in_smem] +...  2.97 us
  transfers between devices with their start and end apart: 8, of which 3 were waited for; matrix products, arithmetic and copies ran while one was open for 0% of the time, Pallas kernels for 32%

profile of v6, /device:TPU:1, one launch (start us, length us, event | category | flops | bytes accessed | tf_op | source)
XLA Modules:
  0.0 63.2 jit_solution(6134413185897214732)
XLA Ops:
  0.6 0.0 copy-start
  0.6 0.0 copy-start.3
  0.7 0.0 copy-start.1
  0.7 0.0 copy-start.2
  0.7 0.9 %mul.3.wet_levels = s32[64,128]{1,0:T(8,128)S(1)} multiply(s32[64,128]{1,0:T(8,128)} %param.16, s32[64,128]{1,0:T(8,128)} %param.17) | non-fusion elementwise | flops 8192 | bytes 98304 | tf_op jit(solution)/shard_map/mul | solution.py:613
  1.6 2.2 %plan.1 = (f32[64,128]{1,0:T(8,128)S(1)}, s32[64,128]{1,0:T(8,128)S(1)}, s32[64,128]{1,0:T(8,128)S(1)}, s32[1,1]{1,0:T(1,128)}) custom-call(s32[64,128]{1,0:T(8,128)S(1)} %mul.3.wet_levels), custom_call_target="tpu_custom_call" | custom-call | flops 40140800 | bytes 4014080 | tf_op jit(solution)/shard_map/plan/pallas_call | solution.py:642
  3.8 2.4 %pack.1 = f32[58,32,128]{2,1,0:T(8,128)S(1)} custom-call(f32[49,64,128]{2,1,0:T(8,128)} %bitcast.10, f32[64,128]{1,0:T(8,128)S(1)} %get-tuple-element.30.wet, s32[64,128]{1,0:T(8,128)S(1)} %get-tuple-element.32.order), custom_call_target="tpu_custom_call" | custom-call | flops 40140800 | bytes 4014080 | tf_op jit(solution)/shard_map/pack/pallas_call | solution.py:652
  6.3 2.2 %collective-permute-start.4 = (f32[58,32,128]{2,1,0:T(8,128)S(1)}, f32[58,32,128]{2,1,0:T(8,128)S(1)}, u32[]{:S(2)}, u32[]{:S(2)}) collective-permute-start(f32[58,32,128]{2,1,0:T(8,128)S(1)} %pack.1), channel_id=1, source_target_pairs={{3,0},{0,1},{1,2},{2,3},{7,4},{4,5},{5,6},{6,7},{11,8},{8,9},{9,10... | collective-permute-start | bytes 2850824 | tf_op jit(solution)/shard_map/ppermute | solution.py:27
  8.5 0.0 copy-done
  8.5 0.0 copy-done.3
  8.5 0.0 copy-start.4
  8.5 1.4 %edges.1 = (f32[79,16,128]{2,1,0:T(8,128)S(1)}, f32[79,16,128]{2,1,0:T(8,128)S(1)}) custom-call(f32[49,64,128]{2,1,0:T(8,128)} %bitcast.11, f32[49,64,128]{2,1,0:T(8,128)S(1)} %bitcast.6, f32[4,64,128]{2,1,0:T(8,128)S(1)} %bitcast.8, f32[64,128]{1,0:T(8,128)S(1)} %copy-done.1, f32[64,128]{1,0:T(8,128)S(1)} %copy-done.2, s32[64,128]{1,0:T(8,128)S(1)} %mul.3.wet_levels), custom_call_target="tpu_custom_call" | custom-call | flops 40140800 | bytes 4014080 | tf_op jit(solution)/shard_map/edges/pallas_call | solution.py:629
  9.9 4.0 %collective-permute-start.2 = (f32[79,16,128]{2,1,0:T(8,128)S(1)}, f32[79,16,128]{2,1,0:T(8,128)S(1)}, u32[]{:S(2)}, u32[]{:S(2)}) collective-permute-start(f32[79,16,128]{2,1,0:T(8,128)S(1)} %get-tuple-element.28), channel_id=1, source_target_pairs={{0,4},{4,8},{8,12},{1,5},{5,9},{9,13},{2,6},{6,10},{10,14},{3,7},{... | collective-permute-start | bytes 1941512 | tf_op jit(solution)/shard_map/ppermute | solution.py:21
  13.9 1.9 %collective-permute-start.3 = (f32[79,16,128]{2,1,0:T(8,128)S(1)}, f32[79,16,128]{2,1,0:T(8,128)S(1)}, u32[]{:S(2)}, u32[]{:S(2)}) collective-permute-start(f32[79,16,128]{2,1,0:T(8,128)S(1)} %get-tuple-element.29), channel_id=1, source_target_pairs={{4,0},{8,4},{12,8},{5,1},{9,5},{13,9},{6,2},{10,6},{14,10},{7,3},{... | collective-permute-start | bytes 1941512 | tf_op jit(solution)/shard_map/ppermute | solution.py:21
  15.8 5.5 %collective-permute-done.2.above = f32[79,16,128]{2,1,0:T(8,128)S(1)} collective-permute-done((f32[79,16,128]{2,1,0:T(8,128)S(1)}, f32[79,16,128]{2,1,0:T(8,128)S(1)}, u32[]{:S(2)}, u32[]{:S(2)}) %collective-permute-start.2) | collective-permute-done | bytes 647200 | tf_op jit(solution)/shard_map/ppermute | solution.py:21
  21.3 4.7 %collective-permute-done.3.below = f32[79,16,128]{2,1,0:T(8,128)S(1)} collective-permute-done((f32[79,16,128]{2,1,0:T(8,128)S(1)}, f32[79,16,128]{2,1,0:T(8,128)S(1)}, u32[]{:S(2)}, u32[]{:S(2)}) %collective-permute-start.3) | collective-permute-done | bytes 647200 | tf_op jit(solution)/shard_map/ppermute | solution.py:21
  26.0 4.2 %forward.1 = (f32[10,80,128]{2,1,0:T(8,128)S(1)}, f32[264,128]{1,0:T(8,128)S(1)}) custom-call(f32[49,64,128]{2,1,0:T(8,128)S(1)} %bitcast.12, f32[79,16,128]{2,1,0:T(8,128)S(1)} %collective-permute-done.2.above, f32[79,16,128]{2,1,0:T(8,128)S(1)} %collective-permute-done.3.below, f32[64,128]{1,0:T(8,128)S(1)} %copy-done.1, ...), custom_call_target="tpu_custom_call" | custom-call | flops 40140800 | bytes 4014080 | tf_op jit(solution)/shard_map/forward/pallas_call | solution.py:664
  30.3 1.3 %collective-permute-start.5 = (f32[264,128]{1,0:T(8,128)S(1)}, f32[264,128]{1,0:T(8,128)S(1)}, u32[]{:S(2)}, u32[]{:S(2)}) collective-permute-start(f32[264,128]{1,0:T(8,128)S(1)} %get-tuple-element.34), channel_id=1, source_target_pairs={{3,0},{0,1},{1,2},{2,3},{7,4},{4,5},{5,6},{6,7},{11,8},{8,9},{9,10... | collective-permute-start | bytes 405512 | tf_op jit(solution)/shard_map/ppermute | solution.py:27
  31.6 5.8 %adjoint.1 = (f32[49,64,128]{2,1,0:T(8,128)}, f32[64,128]{1,0:T(8,128)S(1)}, f32[60,32,128]{2,1,0:T(8,128)S(1)}) custom-call(f32[49,64,128]{2,1,0:T(8,128)S(1)} %bitcast.7, f32[4,64,128]{2,1,0:T(8,128)S(1)} %bitcast.9, f32[10,80,128]{2,1,0:T(8,128)S(1)} %get-tuple-element.31.kept, f32[79,16,128]{2,1,0:T(8,128)S(1)} %collective-permute-done.2.above, ...), custom_call_target="tpu_custom_call" | custom-call | flops 40140800 | bytes 4014080 | tf_op jit(solution)/shard_map/adjoint/pallas_call | solution.py:674
  37.4 0.0 collective-permute-done.5.surfaces
  37.4 0.0 collective-permute-done.4.packed
  37.4 2.0 %collective-permute-start.6 = (f32[60,32,128]{2,1,0:T(8,128)S(1)}, f32[60,32,128]{2,1,0:T(8,128)S(1)}, u32[]{:S(2)}, u32[]{:S(2)}) collective-permute-start(f32[60,32,128]{2,1,0:T(8,128)S(1)} %get-tuple-element.38), channel_id=1, source_target_pairs={{1,0},{2,1},{3,2},{0,3},{5,4},{6,5},{7,6},{4,7},{9,8},{10,9},{11,1... | collective-permute-start | bytes 2949128 | tf_op jit(solution)/shard_map/ppermute | solution.py:27
  39.4 0.0 collective-permute-start.7
  39.4 0.5 collective-permute-start.8
  40.0 2.7 %collective-permute-start.9 = (f32[64,128]{1,0:T(8,128)S(1)}, f32[64,128]{1,0:T(8,128)S(1)}, u32[]{:S(2)}, u32[]{:S(2)}) collective-permute-start(f32[64,128]{1,0:T(8,128)S(1)} %get-tuple-element.42.refs_0_), channel_id=1, source_target_pairs={{1,0},{2,1},{3,2},{0,3},{5,4},{6,5},{7,6},{4,7},{9,8},{10,9},{11,1... | collective-permute-start | bytes 98312 | tf_op jit(solution)/shard_map/ppermute | solution.py:27
  43.4 6.0 %replay.1 = f32[49,64,128]{2,1,0:T(8,128)} custom-call(s32[1,1]{1,0:T(1,128)} %get-tuple-element.27.deepest, f32[58,32,128]{2,1,0:T(8,128)S(1)} %collective-permute-done.4.packed, f32[64,128]{1,0:T(8,128)S(1)} %get-tuple-element.30.wet, s32[64,128]{1,0:T(8,128)S(1)} %get-tuple-element.32.order, s32[64,128]{1,0:T(8,128)S(1)} %get-tuple-element.36.place, ...), custom_call_target="tpu_custom_call" | custom-call | flops 40140800 | bytes 4014080 | tf_op jit(solution)/shard_map/replay/pallas_call | solution.py:701
  49.5 10.2 %collective-permute-done.6.packed = f32[60,32,128]{2,1,0:T(8,128)S(1)} collective-permute-done((f32[60,32,128]{2,1,0:T(8,128)S(1)}, f32[60,32,128]{2,1,0:T(8,128)S(1)}, u32[]{:S(2)}, u32[]{:S(2)}) %collective-permute-start.6) | collective-permute-done | bytes 983072 | tf_op jit(solution)/shard_map/ppermute | solution.py:27
  59.6 3.0 %unpack.1 = (f32[49,64,128]{2,1,0:T(8,128)}, f32[8,128]{1,0:T(8,128)S(1)}) custom-call(s32[1,1]{1,0:T(1,128)} %get-tuple-element.27.deepest, f32[60,32,128]{2,1,0:T(8,128)S(1)} %collective-permute-done.6.packed, f32[64,128]{1,0:T(8,128)S(1)} %get-tuple-element.30.wet, s32[64,128]{1,0:T(8,128)S(1)} %get-tuple-element.32.order, ...), custom_call_target="tpu_custom_call" | custom-call | flops 40140800 | bytes 4014080 | tf_op jit(solution)/shard_map/unpack/pallas_call | solution.py:713
  62.6 0.0 collective-permute-done.7.refs_1_
  62.6 0.0 collective-permute-done.8.refs_2_
  62.6 0.0 collective-permute-done.9.refs_3_
  62.6 0.6 total.1
  (7 shorter events, 0.1 us)
Async XLA Ops:
  0.6 7.8 %copy-start = (f32[1,49,64,128]{3,2,1,0:T(8,128)S(1)}, f32[1,49,64,128]{3,2,1,0:T(8,128)}, u32[]{:S(2)}) copy-start(f32[1,49,64,128]{3,2,1,0:T(8,128)} %param.12) | copy-start | bytes 4816900
  0.6 7.8 %copy-start.3 = (f32[1,4,64,128]{3,2,1,0:T(8,128)S(1)}, f32[1,4,64,128]{3,2,1,0:T(8,128)}, u32[]{:S(2)}) copy-start(f32[1,4,64,128]{3,2,1,0:T(8,128)} %param.13) | copy-start | bytes 393220
  0.7 7.8 %copy-start.1 = (f32[64,128]{1,0:T(8,128)S(1)}, f32[64,128]{1,0:T(8,128)}, u32[]{:S(2)}) copy-start(f32[64,128]{1,0:T(8,128)} %depth.7) | copy-start | bytes 98308
  0.7 7.8 %copy-start.2 = (f32[64,128]{1,0:T(8,128)S(1)}, f32[64,128]{1,0:T(8,128)}, u32[]{:S(2)}) copy-start(f32[64,128]{1,0:T(8,128)} %drag.7) | copy-start | bytes 98308
  6.3 31.1 %collective-permute-start.4 = (f32[58,32,128]{2,1,0:T(8,128)S(1)}, f32[58,32,128]{2,1,0:T(8,128)S(1)}, u32[]{:S(2)}, u32[]{:S(2)}) collective-permute-start(f32[58,32,128]{2,1,0:T(8,128)S(1)} %pack.1), channel_id=1, source_target_pairs={{3,0},{0,1},{1,2},{2,3},{7,4},{4,5},{5,6},{6,7},{11,8},{8,9},{9,10... | collective-permute-start | bytes 2850824 | tf_op jit(solution)/shard_map/ppermute | solution.py:27
  8.5 17.6 %copy-start.4 = (f32[1,49,64,128]{3,2,1,0:T(8,128)S(1)}, f32[1,49,64,128]{3,2,1,0:T(8,128)}, u32[]{:S(2)}) copy-start(f32[1,49,64,128]{3,2,1,0:T(8,128)} %param.11) | copy-start | bytes 4816900
  9.9 11.4 %collective-permute-start.2 = (f32[79,16,128]{2,1,0:T(8,128)S(1)}, f32[79,16,128]{2,1,0:T(8,128)S(1)}, u32[]{:S(2)}, u32[]{:S(2)}) collective-permute-start(f32[79,16,128]{2,1,0:T(8,128)S(1)} %get-tuple-element.28), channel_id=1, source_target_pairs={{0,4},{4,8},{8,12},{1,5},{5,9},{9,13},{2,6},{6,10},{10,14},{3,7},{... | collective-permute-start | bytes 1941512 | tf_op jit(solution)/shard_map/ppermute | solution.py:21
  13.9 12.1 %collective-permute-start.3 = (f32[79,16,128]{2,1,0:T(8,128)S(1)}, f32[79,16,128]{2,1,0:T(8,128)S(1)}, u32[]{:S(2)}, u32[]{:S(2)}) collective-permute-start(f32[79,16,128]{2,1,0:T(8,128)S(1)} %get-tuple-element.29), channel_id=1, source_target_pairs={{4,0},{8,4},{12,8},{5,1},{9,5},{13,9},{6,2},{10,6},{14,10},{7,3},{... | collective-permute-start | bytes 1941512 | tf_op jit(solution)/shard_map/ppermute | solution.py:21
  30.3 7.1 %collective-permute-start.5 = (f32[264,128]{1,0:T(8,128)S(1)}, f32[264,128]{1,0:T(8,128)S(1)}, u32[]{:S(2)}, u32[]{:S(2)}) collective-permute-start(f32[264,128]{1,0:T(8,128)S(1)} %get-tuple-element.34), channel_id=1, source_target_pairs={{3,0},{0,1},{1,2},{2,3},{7,4},{4,5},{5,6},{6,7},{11,8},{8,9},{9,10... | collective-permute-start | bytes 405512 | tf_op jit(solution)/shard_map/ppermute | solution.py:27
  37.4 22.2 %collective-permute-start.6 = (f32[60,32,128]{2,1,0:T(8,128)S(1)}, f32[60,32,128]{2,1,0:T(8,128)S(1)}, u32[]{:S(2)}, u32[]{:S(2)}) collective-permute-start(f32[60,32,128]{2,1,0:T(8,128)S(1)} %get-tuple-element.38), channel_id=1, source_target_pairs={{1,0},{2,1},{3,2},{0,3},{5,4},{6,5},{7,6},{4,7},{9,8},{10,9},{11,1... | collective-permute-start | bytes 2949128 | tf_op jit(solution)/shard_map/ppermute | solution.py:27
  39.4 23.2 %collective-permute-start.7 = (f32[64,128]{1,0:T(8,128)S(1)}, f32[64,128]{1,0:T(8,128)S(1)}, u32[]{:S(2)}, u32[]{:S(2)}) collective-permute-start(f32[64,128]{1,0:T(8,128)S(1)} %get-tuple-element.42.refs_0_), channel_id=1, source_target_pairs={{3,0},{0,1},{1,2},{2,3},{7,4},{4,5},{5,6},{6,7},{11,8},{8,9},{9,10... | collective-permute-start | bytes 98312 | tf_op jit(solution)/shard_map/ppermute | solution.py:27
  39.4 23.2 %collective-permute-start.8 = (f32[64,128]{1,0:T(8,128)S(1)}, f32[64,128]{1,0:T(8,128)S(1)}, u32[]{:S(2)}, u32[]{:S(2)}) collective-permute-start(f32[64,128]{1,0:T(8,128)S(1)} %get-tuple-element.42.refs_0_), channel_id=1, source_target_pairs={{2,0},{3,1},{0,2},{1,3},{6,4},{7,5},{4,6},{5,7},{10,8},{11,9},{8,1... | collective-permute-start | bytes 98312 | tf_op jit(solution)/shard_map/ppermute | solution.py:27
  40.0 22.7 %collective-permute-start.9 = (f32[64,128]{1,0:T(8,128)S(1)}, f32[64,128]{1,0:T(8,128)S(1)}, u32[]{:S(2)}, u32[]{:S(2)}) collective-permute-start(f32[64,128]{1,0:T(8,128)S(1)} %get-tuple-element.42.refs_0_), channel_id=1, source_target_pairs={{1,0},{2,1},{3,2},{0,3},{5,4},{6,5},{7,6},{4,7},{9,8},{10,9},{11,1... | collective-permute-start | bytes 98312 | tf_op jit(solution)/shard_map/ppermute | solution.py:27
